TPU v7x, 32 devices: a whole 2x2x4 slice. The times are simulated.
32 devices in a mesh: shard: 2 (over y), ctx: 4 (over z), tp: 4 (over x, core).
Axes of the slice: x: 2, y: 2, z: 4, core: 2. Of those that a mesh axis runs over, the one named last changes fastest.
Arguments:
- x_in: float32 [4096, 768], P(('shard', 'ctx')), may hold values from -6 to 6
- norm_gain: bfloat16 [768], P(('shard', 'ctx')), may hold values from 0.5 to 1.5
- w_z: bfloat16 [768, 1536], P(('shard', 'ctx'), 'tp'), may hold values from -0.21875 to 0.21875
- w_x: bfloat16 [768, 1536], P(('shard', 'ctx'), 'tp'), may hold values from -0.21875 to 0.21875
- w_bc: bfloat16 [768, 256], P(('shard', 'ctx')), may hold values from -0.21875 to 0.21875
- w_dt: bfloat16 [768, 24], P(('shard', 'ctx'), 'tp'), may hold values from -0.21875 to 0.21875
- w_out: bfloat16 [768, 1536], P(('shard', 'ctx'), 'tp'), may hold values from -0.15625 to 0.15625
- conv_wx: float32 [4, 1536], P(None, 'tp'), may hold values from -3 to 3
- conv_bx: float32 [1536], P('tp'), may hold values from -0.5 to 0.5
- conv_wbc: float32 [4, 256], replicated, may hold values from -3 to 3
- conv_bbc: float32 [256], replicated, may hold values from -0.5 to 0.5
- dt_bias: float32 [24], P('tp'), may hold values from -6 to -3
- a_log: float32 [24], P('tp'), may hold values from -6 to 2
- d_skip: float32 [24], P('tp'), may hold values from 0.5 to 1.5
- gate_gain: float32 [1536], P('tp'), may hold values from 0.5 to 1.5
- seq_lens: int32 [2, 3], P('shard'), may hold values from 1 to 1280, 2048 in all within a row
- token_mask: int32 [4096], P(('shard', 'ctx')), may hold values 0 or 1
- d_out: float32 [4096, 768], P(('shard', 'ctx')), may hold values from -6 to 6
Outputs:
- block_out: float32 [4096, 768], P(('shard', 'ctx'))
- d_x: float32 [4096, 768], P(('shard', 'ctx'))
- d_norm_gain: float32 [768], P(('shard', 'ctx'))
- d_w_z: float32 [768, 1536], P(('shard', 'ctx'), 'tp')
- d_w_x: float32 [768, 1536], P(('shard', 'ctx'), 'tp')
- d_w_bc: float32 [768, 256], P(('shard', 'ctx'))
- d_w_dt: float32 [768, 24], P(('shard', 'ctx'), 'tp')
- d_w_out: float32 [768, 1536], P(('shard', 'ctx'), 'tp')
- d_conv_wx: float32 [4, 1536], P(None, 'tp')
- d_conv_bx: float32 [1536], P('tp')
- d_conv_wbc: float32 [4, 256], replicated
- d_conv_bbc: float32 [256], replicated
- d_dt_bias: float32 [24], P('tp')
- d_a_log: float32 [24], P('tp')
- d_d_skip: float32 [24], P('tp')
- d_gate_gain: float32 [1536], P('tp')
Inputs may be any that keep to these rules, and one draw needn't show every extreme that they name: `seq_lens`: each row sums to 2048, and its longest sequence has exactly 1280 positions.
All inputs are finite; a program needn't handle non-finite values. No bound on the sum of `token_mask` on one device may be relied on, other than what follows from the above.
Results may differ from a plain program's by a relative error of at most 0.014.
Values may be sent and summed in bfloat16 or wider, within the bound.
No kernel may reach another device: no remote copies, remote signals or barrier semaphores. Data moves between devices by JAX's collectives and lax.ppermute only.
A program may use at most 128 MiB of HBM per device.

v0:
```python
import jax
import jax.numpy as jnp
from jax import lax
from jax.experimental import pallas as pl
from jax.experimental.pallas import tpu as pltpu
from jax.sharding import PartitionSpec as P


f32 = jnp.float32
bf16 = jnp.bfloat16
norm_eps = 1e-05
L = 128
NN = ((1,), (0,))
NT = ((1,), (1,))
TN = ((0,), (0,))
HI = lax.Precision.HIGHEST


def dot(a, b, dims=NN, precision=None):
    return lax.dot_general(a, b, (dims, ((), ())), preferred_element_type=f32, precision=precision)


def split(v):
    if v.dtype == bf16:
        return v, None
    high = v.astype(bf16)
    return high, (v - high.astype(f32)).astype(bf16)


def dot3(a, b, dims=NN):
    ah, al = split(a) if not isinstance(a, tuple) else a
    bh, bl = split(b) if not isinstance(b, tuple) else b
    total = dot(ah, bh, dims)
    if bl is not None:
        total = total + dot(ah, bl, dims)
    if al is not None:
        total = total + dot(al, bh, dims)
    return total


def iota(shape, dim):
    return lax.broadcasted_iota(jnp.int32, shape, dim)


def sigmoid(v):
    return 1.0 / (1.0 + jnp.exp(-v))


def softplus(v):
    return jnp.maximum(v, 0.0) + jnp.log1p(jnp.exp(-jnp.abs(v)))


class Meta:
    def __init__(self, ref, sizes):
        self.ref, self.sizes = ref, sizes
        self.me_s, self.me_c, self.me_t = ref[0], ref[1], ref[2]
        self.base = self.me_c * sizes["T"]
        self.half = lax.rem(self.me_t, 2)
        bounds, total = [], 0
        for i in range(sizes["seqs"]):
            total = total + ref[3 + i]
            bounds.append(total)
        self.bounds = bounds

    def place(self, i, sign):
        n_ctx, n_sh = self.sizes["ctx"], self.sizes["shards"] // self.sizes["ctx"]
        shard = lax.rem(self.me_s + i // n_ctx, n_sh)
        ctx = lax.rem(self.me_c + sign * (i % n_ctx) + n_ctx, n_ctx)
        return (shard * n_ctx + ctx) * (self.sizes["D"] // self.sizes["shards"])

    def shard_row(self, i):
        return self.place(i, -1)

    def block_row(self, i):
        return self.place(i, 1)

    def peer(self, k):
        return jnp.bitwise_xor(self.me_t, k)

    def segment(self, pos):
        total = 0
        for bound in self.bounds:
            total = total + jnp.where(pos >= bound, 1, 0)
        return jnp.where(pos < 0, -1, total)


def load_weights(meta, shards, scratch):
    rows = shards[0].shape[0]
    for i, shard in enumerate(shards):
        at = meta.shard_row(i) if len(shards) > 1 else 0
        if len(shards) > 1:
            at = pl.multiple_of(at, 16)
        scratch[pl.ds(at, rows), :] = shard[...]


class Step:
    chunk, inner, count = None, 0, 1


def when_first(body):
    if Step.inner == 0:
        pl.when(pl.program_id(0) == 0)(body)


def when_later(body):
    if Step.inner == 0:
        pl.when(pl.program_id(0) > 0)(body)
    else:
        body()


def when_last(body):
    if Step.inner == Step.count - 1:
        pl.when(pl.program_id(0) == pl.num_programs(0) - 1)(body)


def unrolled(kernel, ins, outs, count):
    axes, wide = [], []
    for item in (*ins, *outs):
        axis = None
        if item[0] != "smem":
            moved = [d for d, (a, b) in enumerate(zip(item[1](0), item[1](1))) if a != b]
            axis = moved[0] if moved else None
        if axis is not None:
            block = tuple(n * count if d == axis else n for d, n in enumerate(item[0]))
            item = (block,) + tuple(item[1:])
        axes.append(axis)
        wide.append(item)

    def body(*refs):
        for inner in range(count):
            views = []
            for k, ref in enumerate(refs):
                axis = axes[k] if k < len(axes) else None
                if axis is None:
                    views.append(ref)
                    continue
                size = wide[k][0][axis] // count
                at = tuple(
                    slice(inner * size, (inner + 1) * size) if d == axis else slice(None)
                    for d in range(len(wide[k][0]))
                )
                views.append(ref.at[at])
            Step.chunk, Step.inner, Step.count = pl.program_id(0) * count + inner, inner, count
            kernel(*views)

    return body, wide[: len(ins)], wide[len(ins) :]


def call(kernel, grid, ins, outs, scratch, flops, args, unroll=1):
    if unroll > 1 and grid % unroll == 0:
        kernel, ins, outs = unrolled(kernel, ins, outs, unroll)
        grid = grid // unroll
    else:
        inner_kernel = kernel

        def kernel(*refs):
            Step.chunk, Step.inner, Step.count = pl.program_id(0), 0, 1
            inner_kernel(*refs)


    def spec(item):
        block, index = item[0], item[1]
        if block == "smem":
            return pl.BlockSpec(memory_space=pltpu.SMEM)
        return pl.BlockSpec(block, index)

    out_shape = [jax.ShapeDtypeStruct(o[2], o[3]) for o in outs]
    nbytes = sum(a.size * a.dtype.itemsize for a in args) + sum(
        o.size * o.dtype.itemsize for o in out_shape
    )
    return pl.pallas_call(
        kernel,
        grid=(grid,),
        in_specs=[spec(i) for i in ins],
        out_specs=[spec(o) for o in outs],
        out_shape=out_shape,
        scratch_shapes=scratch,
        cost_estimate=pl.CostEstimate(flops=flops, bytes_accessed=nbytes, transcendentals=0),
        compiler_params=pltpu.CompilerParams(dimension_semantics=("arbitrary",)),
    )(*args)


def whole(a):
    return (tuple(a.shape), lambda i, n=len(a.shape): (0,) * n)


def rows(a, count=L):
    return ((count, a.shape[1]), lambda i: (i, 0))


def cols(a):
    return ((a.shape[0], L), lambda i: (0, i))


def o_rows(shape, dtype, count=L):
    return ((count, shape[1]), lambda i: (i, 0), shape, dtype)


def o_cols(shape, dtype):
    return ((shape[0], L), lambda i: (0, i), shape, dtype)


def o_whole(shape, dtype):
    return (tuple(shape), lambda i, n=len(shape): (0,) * n, shape, dtype)


SMEM = ("smem", None)


def tri_leq():
    return jnp.where(iota((L, L), 0) <= iota((L, L), 1), 1.0, 0.0)


def pair_mask(hw, which):
    lane = iota((L, 128), 1)
    return (lane >= which * hw) & (lane < (which + 1) * hw)


def allowed_mask(meta, c):
    start = meta.base + c * L
    pt, ps = start + iota((L, L), 0), start + iota((L, L), 1)
    return (meta.segment(pt) == meta.segment(ps)) & (pt >= ps)


def chunk_edges(meta, c):
    start = meta.base + c * L
    return meta.segment(start - 1), meta.segment(start + L - 1)


def pair_sum(left, right):
    def kernel(a, b, out):
        out[...] = (a[...].astype(f32) + b[...].astype(f32)).astype(bf16)

    vmem = pl.BlockSpec(memory_space=pltpu.VMEM)
    return pl.pallas_call(
        kernel, in_specs=[vmem, vmem], out_specs=vmem,
        out_shape=jax.ShapeDtypeStruct(left.shape, bf16),
        cost_estimate=pl.CostEstimate(flops=left.size, bytes_accessed=6 * left.size, transcendentals=0),
    )(left, right)


def to_shift(meta, c, width, distance):
    pos = meta.base + c * L + iota((L, 128), 0)
    same = meta.segment(pos) == meta.segment(pos - distance)
    return tiled(jnp.where(same & (pos - distance >= 0), 1.0, 0.0), width)


def tiled(mask, width):
    return jnp.concatenate([mask] * (width // 128), axis=1)


def flag(cond):
    return jnp.where(cond, 1.0, 0.0).astype(f32)


def build(sizes):
    T, D, IN, N, H, TAPS = (sizes[k] for k in ("T", "D", "IN", "N", "H", "TAPS"))
    n_tp, n_ctx, nC = sizes["tp"], sizes["ctx"], sizes["T"] // L
    HW = IN // H
    HPT = 128 // HW
    SL = 2 * N // n_tp
    PAIRS = IN // 128
    DIRECT = sizes["shards"] > 1
    NSH = sizes["shards"]
    PK = IN + 128 + 2 * N
    EXT = IN + 2 * N
    SP = 16
    HB = T // 2 // nC

    def expand_matrix():
        r, l = iota((128, IN), 0), iota((128, IN), 1)
        return jnp.where((r >= SL) & (r < SL + H) & (l // HW == r - SL), 1.0, 0.0)

    def head_select():
        r, l = iota((8, IN), 0), iota((8, IN), 1)
        return jnp.where((l // HW == r) & (r < H), 1.0, 0.0)

    def slab_select():
        r, l = iota((8, 128), 0), iota((8, 128), 1)
        return jnp.where((l == r + SL) & (r < H), 1.0, 0.0)

    def local_weights(cum, meta, c, last):
        return jnp.exp(cum[L - 1 : L, :] - cum) * in_segment(meta, c, last)

    def in_segment(meta, c, which):
        same = meta.segment(meta.base + c * L + iota((L, 128), 0)) == which
        return tiled(jnp.where(same, 1.0, 0.0), IN)

    def k_project(*refs):
        meta = Meta(refs[0], sizes)
        x_ref, xh_ref, cw_ref, hp_ref, hc_ref, mask_ref = refs[1:7]
        shards = refs[7 : 7 + NSH]
        (nb_ref, pr_ref, prh_ref, sm_ref, act_ref, dt_ref, cum_ref, dtr_ref, cumr_ref, hpre_ref,
         pp_ref, pack_ref) = refs[7 + NSH : 19 + NSH]
        gain_ref, w_ref, ext_ref, st_ref, ps_ref = refs[19 + NSH :]
        c = Step.chunk

        @when_first
        def _():
            load_weights(meta, shards, w_ref)
            xh = xh_ref[...]
            inv_h = lax.rsqrt(jnp.mean(xh * xh, axis=1, keepdims=True) + norm_eps)
            pick = jnp.where(iota((8, 128), 1) == SL + H, 1.0, 0.0).astype(bf16)
            gain_ref[...] = dot(pick, w_ref[:, IN : IN + 128], NT)
            nh = (xh * inv_h * gain_ref[...]).astype(bf16)
            ph = dot(nh, w_ref[...]).astype(bf16).astype(f32)
            prh_ref[...] = ph
            ext_ref[0:8, :IN] = ph[:, :IN]
            ext_ref[0:8, IN:] = ph[:, IN + 128 :]
            st_ref[...] = jnp.zeros((N, IN), f32)
            ps_ref[...] = jnp.ones((8, IN), f32)

        @when_later
        def _():
            ext_ref[0:8, :] = ext_ref[L : L + 8, :]

        x = x_ref[...]
        inv = lax.rsqrt(jnp.mean(x * x, axis=1, keepdims=True) + norm_eps)
        nb = (x * inv * gain_ref[0:1, :]).astype(bf16)
        nb_ref[...] = nb
        pr = dot(nb, w_ref[...]).astype(bf16)
        pr_ref[...] = pr
        prf = pr.astype(f32)
        ext_ref[8 : 8 + L, :IN] = prf[:, :IN]
        ext_ref[8 : 8 + L, IN:] = prf[:, IN + 128 :]
        summed = jnp.zeros((L, EXT), f32) + cw_ref[TAPS : TAPS + 1, :]
        for k in range(TAPS):
            d = TAPS - 1 - k
            term = cw_ref[k : k + 1, :] * ext_ref[8 - d : 8 - d + L, :]
            summed = summed + (term if d == 0 else term * to_shift(meta, c, EXT, d))
        sm_ref[...] = summed
        act = summed * sigmoid(summed)
        act_ref[...] = act
        slab = pr[:, IN : IN + 128]
        hp, hc = hp_ref[...], hc_ref[...]
        mask8 = mask_ref[...]
        mask_c = dot(mask8, jnp.where(iota((8, IN), 0) == 0, 1.0, 0.0), TN)
        dt = softplus(dot(slab, expand_matrix().astype(bf16)) + hp[0:1, :]) * mask_c
        dtr = softplus(dot(slab_select().astype(bf16), slab, NT) + hc[:, 0:1]) * mask8[0:1, :]
        tri = tri_leq()
        cum = dot(tri, dt * hp[1:2, :], TN, HI)
        cumr = dot(dtr * hc[:, 1:2], tri, NN, HI)
        dt_ref[...], cum_ref[...], dtr_ref[...], cumr_ref[...] = dt, cum, dtr, cumr
        prev, last = chunk_edges(meta, c)
        xd = dt * act[:, :IN]
        ws = local_weights(cum, meta, c, last)
        b = act[:, IN : IN + N]
        passing = jnp.exp(cum[L - 1 : L, :]) * flag(prev == last)
        at = pl.multiple_of(c * N, N)
        st, ps = st_ref[...], ps_ref[...]
        hpre_ref[pl.ds(at, N), :] = st
        pp_ref[pl.ds(pl.multiple_of(c * 8, 8), 8), :] = ps
        st = passing * st + dot3(b, ws * xd, TN)
        ps = ps * passing
        st_ref[...], ps_ref[...] = st, ps

        @when_last
        def _():
            hpre_ref[nC * N : (nC + 1) * N, :] = st
            pp_ref[nC * 8 : nC * 8 + 8, :] = ps
            pack_ref[:N, :] = st.astype(bf16)
            pack_ref[N:, :] = jnp.concatenate([ps, ps], axis=0).astype(bf16)

    def project(meta, x, xh, cw, hp, hc, mask8, shards):
        outs = [
            o_rows((T, D), bf16), o_rows((T, PK), bf16), o_whole((8, PK), f32),
            o_rows((T, EXT), f32), o_rows((T, EXT), f32), o_rows((T, IN), f32),
            o_rows((T, IN), f32), o_cols((8, T), f32), o_cols((8, T), f32),
            o_whole(((nC + 1) * N, IN), f32), o_whole(((nC + 1) * 8, IN), f32),
            o_whole((N + SP, IN), bf16), o_whole((8, D), f32),
        ]
        ins = [SMEM, rows(x), whole(xh), whole(cw), whole(hp), whole(hc), cols(mask8)]
        ins += [whole(s) for s in shards]
        scratch = [
            pltpu.VMEM((D, PK), bf16), pltpu.VMEM((L + 8, EXT), f32),
            pltpu.VMEM((N, IN), f32), pltpu.VMEM((8, IN), f32),
        ]
        return call(k_project, nC, ins, outs, scratch, 2 * T * D * PK,
                    [meta, x, xh, cw, hp, hc, mask8, *shards], unroll=2)

    def head_decay(meta_mask, cum, cumr, h):
        gap = cum[:, h * HW : h * HW + 1] - cumr[h : h + 1, :]
        return jnp.where(meta_mask, jnp.exp(gap), 0.0)

    def k_intra(mref, act_ref, dt_ref, cum_ref, cumr_ref, y_ref):
        meta = Meta(mref, sizes)
        c = Step.chunk
        ok = allowed_mask(meta, c)
        b = act_ref[:, IN : IN + N]
        cc = act_ref[:, IN + N :]
        scores = dot3(cc, b, NT)
        cum, cumr = cum_ref[...], cumr_ref[...]
        for p in range(PAIRS):
            sl = slice(p * 128, p * 128 + 128)
            xd = (dt_ref[:, sl] * act_ref[:, sl])
            y = None
            for j in range(HPT):
                g = (scores * head_decay(ok, cum, cumr, p * HPT + j))
                part = dot3(g, xd)
                y = part if y is None else jnp.where(pair_mask(HW, j), part, y)
            y_ref[:, sl] = y

    def intra(meta, act, dt, cum, cumr):
        return call(k_intra, nC, [SMEM, rows(act), rows(dt), rows(cum), cols(cumr)],
                    [o_rows((T, IN), f32)], [], 4 * T * L * IN, [meta, act, dt, cum, cumr], unroll=2)[0]

    def k_gate(*refs):
        meta = Meta(refs[0], sizes)
        nb_ref, do_ref = refs[1:3]
        shards = refs[3 : 3 + NSH]
        z_ref, dm_ref, w_ref = refs[3 + NSH :]

        @when_first
        def _():
            load_weights(meta, shards, w_ref)

        z_ref[...] = dot(nb_ref[...], w_ref[:, :IN]).astype(bf16)
        dm_ref[...] = dot(do_ref[...].astype(bf16), w_ref[:, IN:])

    def gate(meta, nb, d_out, shards):
        return call(k_gate, nC, [SMEM, rows(nb), rows(d_out)] + [whole(s) for s in shards],
                    [o_rows((T, IN), bf16), o_rows((T, IN), f32)],
                    [pltpu.VMEM((D, 2 * IN), bf16)], 4 * T * D * IN, [meta, nb, d_out, *shards], unroll=2)

    def chain(packs):
        total = None
        for pack in reversed(packs):
            state = pack[:N, :].astype(f32)
            total = state if total is None else state + pack[N : N + 1, :].astype(f32) * total
        return total

    def k_output(*refs):
        meta = Meta(refs[0], sizes)
        act_ref, cum_ref, y_ref, z_ref, dm_ref, hpre_ref, pp_ref, hp_ref, gg_ref = refs[1:10]
        packs = refs[10 : 10 + n_ctx - 1]
        yo_ref, stat_ref, ent_ref = refs[9 + n_ctx :]
        c = Step.chunk

        @when_first
        def _():
            ent_ref[...] = chain(packs)

        prev, _ = chunk_edges(meta, c)
        hin = (hpre_ref[...] + pp_ref[0:1, :] * ent_ref[...])
        cum = cum_ref[...]
        ent = jnp.exp(cum) * in_segment(meta, c, prev)
        y = y_ref[...] + ent * dot3(act_ref[:, IN + N :], hin)
        yo_ref[...] = y
        out = y + hp_ref[2:3, :] * act_ref[:, :IN]
        z = z_ref[...].astype(f32)
        gated = out * (z * sigmoid(z))
        ones = jnp.ones((8, IN), f32)
        sq = dot(ones, gated * gated, NT, HI)
        bd = dot(ones, dm_ref[...] * gg_ref[0:1, :] * gated, NT, HI)
        stat_ref[...] = jnp.where(iota((8, L), 0) == 0, sq, bd)

    def output(meta, act, cum, y, z, dm, hpre, pp, hp, gg, packs):
        ins = [SMEM, rows(act), rows(cum), rows(y), rows(z), rows(dm), rows(hpre, N), rows(pp, 8),
               whole(hp), whole(gg)] + [whole(p) for p in packs]
        outs = [o_rows((T, IN), f32), o_cols((8, T), f32), o_whole((N, IN), f32)]
        return call(k_output, nC, ins, outs, [], 4 * T * IN * N,
                    [meta, act, cum, y, z, dm, hpre, pp, hp, gg, *packs], unroll=2)

    def k_norm(*refs):
        meta = Meta(refs[0], sizes)
        act_ref, cum_ref, y_ref, z_ref, dm_ref, hp_ref, gg_ref = refs[1:8]
        stats = refs[8 : 8 + n_tp]
        mix_ref, dz_ref, dy_ref, suf_ref, psuf_ref, pack_ref, sums_ref = refs[8 + n_tp : 15 + n_tp]
        st_ref, ps_ref = refs[15 + n_tp :]
        c = nC - 1 - pl.program_id(0)

        @pl.when(pl.program_id(0) == 0)
        def _():
            st_ref[...] = jnp.zeros((N, IN), f32)
            ps_ref[...] = jnp.ones((8, IN), f32)
            sums_ref[...] = jnp.zeros((8, IN), f32)

        stat = stats[0][...]
        for s in stats[1:]:
            stat = stat + s[...]
        inner = float(IN * n_tp)
        inv_r = lax.rsqrt(stat[0:1, :] / inner + norm_eps)
        beta_r = inv_r * inv_r * inv_r * stat[1:2, :] / inner
        row = iota((8, L), 0)
        both = jnp.where(row == 0, inv_r, jnp.where(row == 1, beta_r, 0.0))
        inv = dot(both, jnp.where(iota((8, IN), 0) == 0, 1.0, 0.0), TN, HI)
        beta = dot(both, jnp.where(iota((8, IN), 0) == 1, 1.0, 0.0), TN, HI)
        gg, skip = gg_ref[0:1, :], hp_ref[2:3, :]
        x = act_ref[:, :IN]
        out = y_ref[...] + skip * x
        z = z_ref[...].astype(f32)
        sig = sigmoid(z)
        ga = z * sig
        gated = out * ga
        dm = dm_ref[...]
        normal = gated * inv
        mix_ref[...] = (normal * gg).astype(bf16)
        dg = dm * gg * inv - gated * beta
        dz_ref[...] = (dg * out * sig * (1.0 + z * (1.0 - sig))).astype(bf16)
        dy = dg * ga
        dyb = dy
        dy_ref[...] = dyb
        s0 = jnp.sum(dm * normal, axis=0, keepdims=True)
        s1 = jnp.sum(dy * x, axis=0, keepdims=True)
        r8 = iota((8, IN), 0)
        sums_ref[...] += jnp.where(r8 == 0, s0, jnp.where(r8 == 1, s1, 0.0))
        prev, last = chunk_edges(meta, c)
        cum = cum_ref[...]
        ent = jnp.exp(cum) * in_segment(meta, c, prev)
        passing = jnp.exp(cum[L - 1 : L, :]) * flag(prev == last)
        st, ps = st_ref[...], ps_ref[...]
        suf_ref[...] = st
        psuf_ref[...] = ps
        cc = act_ref[:, IN + N :]
        st = passing * st + dot3(cc, ent * dyb.astype(f32), TN)
        ps = passing * ps
        st_ref[...], ps_ref[...] = st, ps

        @pl.when(c == 0)
        def _():
            pack_ref[:N, :] = st.astype(bf16)
            pack_ref[N:, :] = jnp.concatenate([ps, ps], axis=0).astype(bf16)

    def norm(meta, act, cum, y, z, dm, hp, gg, stats):
        def back(item):
            block, index = item[0], item[1]
            return (block, lambda i: index(nC - 1 - i)) + tuple(item[2:])

        ins = [SMEM] + [back(rows(a)) for a in (act, cum, y, z, dm)] + [whole(hp), whole(gg)]
        ins += [back(cols(s)) for s in stats]
        outs = [back(o_rows((T, IN), bf16)), back(o_rows((T, IN), bf16)), back(o_rows((T, IN), f32)),
                back(o_rows((nC * N, IN), f32, N)), back(o_rows((nC * 8, IN), f32, 8)),
                o_whole((N + SP, IN), bf16), o_whole((8, IN), f32)]
        scratch = [pltpu.VMEM((N, IN), f32), pltpu.VMEM((8, IN), f32)]
        return call(k_norm, nC, ins, outs, scratch, 2 * T * IN * N,
                    [meta, act, cum, y, z, dm, hp, gg, *stats])

    def k_intra_back(mref, act_ref, dt_ref, cum_ref, cumr_ref, dy_ref, dxd_ref, dbc_ref):
        meta = Meta(mref, sizes)
        c = Step.chunk
        ok = allowed_mask(meta, c)
        b = act_ref[:, IN : IN + N]
        cc = act_ref[:, IN + N :]
        scores = dot3(cc, b, NT)
        cum, cumr = cum_ref[...], cumr_ref[...]
        d_scores = jnp.zeros((L, L), f32)
        for p in range(PAIRS):
            sl = slice(p * 128, p * 128 + 128)
            xd = (dt_ref[:, sl] * act_ref[:, sl])
            dy = dy_ref[:, sl]
            dxd = None
            for j in range(HPT):
                decay = head_decay(ok, cum, cumr, p * HPT + j)
                g = (scores * decay)
                part = dot3(g, dy, TN)
                dxd = part if dxd is None else jnp.where(pair_mask(HW, j), part, dxd)
                own = jnp.where(pair_mask(HW, j), dy.astype(f32), 0.0)
                d_scores = d_scores + dot3(own, xd, NT) * decay
            dxd_ref[:, sl] = dxd
        ds = d_scores
        dbc_ref[:, :N] = dot3(ds, cc, TN)
        dbc_ref[:, N:] = dot3(ds, b)

    def intra_back(meta, act, dt, cum, cumr, dy):
        return call(k_intra_back, nC,
                    [SMEM, rows(act), rows(dt), rows(cum), cols(cumr), rows(dy)],
                    [o_rows((T, IN), f32), o_rows((T, 2 * N), f32)], [], 8 * T * L * IN,
                    [meta, act, dt, cum, cumr, dy], unroll=2)

    def write_blocks(meta, total, outs):
        if not DIRECT:
            outs[0][...] = total[...].astype(bf16)
            return
        br = D // NSH
        for i in range(NSH):
            at = pl.multiple_of(meta.block_row(i), 8)
            outs[i % n_ctx][(i // n_ctx) * br : (i // n_ctx + 1) * br, :] = total[
                pl.ds(at, br), :
            ].astype(bf16)

    n_groups = n_ctx if DIRECT else 1
    group_rows = D // n_ctx if DIRECT else D

    def split_rows(meta, c, value, keep, send):
        at = pl.multiple_of(lax.rem(c, nC // 2) * L, L)

        @pl.when(c // (nC // 2) == meta.half)
        def _():
            keep[pl.ds(at, L), :] = value

        @pl.when(c // (nC // 2) != meta.half)
        def _():
            send[pl.ds(at, L), :] = value.astype(bf16)

    def k_outer(*refs):
        meta = Meta(refs[0], sizes)
        nb_ref, do_ref, mix_ref, dz_ref = refs[1:5]
        shards = refs[5 : 5 + NSH]
        outs = refs[5 + NSH : 5 + NSH + n_groups]
        keep_ref, send_ref = refs[5 + NSH + n_groups : 7 + NSH + n_groups]
        w_ref, total = refs[7 + NSH + n_groups :]
        c = pl.program_id(0)

        @pl.when(c == 0)
        def _():
            load_weights(meta, shards, w_ref)
            total[...] = jnp.zeros((D, 2 * IN), f32)

        total[:, :IN] += dot(nb_ref[...], dz_ref[...], TN)
        total[:, IN:] += dot(do_ref[...].astype(bf16), mix_ref[...], TN)
        split_rows(meta, c, dot(mix_ref[...], w_ref[:, IN:], NT), keep_ref, send_ref)

        @pl.when(c == nC - 1)
        def _():
            write_blocks(meta, total, outs)

    def outer(meta, nb, d_out, mix, dz, shards):
        outs = [o_whole((group_rows, 2 * IN), bf16)] * n_groups
        outs += [o_whole((T // 2, D), f32), o_whole((T // 2, D), bf16)]
        ins = [SMEM, rows(nb), rows(d_out), rows(mix), rows(dz)] + [whole(s) for s in shards]
        scratch = [pltpu.VMEM((D, 2 * IN), bf16), pltpu.VMEM((D, 2 * IN), f32)]
        got = call(k_outer, nC, ins, outs, scratch, 6 * T * D * IN,
                   [meta, nb, d_out, mix, dz, *shards])
        return got[:n_groups], got[n_groups], got[n_groups + 1]

    def k_scan_back(*refs):
        meta = Meta(refs[0], sizes)
        (act_ref, sm_ref, pr_ref, dt_ref, cum_ref, dtr_ref, y_ref, dy_ref, dxd_ref, dbc_ref, hpre_ref,
         hnext_ref, pp_ref, pnext_ref, ent_ref, suf_ref, psuf_ref, hp_ref, hc_ref, mask_ref, bk_ref,
         bg_ref) = refs[1:23]
        packs, at = refs[23 : 22 + n_ctx], 22 + n_ctx
        dsx_ref, ddt_ref, sums_ref, edge_ref, pair_ref = refs[at : at + 5]
        slices = refs[at + 5 : at + 5 + n_tp]
        edges = refs[at + 5 + n_tp : at + 4 + 2 * n_tp]
        exit_ref = refs[at + 4 + 2 * n_tp]
        c = pl.program_id(0)
        pair_ref[...] = (bk_ref[...] + bg_ref[...].astype(f32)).astype(bf16)

        @pl.when(c == 0)
        def _():
            exit_ref[...] = chain(packs)
            sums_ref[...] = jnp.zeros((16, 128), f32)

        prev, last = chunk_edges(meta, c)
        hin = hpre_ref[...] + pp_ref[0:1, :] * ent_ref[...]
        hout = hnext_ref[...] + pnext_ref[0:1, :] * ent_ref[...]
        dh = suf_ref[...] + psuf_ref[0:1, :] * exit_ref[...]
        hinb, dhb = hin, dh
        cum, dt, x = cum_ref[...], dt_ref[...], act_ref[:, :IN]
        b = act_ref[:, IN : IN + N]
        ws = local_weights(cum, meta, c, last)
        ent = jnp.exp(cum) * in_segment(meta, c, prev)
        xd = dt * x
        dyf = dy_ref[...].astype(f32)
        leaving = dot3(b, dhb)
        wx = ws * xd
        dxd_in = dxd_ref[...]
        dxd = dxd_in + ws * leaving
        db = dbc_ref[:, :N] + dot3(wx, dhb, NT)
        dc = dbc_ref[:, N:] + dot3(ent * dyf, hinb, NT)
        hs = head_select()
        dcum = dot(hs, dyf * y_ref[...] - xd * dxd_in - wx.astype(f32) * leaving, NT, HI)
        final = dot(hs, jnp.zeros((8, IN), f32) + jnp.sum(dhb.astype(f32) * hout, axis=0, keepdims=True), NT, HI)
        da = dot(dcum, tri_leq(), NT, HI) + final[:, 0:1]
        hc = hc_ref[...]
        dtr, mask8 = dtr_ref[...], mask_ref[...]
        ddt = da * hc[:, 1:2] + dot(hs, dxd * x, NT, HI)
        slab = pr_ref[:, IN : IN + 128]
        pre_r = dot(slab_select().astype(bf16), slab, NT) + hc[:, 0:1]
        dpre = ddt * mask8[0:1, :] * sigmoid(pre_r)
        ddt_ref[...] = dot(dpre.astype(bf16), slab_select().astype(bf16), TN).astype(bf16)
        ones = jnp.ones((L, 128), f32)
        sums_ref[0:8, :] += dot(dpre, ones, NN, HI)
        sums_ref[8:16, :] += dot(da * dtr, ones, NN, HI)
        sm = sm_ref[...]
        sig = sigmoid(sm)
        dsilu = sig * (1.0 + sm * (1.0 - sig))
        dsx = (hp_ref[2:3, :] * dyf + dt * dxd) * dsilu[:, :IN]
        dsx_ref[...] = dsx
        dsb = (jnp.concatenate([db, dc], axis=1) * dsilu[:, IN:]).astype(bf16)
        quarter = c // (nC // 2)
        at = pl.multiple_of(lax.rem(c, nC // 2) * L, L)
        r, l = iota((2 * N, 128), 0), iota((2 * N, 128), 1)
        for k in range(n_tp):
            left = meta.peer(k) * SL
            lane0 = quarter * SL
            pick = jnp.where((r - left == l - lane0) & (l >= lane0) & (l < lane0 + SL), 1.0, 0.0)
            part = dot(dsb, pick.astype(bf16)).astype(bf16)

            @pl.when(quarter == 0)
            def _():
                slices[k][pl.ds(at, L), :] = part

            @pl.when(quarter != 0)
            def _():
                slices[k][pl.ds(at, L), :] = slices[k][pl.ds(at, L), :] + part

            @pl.when(c == 0)
            def _():
                if k == 0:
                    edge_ref[:, :IN] = dsx[0:8, :]
                    edge_ref[:, IN:] = part[0:8, :].astype(f32)
                else:
                    edges[k - 1][...] = part[0:8, :].astype(f32)

    def scan_back(meta, act, sm, pr, dt, cum, dtr, y, dy, dxd, dbc, hpre, pp, ent, suf, psuf, hp, hc,
                  mask8, b_keep, b_got, packs):
        def later(item):
            return (item[0], lambda i: item[1](i + 1))

        ins = [SMEM, rows(act), rows(sm), rows(pr), rows(dt), rows(cum), cols(dtr), rows(y), rows(dy),
               rows(dxd), rows(dbc), rows(hpre, N), later(rows(hpre, N)), rows(pp, 8),
               later(rows(pp, 8)), whole(ent), rows(suf, N), rows(psuf, 8), whole(hp), whole(hc),
               cols(mask8), rows(b_keep, HB), rows(b_got, HB)] + [whole(p) for p in packs]
        outs = [o_rows((T, IN), f32), o_rows((T, 128), bf16), o_whole((16, 128), f32),
                o_whole((8, IN + 128), f32), o_rows((T // 2, D), bf16, HB)]
        outs += [o_whole((T // 2, 128), bf16)] * n_tp + [o_whole((8, 128), f32)] * (n_tp - 1)
        got = call(k_scan_back, nC, ins, outs, [pltpu.VMEM((N, IN), f32)],
                   6 * T * IN * N,
                   [meta, act, sm, pr, dt, cum, dtr, y, dy, dxd, dbc, hpre, hpre, pp, pp, ent, suf,
                    psuf, hp, hc, mask8, b_keep, b_got, *packs])
        return got[:5], got[5 : 5 + n_tp], got[5 + n_tp :]

    PW = IN + 128
    br9 = D // NSH

    def k_conv_back(*refs):
        meta = Meta(refs[0], sizes)
        nb_ref, pr_ref, prp_ref, prh_ref, dz_ref, ddt_ref, dsx_ref, dsn_ref = refs[1:9]
        cw_ref, sums_ref, ssum_ref, edge_ref = refs[9:13]
        at = 13
        slices, at = refs[at : at + n_tp], at + n_tp
        edges, at = refs[at : at + n_tp - 1], at + n_tp - 1
        shards, at = refs[at : at + NSH], at + NSH
        zshards, at = refs[at : at + NSH], at + NSH
        halves, at = refs[at : at + n_tp // 2], at + n_tp // 2
        gs, at = refs[at : at + NSH], at + NSH
        keep_ref, send_ref, half_ref = refs[at : at + 3]
        at += 3
        w_ref, wz_ref, ex_ref, px_ref, sl_ref, total, tap_ref = refs[at:]
        c = pl.program_id(0)
        half = halves[0][...].astype(f32)
        for h in halves[1:]:
            half = half + h[...].astype(f32)
        half_ref[...] = half.astype(bf16)

        @pl.when(c == 0)
        def _():
            load_weights(meta, shards, w_ref)
            load_weights(meta, zshards, wz_ref)
            total[...] = jnp.zeros((D, PW), f32)
            tap_ref[...] = jnp.zeros((8, PW), f32)
            sl = slices[0][...].astype(f32)
            for s in slices[1:]:
                sl = sl + s[...].astype(f32)
            low = iota((T // 2, 128), 1) < SL
            sl_ref[0 : T // 2, :] = jnp.where(low, sl, 0.0)
            sl_ref[T // 2 : T, :] = jnp.where(low, pltpu.roll(sl, 128 - SL, 1), 0.0)
            e = edge_ref[:, IN:]
            for s in edges:
                e = e + s[...]
            sl_ref[T : T + 8, :] = jnp.where(iota((8, 128), 1) < SL, e, 0.0)

        here = pl.multiple_of(c * L, L)
        after = pl.multiple_of(c * L + L, L)
        ex_ref[0:L, :IN] = dsx_ref[...]
        ex_ref[0:L, IN:] = sl_ref[pl.ds(here, L), :]
        ex_ref[L : L + 8, IN:] = sl_ref[pl.ds(after, 8), :]
        ex_ref[L : L + 8, :IN] = jnp.where(c == nC - 1, edge_ref[:, :IN], dsn_ref[...])
        low = iota((L, PW), 1) < IN + SL
        px_ref[8 : 8 + L, :] = pr_ref[:, :PW].astype(f32)
        px_ref[0:8, :] = jnp.where(c == 0, prh_ref[:, :PW], prp_ref[8:16, :PW].astype(f32))
        cw = cw_ref[...]
        ds = ex_ref[0:L, :]
        dpre = jnp.zeros((L, PW), f32)
        pos = meta.base + c * L + iota((L, 128), 0)
        seg = meta.segment(pos)
        group = T * n_ctx
        r8 = iota((8, PW), 0)
        taps = jnp.where(r8 == TAPS, jnp.sum(ds, axis=0, keepdims=True), 0.0)
        for k in range(TAPS):
            d = TAPS - 1 - k
            reach = cw[k : k + 1, :] * ex_ref[d : d + L, :]
            prior = ds * px_ref[8 - d : 8 - d + L, :]
            if d > 0:
                ahead = jnp.where((seg == meta.segment(pos + d)) & (pos + d < group), 1.0, 0.0)
                reach = reach * tiled(ahead, PW)
                prior = prior * to_shift(meta, c, PW, d)
            dpre = dpre + reach
            taps = taps + jnp.where(r8 == k, jnp.sum(prior, axis=0, keepdims=True), 0.0)
        tap_ref[...] += taps
        dpre = jnp.where(low, dpre, 0.0)
        dproj = dpre.astype(bf16)
        dslab = (dpre[:, IN:] + ddt_ref[...].astype(f32)).astype(bf16)
        dproj = jnp.concatenate([dproj[:, :IN], dslab], axis=1)
        nb = nb_ref[...]
        total[...] += dot(nb, dproj, TN)
        q = dot(dproj, w_ref[:, :PW], NT) + dot(dz_ref[...], wz_ref[:, :IN], NT)
        split_rows(meta, c, q, keep_ref, send_ref)

        @pl.when(c == nC - 1)
        def _():
            low8 = iota((8, PW), 1) < IN + SL
            s = ssum_ref[...]
            zero = jnp.zeros((8, 128), f32)
            pad = jnp.concatenate([s, jnp.zeros((8, PW - IN), f32)], axis=1)
            first = jnp.where(low8, tap_ref[...], 0.0)
            first = jnp.where(r8 == 5, pad[0:1, :], jnp.where(r8 == 6, pad[1:2, :], first))
            lead = first.astype(bf16).astype(f32)
            first = jnp.where(r8 == 7, (first - lead)[TAPS : TAPS + 1, :], first)
            pair = [sums_ref[0:8, :], sums_ref[8:16, :]]
            rest = [p - p.astype(bf16).astype(f32) for p in pair]
            tail = pair + rest + [zero] * (PW // 128 - 4)
            small = jnp.concatenate([first, jnp.concatenate(tail, axis=1)], axis=0).astype(bf16)
            if not DIRECT:
                gs[0][:D, :] = total[...].astype(bf16)
                gs[0][D:, :] = small
            else:
                for i in range(NSH):
                    at = pl.multiple_of(meta.block_row(i), 8)
                    gs[i][:br9, :] = total[pl.ds(at, br9), :].astype(bf16)
                    gs[i][br9:, :] = small

    def conv_back(meta, nb, pr, prh, dz, ddt, dsx, cw9, sums, ssum, edge, slices, edges, shards,
                  zshards, halves):
        step = L // 16
        prior = ((16, PK), lambda i: (jnp.maximum(i * step - 1, 0), 0))
        after = ((8, IN), lambda i: (jnp.minimum((i + 1) * (L // 8), T // 8 - 1), 0))
        ins = [SMEM, rows(nb), rows(pr), prior, whole(prh), rows(dz), rows(ddt), rows(dsx), after,
               whole(cw9), whole(sums), whole(ssum), whole(edge)]
        ins += [whole(a) for a in (*slices, *edges, *shards, *zshards)]
        ins += [rows(h, HB) for h in halves]
        outs = [o_whole((br9 + 16, PW), bf16)] * NSH
        outs += [o_whole((T // 2, D), f32), o_whole((T // 2, D), bf16), o_rows((T // 2, D), bf16, HB)]
        scratch = [pltpu.VMEM((D, PK), bf16), pltpu.VMEM((D, 2 * IN), bf16),
                   pltpu.VMEM((L + 8, PW), f32), pltpu.VMEM((L + 8, PW), f32),
                   pltpu.VMEM((T + 8, 128), f32), pltpu.VMEM((D, PW), f32),
                   pltpu.VMEM((8, PW), f32)]
        got = call(k_conv_back, nC, ins, outs, scratch, 4 * T * D * (PW + IN),
                    [meta, nb, pr, pr, prh, dz, ddt, dsx, dsx, cw9, sums, ssum, edge, *slices, *edges,
                     *shards, *zshards, *halves])
        return got[:NSH], got[NSH:]

    def k_tables(mref, wx, bx, wbc, bbc, bias, alog, skip, gain, mask, cw, cw9, hp, hc, gg, mask8):
        meta = Meta(mref, sizes)
        zeros = lambda n, w: jnp.zeros((n, w), f32)
        left = jnp.concatenate([wx[...], bx[...], zeros(7 - TAPS, IN)], axis=0)
        right = jnp.concatenate([wbc[...], bbc[...], zeros(7 - TAPS, 2 * N)], axis=0)
        cw[...] = jnp.concatenate([left, right], axis=1)
        r, l = iota((2 * N, 128), 0), iota((2 * N, 128), 1)
        pick = jnp.where((r == l + meta.me_t * SL) & (l < SL), 1.0, 0.0)
        cw9[...] = jnp.concatenate([left, dot(right, pick, NN, HI)], axis=1)
        rate = -jnp.exp(alog[...])
        row = iota((8, H), 0)
        rows8 = jnp.where(row == 0, bias[...], jnp.where(row == 1, rate, jnp.where(row == 2, skip[...], 0.0)))
        spread = jnp.where(iota((H, IN), 1) // HW == iota((H, IN), 0), 1.0, 0.0)
        hp[...] = dot(rows8, spread, NN, HI)
        eye = jnp.where(iota((8, 128), 0) == iota((8, 128), 1), 1.0, 0.0)
        turn = jnp.where(iota((8, H), 0) == iota((8, H), 1), 1.0, 0.0)
        hc[...] = dot(dot(turn, rows8, NT, HI), eye, NN, HI)
        gg[...] = jnp.zeros((8, IN), f32) + gain[...]
        mask8[...] = jnp.zeros((8, T), f32) + mask[...].astype(f32)

    def tables(*args):
        outs = [o_whole((8, EXT), f32), o_whole((8, PW), f32), o_whole((8, IN), f32),
                o_whole((8, 128), f32), o_whole((8, IN), f32), o_whole((8, T), f32)]
        return call(k_tables, 1, [SMEM] + [whole(a) for a in args[1:]], outs, [], 0, args)

    def k_finish(*refs):
        meta = Meta(refs[0], sizes)
        first_ref, second_ref = refs[1:3]
        blocks, parts = refs[3 : 3 + n_ctx], refs[3 + n_ctx : 5 + n_ctx]
        alog = refs[5 + n_ctx]
        gz, go, gx, slab_ref, wx, bx, gain_row, h_dt, h_log, h_skip, last, order = refs[6 + n_ctx :]
        zo = parts[0][...]
        for p in parts[1:]:
            zo = zo + p[...].astype(f32)
        gz[...], go[...] = zo[:, :IN], zo[:, IN:]
        total = None
        for r in range(n_ctx):
            b = blocks[r][...].astype(f32)
            total = b[:br9] if total is None else total + b[:br9]
            order[lax.rem(meta.me_c - r + n_ctx, n_ctx)] = b[br9:]
        small = order[0]
        for r in range(1, n_ctx):
            small = small + order[r]
        gx[...] = total[:, :IN]
        slab = total[:, IN:]
        slab_ref[...] = slab
        lane = iota((br9, 128), 1)
        w_slab = first_ref[:, IN : IN + 128].astype(f32)
        gain = jnp.sum(jnp.where(lane == SL + H, w_slab, 0.0), axis=1, keepdims=True)
        d_gain = jnp.sum(first_ref[:, :IN].astype(f32) * total[:, :IN], axis=1, keepdims=True)
        d_gain = d_gain + jnp.sum(second_ref[:, :IN].astype(f32) * zo[:, :IN], axis=1, keepdims=True)
        d_gain = d_gain + jnp.sum(jnp.where(lane < SL + H, w_slab * slab, 0.0), axis=1, keepdims=True)
        last[:br9, :] = jnp.where(lane < SL, slab, jnp.where(lane == SL, d_gain / gain, 0.0))
        top = small[0:8]
        bias = top[TAPS : TAPS + 1] + top[7:8]
        wx[...] = top[:TAPS, :IN]
        bx[...] = bias[:, :IN].reshape(IN)
        gain_row[...] = top[5:6, :IN].reshape(IN)
        taps = jnp.where(iota((8, PW), 0) == TAPS, bias, top)
        last[br9:, :] = jnp.where(iota((8, 128), 1) < SL, taps[:, IN:], 0.0)
        pair = small[8:16, 0:256] + small[8:16, 256:512]
        skip = dot(head_select(), jnp.zeros((8, IN), f32) + top[6:7, :IN], NT, HI)
        eye8 = iota((8, 128), 0) == iota((8, 128), 1)

        def flat(col):
            return jnp.sum(jnp.where(eye8, col, 0.0), axis=0, keepdims=True)[:, :H]

        h_dt[...] = flat(pair[:, 0:1]).reshape(H)
        h_log[...] = (flat(pair[:, 128:129]) * -jnp.exp(alog[...])).reshape(H)
        h_skip[...] = flat(skip[:, 0:1]).reshape(H)

    def finish(meta, first, second, blocks, parts, a_log):
        args = [meta, first, second, *blocks, *parts, a_log]
        outs = [o_whole((br9, IN), f32)] * 3 + [o_whole((br9, 128), f32), o_whole((TAPS, IN), f32),
                o_whole((IN,), f32), o_whole((IN,), f32), o_whole((H,), f32), o_whole((H,), f32),
                o_whole((H,), f32), o_whole((br9 + 8, 128), f32)]
        return call(k_finish, 1, [SMEM] + [whole(a) for a in args[1:]], outs,
                    [pltpu.VMEM((n_ctx, 16, PW), f32)], 0, args)

    def k_spread(mref, *refs):
        meta = Meta(mref, sizes)
        parts = refs[:n_tp]
        wbc, gain, taps, bias, last = refs[n_tp:]
        for k in range(n_tp):
            last[meta.peer(k)] = parts[k][...]
        per = 128 // SL
        lane = iota((br9 + 8, 128), 1)
        for t in range(n_tp // per):
            tile = last[t * per]
            for j in range(1, per):
                tile = jnp.where(lane >= j * SL, pltpu.roll(last[t * per + j], j * SL, 1), tile)
            sl = slice(t * 128, t * 128 + 128)
            wbc[:, sl] = tile[:br9]
            taps[:, sl] = tile[br9 : br9 + TAPS]
            bias[sl] = tile[br9 + TAPS : br9 + TAPS + 1].reshape(128)
        total = last[0][:br9]
        for k in range(1, n_tp):
            total = total + last[k][:br9]
        col = jnp.sum(jnp.where(iota((br9, 128), 1) == SL, total, 0.0), axis=1, keepdims=True)
        eye = iota((br9, br9), 0) == iota((br9, br9), 1)
        gain[...] = jnp.sum(jnp.where(eye, col, 0.0), axis=0, keepdims=True).reshape(br9)

    def spread(meta, parts):
        outs = [o_whole((br9, 2 * N), f32), o_whole((br9,), f32), o_whole((TAPS, 2 * N), f32),
                o_whole((2 * N,), f32)]
        return call(k_spread, 1, [SMEM] + [whole(p) for p in parts], outs,
                    [pltpu.VMEM((n_tp, br9 + 8, 128), f32)], 0, [meta, *parts])

    return dict(tables=tables, finish=finish, spread=spread, project=project, intra=intra, gate=gate, output=output, norm=norm,
                intra_back=intra_back, outer=outer, scan_back=scan_back, conv_back=conv_back,
                SL=SL, PW=PW)


def block(x_in, norm_gain, w_z, w_x, w_bc, w_dt, w_out, conv_wx, conv_bx, conv_wbc, conv_bbc, dt_bias,
          a_log, d_skip, gate_gain, seq_lens, token_mask, d_out):
    T, D = x_in.shape
    H, IN, N, TAPS = dt_bias.shape[0], w_z.shape[1], w_bc.shape[1] // 2, conv_wx.shape[0]
    n_sh, n_ctx, n_tp = (lax.axis_size(a) for a in ("shard", "ctx", "tp"))
    me_s, me_c, me_t = (lax.axis_index(a) for a in ("shard", "ctx", "tp"))
    direct = n_sh == 2 and n_ctx == 4
    NSH = n_sh * n_ctx if direct else 1
    seqs = seq_lens.shape[1]
    sizes = dict(T=T, D=D, IN=IN, N=N, H=H, TAPS=TAPS, tp=n_tp, ctx=n_ctx, seqs=seqs, shards=NSH)
    ops = build(sizes)
    SL = ops["SL"]
    HW = IN // H
    br = w_z.shape[0]

    def ring(count, step):
        return [(i, (i + step) % count) for i in range(count)]

    def xor(count, step):
        return [(i, i ^ step) for i in range(count)]

    def gather(part):
        if not direct:
            return [lax.all_gather(part, ("shard", "ctx"), axis=0, tiled=True)]
        here = [part]
        for k in range(1, n_ctx):
            here.append(lax.ppermute(part, "ctx", ring(n_ctx, k)))
        there = []
        for p in here:
            there.append(lax.ppermute(p, "shard", ring(n_sh, 1)))
        return here + there

    meta = jnp.concatenate([jnp.stack([me_s, me_c, me_t]).astype(jnp.int32), seq_lens[0]])

    w_slice = lax.dynamic_slice_in_dim(w_bc, me_t * SL, SL, 1)
    first = jnp.concatenate(
        [w_x, w_slice, w_dt, norm_gain[:, None], jnp.zeros((br, 127 - SL - H), bf16), w_bc], axis=1
    )
    x_tail = lax.ppermute(x_in[T - 8 :], "ctx", [(i, i + 1) for i in range(n_ctx - 1)])
    shards = gather(first)
    second = jnp.concatenate([w_z, w_out], axis=1)
    shards2 = gather(second)

    cw, cw9, hp, hc, gg, mask8 = ops["tables"](
        meta, conv_wx, conv_bx[None, :], conv_wbc, conv_bbc[None, :], dt_bias[None, :],
        a_log[None, :], d_skip[None, :], gate_gain[None, :], token_mask[None, :])

    (nb, pr, prh, sm, act, dt, cum, dtr, cumr, hpre, pp, pack, gain_row) = ops["project"](
        meta, x_in, x_tail, cw, hp, hc, mask8, shards)
    packs = [lax.ppermute(pack, "ctx", [(i, i + k) for i in range(n_ctx - k)]) for k in range(1, n_ctx)]
    y_in = ops["intra"](meta, act, dt, cum, cumr)
    z, dm = ops["gate"](meta, nb, d_out, shards2)
    y, stat, entry = ops["output"](meta, act, cum, y_in, z, dm, hpre, pp, hp, gg, packs)
    stats = [stat] + [lax.ppermute(stat, "tp", xor(n_tp, k)) for k in range(1, n_tp)]
    mix, dz, dy, suf, psuf, bpack, ssum = ops["norm"](meta, act, cum, y, z, dm, hp, gg, stats)
    bpacks = []
    for k in range(1, n_ctx):
        bpacks.append(lax.ppermute(bpack, "ctx", [(i + k, i) for i in range(n_ctx - k)]))
    dxd, dbc = ops["intra_back"](meta, act, dt, cum, cumr, dy)
    groups, b_keep, b_send = ops["outer"](meta, nb, d_out, mix, dz, shards2)

    def both_halves(part):
        mine = part.astype(bf16)
        other = lax.ppermute(mine, "tp", xor(n_tp, 1))
        flip = me_t % 2 == 1
        low, high = jnp.where(flip, other, mine), jnp.where(flip, mine, other)
        return jnp.concatenate([low, high], axis=0).astype(f32)

    b_got = lax.ppermute(b_send, "tp", xor(n_tp, 1))
    (dsx, ddt, sums, edge, b_pair), slices, edges = ops["scan_back"](
        meta, act, sm, pr, dt, cum, dtr, y, dy, dxd, dbc, hpre, pp, entry, suf, psuf, hp, hc, mask8,
        b_keep, b_got, bpacks)
    got_edge = lax.ppermute(edge, "ctx", [(i + 1, i) for i in range(n_ctx - 1)])
    got_slices = [slices[0]] + [lax.ppermute(slices[k], "tp", xor(n_tp, k)) for k in range(1, n_tp)]
    got_edges = [
        lax.ppermute(edges[k - 1], ("ctx", "tp"),
                     [((i + 1) * n_tp + j, i * n_tp + (j ^ k)) for i in range(n_ctx - 1) for j in range(n_tp)])
        for k in range(1, n_tp)
    ]
    halves = [b_pair] + [lax.ppermute(b_pair, "tp", xor(n_tp, k)) for k in range(2, n_tp, 2)]
    if direct:
        total = groups[0].astype(f32)
        for r in range(1, n_ctx):
            got = lax.ppermute(groups[r], "ctx", ring(n_ctx, r))
            total = total + got.astype(f32)
        other = lax.ppermute(total[br:].astype(bf16), "shard", ring(n_sh, 1))
        parts = [total[:br], other]
    grads, (q_keep, q_send, b_half) = ops["conv_back"](
        meta, nb, pr, prh, dz, ddt, dsx, cw9, sums, ssum, got_edge, got_slices, got_edges, shards,
        shards2, halves)
    if direct:
        moved = []
        for r in [*range(1, n_ctx), 0]:
            got = lax.ppermute(grads[n_ctx + r], "shard", ring(n_sh, 1))
            moved.append(pair_sum(grads[r], got))
        blocks = [moved[-1]]
        for r in range(1, n_ctx):
            blocks.append(lax.ppermute(moved[r - 1], "ctx", ring(n_ctx, r)))

    q_got = lax.ppermute(q_send, "tp", xor(n_tp, 1))
    q_pair = pair_sum(q_keep, q_got)
    q_half = q_pair.astype(f32)
    for k in range(2, n_tp, 2):
        q_half = q_half + lax.ppermute(q_pair, "tp", xor(n_tp, k)).astype(f32)
    block_out = x_in + both_halves(b_half)

    x_half = lax.dynamic_slice_in_dim(x_in, (me_t % 2) * (T // 2), T // 2, 0)
    inv = lax.rsqrt(jnp.mean(x_half * x_half, axis=1, keepdims=True) + norm_eps)
    q_half = q_half * gain_row[0:1, :]
    row_dot = jnp.sum(q_half * x_half, axis=1, keepdims=True)
    d_input = d_out + both_halves(q_half * inv - x_half * (inv * inv * inv) * row_dot / D)

    if direct:
        g_z, g_out, g_x, g_slab, d_cx, d_bx, d_gg, d_dt_bias, d_a_log, d_skips, last = ops["finish"](
            meta, first, second, blocks, parts, a_log[None, :])
        lasts = [last] + [lax.ppermute(last, "tp", xor(n_tp, k)) for k in range(1, n_tp)]
        d_w_bc, d_norm_gain, d_cbc, d_bbc = ops["spread"](meta, lasts)
        return (
            block_out, d_input, d_norm_gain, g_z, g_x, d_w_bc, g_slab[:, SL : SL + H], g_out,
            d_cx, d_bx, d_cbc, d_bbc, d_dt_bias, d_a_log, d_skips, d_gg,
        )

    axes = ("shard", "ctx")
    total = lax.psum_scatter(groups[0].astype(f32), axes, scatter_dimension=0, tiled=True)
    g_first = lax.psum_scatter(grads[0][:D].astype(f32), axes, scatter_dimension=0, tiled=True)
    small = lax.psum(grads[0][D:].astype(f32), axes)
    bias_row = small[TAPS] + small[7]
    sums = small[8 : 8 + H, 0:256] + small[8 : 8 + H, 256:512]
    gain = norm_gain.astype(f32)[:, None]
    g_z, g_out = total[:, :IN], total[:, IN:]
    w_slab = jnp.concatenate([w_slice, w_dt], axis=1).astype(f32)
    g_slab = g_first[:, IN : IN + SL + H]
    d_gain = jnp.sum(w_z.astype(f32) * g_z + w_x.astype(f32) * g_first[:, :IN], axis=1)
    d_gain = (d_gain + jnp.sum(w_slab * g_slab, axis=1)) / gain[:, 0]
    last = jnp.concatenate([
        jnp.concatenate([g_slab[:, :SL], d_gain[:, None], jnp.zeros((br, 127 - SL), f32)], axis=1),
        jnp.pad(jnp.concatenate([small[:TAPS], bias_row[None, :]], axis=0)[:, IN : IN + SL],
                ((0, 7 - TAPS), (0, 128 - SL)))], axis=0)
    last = lax.all_gather(last, "tp")
    d_w_bc = jnp.concatenate([last[k, :br, :SL] for k in range(n_tp)], axis=1)
    d_norm_gain = jnp.sum(last[:, :br, SL], axis=0)
    d_cbc = jnp.concatenate([last[k, br : br + TAPS + 1, :SL] for k in range(n_tp)], axis=1)
    return (
        block_out, d_input, d_norm_gain,
        g_z, g_first[:, :IN], d_w_bc, g_slab[:, SL:], g_out,
        small[:TAPS, :IN], bias_row[:IN], d_cbc[:TAPS], d_cbc[TAPS],
        sums[:, 0], sums[:, 128] * -jnp.exp(a_log),
        jnp.sum(small[6, :IN].reshape(H, HW), axis=1), small[5, :IN],
    )


def solution(mesh):
    row = ("shard", "ctx")
    in_specs = (
        P(row, None), P(row), P(row, "tp"), P(row, "tp"), P(row, None), P(row, "tp"), P(row, "tp"),
        P(None, "tp"), P("tp"), P(), P(), P("tp"), P("tp"), P("tp"), P("tp"), P("shard", None), P(row),
        P(row, None),
    )
    out_specs = (
        P(row, None), P(row, None), P(row), P(row, "tp"), P(row, "tp"), P(row, None), P(row, "tp"),
        P(row, "tp"), P(None, "tp"), P("tp"), P(), P(), P("tp"), P("tp"), P("tp"), P("tp"),
    )
    return jax.shard_map(block, mesh=mesh, in_specs=in_specs, out_specs=out_specs, check_vma=False)
```

profile of v0, /device:TPU:0, one launch (start us, length us, event | category | flops | bytes accessed | tf_op | source)
XLA Modules:
  0.0 228.0 jit_solution(7175630346149105144)
XLA Ops:
  2.4 5.1 %collective-permute-start.10 = (bf16[96,768]{1,0:T(8,128)(2,1)S(1)}, bf16[96,768]{1,0:T(8,128)(2,1)S(1)}, u32[]{:S(2)}, u32[]{:S(2)}) collective-permute-start(bf16[96,768]{1,0:T(8,128)(2,1)S(1)} %constant_dynamic-update-slice_fusion.refs_3_.refs_5_.refs_28_.refs_2_), channel_id=1, source_target_pairs={{0,12},{4,0},{8,4},{12,8},{1,13},{5,1},{9,5},{13,9},{2,14},{6,2},{... | collective-permute-start | bytes 442376 | tf_op jit(solution)/shard_map/ppermute | solution.py:984
  11.5 2.6 %collective-permute-start.2 = (bf16[96,768]{1,0:T(8,128)(2,1)S(1)}, bf16[96,768]{1,0:T(8,128)(2,1)S(1)}, u32[]{:S(2)}, u32[]{:S(2)}) collective-permute-start(bf16[96,768]{1,0:T(8,128)(2,1)S(1)} %concatenate.16.refs_7_.refs_20_.refs_1_), channel_id=1, source_target_pairs={{0,8},{4,12},{8,0},{12,4},{1,9},{5,13},{9,1},{13,5},{2,10},{6,14},... | collective-permute-start | bytes 442376 | tf_op jit(solution)/shard_map/ppermute | solution.py:984
  14.8 3.8 %collective-permute-start = (f32[8,768]{1,0:T(8,128)S(1)}, f32[8,768]{1,0:T(8,128)S(1)}, u32[]{:S(2)}, u32[]{:S(2)}) collective-permute-start(f32[8,768]{1,0:T(8,128)S(1)} %slice.16), channel_id=1, source_target_pairs={{0,4},{4,8},{8,12},{1,5},{5,9},{9,13},{2,6},{6,10},{10,14},{3,7},{... | collective-permute-start | bytes 73736 | tf_op jit(solution)/shard_map/ppermute | solution.py:996
  18.6 2.1 collective-permute-done.refs_2_
  20.7 7.0 %collective-permute-start.1 = (bf16[96,768]{1,0:T(8,128)(2,1)S(1)}, bf16[96,768]{1,0:T(8,128)(2,1)S(1)}, u32[]{:S(2)}, u32[]{:S(2)}) collective-permute-start(bf16[96,768]{1,0:T(8,128)(2,1)S(1)} %concatenate.16.refs_7_.refs_20_.refs_1_), channel_id=1, source_target_pairs={{0,4},{4,8},{8,12},{12,0},{1,5},{5,9},{9,13},{13,1},{2,6},{6,10},{... | collective-permute-start | bytes 442376 | tf_op jit(solution)/shard_map/ppermute | solution.py:984
  27.8 2.5 %collective-permute-start.8 = (bf16[96,768]{1,0:T(8,128)(2,1)S(1)}, bf16[96,768]{1,0:T(8,128)(2,1)S(1)}, u32[]{:S(2)}, u32[]{:S(2)}) collective-permute-start(bf16[96,768]{1,0:T(8,128)(2,1)S(1)} %constant_dynamic-update-slice_fusion.refs_3_.refs_5_.refs_28_.refs_2_), channel_id=1, source_target_pairs={{0,4},{4,8},{8,12},{12,0},{1,5},{5,9},{9,13},{13,1},{2,6},{6,10},{... | collective-permute-start | bytes 442376 | tf_op jit(solution)/shard_map/ppermute | solution.py:984
  48.6 1.8 shard_map.297
  51.0 9.3 %shard_map.298 = (bf16[512,768]{1,0:T(8,128)(2,1)}, bf16[512,768]{1,0:T(8,128)(2,1)}, f32[8,768]{1,0:T(8,128)}, f32[512,640]{1,0:T(8,128)}, f32[512,640]{1,0:T(8...) custom-call(s32[6]{0:T(128)} %pad_add_fusion.refs_0_, ...), custom_call_target="tpu_custom_call" | custom-call | flops 603979776 | bytes 9834520 | tf_op jit(solution)/shard_map/pallas_call | solution.py:172
  60.4 3.2 %collective-permute-start.17 = (bf16[144,384]{1,0:T(8,128)(2,1)}, bf16[144,384]{1,0:T(8,128)(2,1)S(1)}, u32[]{:S(2)}, u32[]{:S(2)}) collective-permute-start(bf16[144,384]{1,0:T(8,128)(2,1)} %get-tuple-element.109), channel_id=1, source_target_pairs={{0,12},{1,13},{2,14},{3,15},{16,28},{17,29},{18,30},{19,31}} | collective-permute-start | bytes 331784 | tf_op jit(solution)/shard_map/ppermute | solution.py:1007
  65.0 2.5 %collective-permute-start.15 = (bf16[144,384]{1,0:T(8,128)(2,1)}, bf16[144,384]{1,0:T(8,128)(2,1)S(1)}, u32[]{:S(2)}, u32[]{:S(2)}) collective-permute-start(bf16[144,384]{1,0:T(8,128)(2,1)} %get-tuple-element.109), channel_id=1, source_target_pairs={{0,4},{4,8},{8,12},{1,5},{5,9},{9,13},{2,6},{6,10},{10,14},{3,7},{... | collective-permute-start | bytes 331784 | tf_op jit(solution)/shard_map/ppermute | solution.py:1007
  67.5 4.0 %shard_map.299.refs_3_ = f32[512,384]{1,0:T(8,128)} custom-call(s32[6]{0:T(128)} %pad_add_fusion.refs_0_, f32[512,640]{1,0:T(8,128)} %get-tuple-element.100.refs_1_, f32[512,384]{1,0:T(8,128)} %get-tuple-element.102.refs_2_.refs_4_, f32[512,384]{1,0:T(8,128)} %get-tuple-element.101.refs_3_.refs_2_.refs_5_, f32[8,512]{1,0:T(8,128)} %get-tuple-element.103.refs_4_), custom_call_target="tpu_custom_call" | custom-call | flops 100663296 | bytes 3686424 | tf_op jit(solution)/shard_map/pallas_call | solution.py:172
  72.2 3.6 %shard_map.300 = (bf16[512,384]{1,0:T(8,128)(2,1)}, f32[512,384]{1,0:T(8,128)}) custom-call(s32[6]{0:T(128)} %pad_add_fusion.refs_0_, bf16[512,768]{1,0:T(8,128)(2,1)} %get-tuple-element.97.refs_1_, f32[512,768]{1,0:T(8,128)} %refs_2_.3, bf16[96,768]{1,0:T(8,128)(2,1)} %copy-done.3, bf16[96,768]{1,0:T(8,128)(2,1)} %copy-done.7, bf16[96,768]{1,0:T(8,128)(2,1)} %copy-done.6, ...), custom_call_target="tpu_custom_call" | custom-call | flops 603979776 | bytes 4718616 | tf_op jit(solution)/shard_map/pallas_call | solution.py:172
  76.7 5.3 %shard_map.301 = (f32[512,384]{1,0:T(8,128)}, f32[8,512]{1,0:T(8,128)}, f32[128,384]{1,0:T(8,128)}) custom-call(s32[6]{0:T(128)} %pad_add_fusion.refs_0_, f32[512,640]{1,0:T(8,128)} %get-tuple-element.100.refs_1_, f32[512,384]{1,0:T(8,128)} %get-tuple-element.101.refs_3_.refs_2_.refs_5_, f32[512,384]{1,0:T(8,128)} %shard_map.299.refs_3_, ...), custom_call_target="tpu_custom_call" | custom-call | flops 100663296 | bytes 6463512 | tf_op jit(solution)/shard_map/pallas_call | solution.py:172
  86.7 6.3 %shard_map.302 = (bf16[512,384]{1,0:T(8,128)(2,1)}, bf16[512,384]{1,0:T(8,128)(2,1)}, f32[512,384]{1,0:T(8,128)}, f32[512,384]{1,0:T(8,128)}, f32[32,384]{1,0:T(...) custom-call(s32[6]{0:T(128)} %pad_add_fusion.refs_0_, f32[512,640]{1,0:T(8,128)} %get-tuple-element.100.refs_1_, ...), custom_call_target="tpu_custom_call" | custom-call | flops 50331648 | bytes 6684696 | tf_op jit(solution)/shard_map/pallas_call | solution.py:172
  93.0 6.8 %shard_map.304 = (bf16[192,768]{1,0:T(8,128)(2,1)}, bf16[192,768]{1,0:T(8,128)(2,1)}, bf16[192,768]{1,0:T(8,128)(2,1)}, bf16[192,768]{1,0:T(8,128)(2,1)}, f32[256,768]{1,0:T(8,128)}, /*index=5*/bf16[256,768]{1,0:T(8,128)(2,1)}) custom-call(s32[6]{0:T(128)} %pad_add_fusion.refs_0_, bf16[512,768]{1,0:T(8,128)(2,1)} %get-tuple-element.97.refs_1_, ...), custom_call_target="tpu_custom_call" | custom-call | flops 905969664 | bytes 6684696 | tf_op jit(solution)/shard_map/pallas_call | solution.py:172
  104.3 6.5 %shard_map.303 = (f32[512,384]{1,0:T(8,128)}, f32[512,256]{1,0:T(8,128)}) custom-call(s32[6]{0:T(128)} %pad_add_fusion.refs_0_, f32[512,640]{1,0:T(8,128)} %get-tuple-element.100.refs_1_, f32[512,384]{1,0:T(8,128)} %get-tuple-element.102.refs_2_.refs_4_, f32[512,384]{1,0:T(8,128)} %get-tuple-element.101.refs_3_.refs_2_.refs_5_, ...), custom_call_target="tpu_custom_call" | custom-call | flops 201326592 | bytes 4997144 | tf_op jit(solution)/shard_map/pallas_call | solution.py:172
  110.8 3.0 %collective-permute-done.23.refs_24_ = bf16[144,384]{1,0:T(8,128)(2,1)S(1)} collective-permute-done((bf16[144,384]{1,0:T(8,128)(2,1)S(1)}, bf16[144,384]{1,0:T(8,128)(2,1)S(1)}, u32[]{:S(2)}, u32[]{:S(2)}) %collective-permute-start.23) | collective-permute-done | bytes 110624 | tf_op jit(solution)/shard_map/ppermute | solution.py:1015
  114.7 12.8 %shard_map.305 = (f32[512,384]{1,0:T(8,128)}, bf16[512,128]{1,0:T(8,128)(2,1)}, f32[16,128]{1,0:T(8,128)}, f32[8,512]{1,0:T(8,128)}, bf16[256,768]{1,0:T(8,128)(...) custom-call(s32[6]{0:T(128)} %pad_add_fusion.refs_0_, ...), custom_call_target="tpu_custom_call" | custom-call | flops 150994944 | bytes 14155800 | tf_op jit(solution)/shard_map/pallas_call | solution.py:172
  132.1 4.8 %collective-permute-done.29.refs_17_ = f32[8,128]{1,0:T(8,128)S(1)} collective-permute-done((f32[8,128]{1,0:T(8,128)}, f32[8,128]{1,0:T(8,128)S(1)}, u32[]{:S(2)}, u32[]{:S(2)}) %collective-permute-start.29) | collective-permute-done | bytes 4128 | tf_op jit(solution)/shard_map/ppermute | solution.py:1033
  138.3 5.3 %collective-permute-done.30.refs_18_ = f32[8,128]{1,0:T(8,128)S(1)} collective-permute-done((f32[8,128]{1,0:T(8,128)}, f32[8,128]{1,0:T(8,128)S(1)}, u32[]{:S(2)}, u32[]{:S(2)}) %collective-permute-start.30) | collective-permute-done | bytes 4128 | tf_op jit(solution)/shard_map/ppermute | solution.py:1033
  144.9 4.7 %collective-permute-done.31.refs_19_ = f32[8,128]{1,0:T(8,128)S(1)} collective-permute-done((f32[8,128]{1,0:T(8,128)}, f32[8,128]{1,0:T(8,128)S(1)}, u32[]{:S(2)}, u32[]{:S(2)}) %collective-permute-start.31) | collective-permute-done | bytes 4128 | tf_op jit(solution)/shard_map/ppermute | solution.py:1033
  150.9 4.5 %collective-permute-done.25.refs_12_ = f32[8,512]{1,0:T(8,128)S(1)} collective-permute-done((f32[8,512]{1,0:T(8,128)}, f32[8,512]{1,0:T(8,128)S(1)}, u32[]{:S(2)}, u32[]{:S(2)}) %collective-permute-start.25) | collective-permute-done | bytes 16416 | tf_op jit(solution)/shard_map/ppermute | solution.py:1030
  156.3 10.0 %shard_map.306 = (bf16[112,512]{1,0:T(8,128)(2,1)}, bf16[112,512]{1,0:T(8,128)(2,1)}, bf16[112,512]{1,0:T(8,128)(2,1)}, bf16[112,512]{1,0:T(8,128)(2,1)}, bf16[1...) custom-call(s32[6]{0:T(128)} %pad_add_fusion.refs_0_, ...), custom_call_target="tpu_custom_call" | custom-call | flops 1409286144 | bytes 10444824 | tf_op jit(solution)/shard_map/pallas_call | solution.py:172
  166.4 1.9 collective-permute-start.44
  168.3 2.6 %collective-permute-start.46 = (bf16[192,768]{1,0:T(8,128)(2,1)S(1)}, bf16[192,768]{1,0:T(8,128)(2,1)S(1)}, u32[]{:S(2)}, u32[]{:S(2)}) collective-permute-start(bf16[192,768]{1,0:T(8,128)(2,1)S(1)} %copy-done.46), channel_id=1, source_target_pairs={{0,12},{4,0},{8,4},{12,8},{1,13},{5,1},{9,5},{13,9},{2,14},{6,2},{... | collective-permute-start | bytes 884744 | tf_op jit(solution)/shard_map/ppermute | solution.py:1041
  172.9 2.0 shard_map.307
  174.9 3.3 %collective-permute-done.44 = bf16[192,768]{1,0:T(8,128)(2,1)S(1)} collective-permute-done((bf16[192,768]{1,0:T(8,128)(2,1)S(1)}, bf16[192,768]{1,0:T(8,128)(2,1)S(1)}, u32[]{:S(2)}, u32[]{:S(2)}) %collective-permute-start.44) | collective-permute-done | bytes 294944 | tf_op jit(solution)/shard_map/ppermute | solution.py:1041
  178.7 11.6 %collective-permute-done.45 = bf16[192,768]{1,0:T(8,128)(2,1)S(1)} collective-permute-done((bf16[192,768]{1,0:T(8,128)(2,1)S(1)}, bf16[192,768]{1,0:T(8,128)(2,1)S(1)}, u32[]{:S(2)}, u32[]{:S(2)}) %collective-permute-start.45) | collective-permute-done | bytes 294944 | tf_op jit(solution)/shard_map/ppermute | solution.py:1041
  194.8 5.4 %collective-permute-start.39 = (bf16[112,512]{1,0:T(8,128)(2,1)}, bf16[112,512]{1,0:T(8,128)(2,1)}, u32[]{:S(2)}, u32[]{:S(2)}) collective-permute-start(bf16[112,512]{1,0:T(8,128)(2,1)} %shard_map.309), channel_id=1, source_target_pairs={{0,4},{4,8},{8,12},{12,0},{1,5},{5,9},{9,13},{13,1},{2,6},{6,10},{... | collective-permute-start | bytes 344072 | tf_op jit(solution)/shard_map/ppermute | solution.py:1055
  200.2 1.8 shard_map.310
  202.0 2.1 collective-permute-start.41
  211.4 2.4 %shard_map.312 = (f32[96,384]{1,0:T(8,128)}, f32[96,384]{1,0:T(8,128)}, f32[96,384]{1,0:T(8,128)}, f32[96,128]{1,0:T(8,128)}, f32[4,384]{1,0:T(4,128)}, /*index=...) custom-call(s32[6]{0:T(128)} %pad_add_fusion.refs_0_, ...), custom_call_target="tpu_custom_call" | custom-call | bytes 1750136 | tf_op jit(solution)/shard_map/pallas_call | solution.py:172
  (211 shorter events, 76.0 us)
Async XLA Ops:
  2.4 25.3 %collective-permute-start.10 = (bf16[96,768]{1,0:T(8,128)(2,1)S(1)}, bf16[96,768]{1,0:T(8,128)(2,1)S(1)}, u32[]{:S(2)}, u32[]{:S(2)}) collective-permute-start(bf16[96,768]{1,0:T(8,128)(2,1)S(1)} %constant_dynamic-update-slice_fusion.refs_3_.refs_5_.refs_28_.refs_2_), channel_id=1, source_target_pairs={{0,12},{4,0},{8,4},{12,8},{1,13},{5,1},{9,5},{13,9},{2,14},{6,2},{... | collective-permute-start | bytes 442376 | tf_op jit(solution)/shard_map/ppermute | solution.py:984
  7.6 22.7 %collective-permute-start.9 = (bf16[96,768]{1,0:T(8,128)(2,1)S(1)}, bf16[96,768]{1,0:T(8,128)(2,1)S(1)}, u32[]{:S(2)}, u32[]{:S(2)}) collective-permute-start(bf16[96,768]{1,0:T(8,128)(2,1)S(1)} %constant_dynamic-update-slice_fusion.refs_3_.refs_5_.refs_28_.refs_2_), channel_id=1, source_target_pairs={{0,8},{4,12},{8,0},{12,4},{1,9},{5,13},{9,1},{13,5},{2,10},{6,14},... | collective-permute-start | bytes 442376 | tf_op jit(solution)/shard_map/ppermute | solution.py:984
  11.0 20.8 %collective-permute-start.3 = (bf16[96,768]{1,0:T(8,128)(2,1)S(1)}, bf16[96,768]{1,0:T(8,128)(2,1)S(1)}, u32[]{:S(2)}, u32[]{:S(2)}) collective-permute-start(bf16[96,768]{1,0:T(8,128)(2,1)S(1)} %concatenate.16.refs_7_.refs_20_.refs_1_), channel_id=1, source_target_pairs={{0,12},{4,0},{8,4},{12,8},{1,13},{5,1},{9,5},{13,9},{2,14},{6,2},{... | collective-permute-start | bytes 442376 | tf_op jit(solution)/shard_map/ppermute | solution.py:984
  11.5 20.8 %collective-permute-start.2 = (bf16[96,768]{1,0:T(8,128)(2,1)S(1)}, bf16[96,768]{1,0:T(8,128)(2,1)S(1)}, u32[]{:S(2)}, u32[]{:S(2)}) collective-permute-start(bf16[96,768]{1,0:T(8,128)(2,1)S(1)} %concatenate.16.refs_7_.refs_20_.refs_1_), channel_id=1, source_target_pairs={{0,8},{4,12},{8,0},{12,4},{1,9},{5,13},{9,1},{13,5},{2,10},{6,14},... | collective-permute-start | bytes 442376 | tf_op jit(solution)/shard_map/ppermute | solution.py:984
  20.7 13.1 %collective-permute-start.1 = (bf16[96,768]{1,0:T(8,128)(2,1)S(1)}, bf16[96,768]{1,0:T(8,128)(2,1)S(1)}, u32[]{:S(2)}, u32[]{:S(2)}) collective-permute-start(bf16[96,768]{1,0:T(8,128)(2,1)S(1)} %concatenate.16.refs_7_.refs_20_.refs_1_), channel_id=1, source_target_pairs={{0,4},{4,8},{8,12},{12,0},{1,5},{5,9},{9,13},{13,1},{2,6},{6,10},{... | collective-permute-start | bytes 442376 | tf_op jit(solution)/shard_map/ppermute | solution.py:984
  32.3 11.0 %collective-permute-start.6 = (bf16[96,768]{1,0:T(8,128)(2,1)S(1)}, bf16[96,768]{1,0:T(8,128)(2,1)S(1)}, u32[]{:S(2)}, u32[]{:S(2)}) collective-permute-start(bf16[96,768]{1,0:T(8,128)(2,1)S(1)} %collective-permute-done.2.refs_9_.refs_22_), channel_id=1, source_target_pairs={{0,16},{16,0},{1,17},{17,1},{2,18},{18,2},{3,19},{19,3},{4,20},{20... | collective-permute-start | bytes 442376 | tf_op jit(solution)/shard_map/ppermute | solution.py:987
  33.8 16.6 %collective-permute-start.5 = (bf16[96,768]{1,0:T(8,128)(2,1)S(1)}, bf16[96,768]{1,0:T(8,128)(2,1)S(1)}, u32[]{:S(2)}, u32[]{:S(2)}) collective-permute-start(bf16[96,768]{1,0:T(8,128)(2,1)S(1)} %collective-permute-done.1.refs_8_.refs_21_), channel_id=1, source_target_pairs={{0,16},{16,0},{1,17},{17,1},{2,18},{18,2},{3,19},{19,3},{4,20},{20... | collective-permute-start | bytes 442376 | tf_op jit(solution)/shard_map/ppermute | solution.py:987
  34.7 29.0 %collective-permute-start.11 = (bf16[96,768]{1,0:T(8,128)(2,1)S(1)}, bf16[96,768]{1,0:T(8,128)(2,1)S(1)}, u32[]{:S(2)}, u32[]{:S(2)}) collective-permute-start(bf16[96,768]{1,0:T(8,128)(2,1)S(1)} %constant_dynamic-update-slice_fusion.refs_3_.refs_5_.refs_28_.refs_2_), channel_id=1, source_target_pairs={{0,16},{16,0},{1,17},{17,1},{2,18},{18,2},{3,19},{19,3},{4,20},{20... | collective-permute-start | bytes 442376 | tf_op jit(solution)/shard_map/ppermute | solution.py:987
  37.0 28.0 %collective-permute-start.14 = (bf16[96,768]{1,0:T(8,128)(2,1)S(1)}, bf16[96,768]{1,0:T(8,128)(2,1)S(1)}, u32[]{:S(2)}, u32[]{:S(2)}) collective-permute-start(bf16[96,768]{1,0:T(8,128)(2,1)S(1)} %collective-permute-done.10.refs_6_.refs_8_.refs_31_), channel_id=1, source_target_pairs={{0,16},{16,0},{1,17},{17,1},{2,18},{18,2},{3,19},{19,3},{4,20},{20... | collective-permute-start | bytes 442376 | tf_op jit(solution)/shard_map/ppermute | solution.py:987
  40.1 31.4 %collective-permute-start.13 = (bf16[96,768]{1,0:T(8,128)(2,1)S(1)}, bf16[96,768]{1,0:T(8,128)(2,1)S(1)}, u32[]{:S(2)}, u32[]{:S(2)}) collective-permute-start(bf16[96,768]{1,0:T(8,128)(2,1)S(1)} %collective-permute-done.9.refs_5_.refs_7_.refs_30_), channel_id=1, source_target_pairs={{0,16},{16,0},{1,17},{17,1},{2,18},{18,2},{3,19},{19,3},{4,20},{20... | collective-permute-start | bytes 442376 | tf_op jit(solution)/shard_map/ppermute | solution.py:987
  43.3 28.2 %collective-permute-start.12 = (bf16[96,768]{1,0:T(8,128)(2,1)S(1)}, bf16[96,768]{1,0:T(8,128)(2,1)S(1)}, u32[]{:S(2)}, u32[]{:S(2)}) collective-permute-start(bf16[96,768]{1,0:T(8,128)(2,1)S(1)} %collective-permute-done.8.refs_4_.refs_6_.refs_29_), channel_id=1, source_target_pairs={{0,16},{16,0},{1,17},{17,1},{2,18},{18,2},{3,19},{19,3},{4,20},{20... | collective-permute-start | bytes 442376 | tf_op jit(solution)/shard_map/ppermute | solution.py:987
  60.4 15.5 %collective-permute-start.17 = (bf16[144,384]{1,0:T(8,128)(2,1)}, bf16[144,384]{1,0:T(8,128)(2,1)S(1)}, u32[]{:S(2)}, u32[]{:S(2)}) collective-permute-start(bf16[144,384]{1,0:T(8,128)(2,1)} %get-tuple-element.109), channel_id=1, source_target_pairs={{0,12},{1,13},{2,14},{3,15},{16,28},{17,29},{18,30},{19,31}} | collective-permute-start | bytes 331784 | tf_op jit(solution)/shard_map/ppermute | solution.py:1007
  63.7 12.2 %collective-permute-start.16 = (bf16[144,384]{1,0:T(8,128)(2,1)}, bf16[144,384]{1,0:T(8,128)(2,1)S(1)}, u32[]{:S(2)}, u32[]{:S(2)}) collective-permute-start(bf16[144,384]{1,0:T(8,128)(2,1)} %get-tuple-element.109), channel_id=1, source_target_pairs={{0,8},{4,12},{1,9},{5,13},{2,10},{6,14},{3,11},{7,15},{16,24},{20,... | collective-permute-start | bytes 331784 | tf_op jit(solution)/shard_map/ppermute | solution.py:1007
  65.0 10.9 %collective-permute-start.15 = (bf16[144,384]{1,0:T(8,128)(2,1)}, bf16[144,384]{1,0:T(8,128)(2,1)S(1)}, u32[]{:S(2)}, u32[]{:S(2)}) collective-permute-start(bf16[144,384]{1,0:T(8,128)(2,1)} %get-tuple-element.109), channel_id=1, source_target_pairs={{0,4},{4,8},{8,12},{1,5},{5,9},{9,13},{2,6},{6,10},{10,14},{3,7},{... | collective-permute-start | bytes 331784 | tf_op jit(solution)/shard_map/ppermute | solution.py:1007
  99.8 14.0 %collective-permute-start.21 = (bf16[256,768]{1,0:T(8,128)(2,1)}, bf16[256,768]{1,0:T(8,128)(2,1)S(1)}, u32[]{:S(2)}, u32[]{:S(2)}) collective-permute-start(bf16[256,768]{1,0:T(8,128)(2,1)} %get-tuple-element.123), channel_id=1, source_target_pairs={{0,1},{1,0},{2,3},{3,2},{4,5},{5,4},{6,7},{7,6},{8,9},{9,8},{10,11... | collective-permute-start | bytes 1179656 | tf_op jit(solution)/shard_map/ppermute | solution.py:1026
  100.2 10.6 %collective-permute-start.24 = (bf16[144,384]{1,0:T(8,128)(2,1)S(1)}, bf16[144,384]{1,0:T(8,128)(2,1)S(1)}, u32[]{:S(2)}, u32[]{:S(2)}) collective-permute-start(bf16[144,384]{1,0:T(8,128)(2,1)S(1)} %copy-done.49), channel_id=1, source_target_pairs={{12,0},{13,1},{14,2},{15,3},{28,16},{29,17},{30,18},{31,19}} | collective-permute-start | bytes 331784 | tf_op jit(solution)/shard_map/ppermute | solution.py:1015
  101.5 12.3 %collective-permute-start.23 = (bf16[144,384]{1,0:T(8,128)(2,1)S(1)}, bf16[144,384]{1,0:T(8,128)(2,1)S(1)}, u32[]{:S(2)}, u32[]{:S(2)}) collective-permute-start(bf16[144,384]{1,0:T(8,128)(2,1)S(1)} %copy-done.49), channel_id=1, source_target_pairs={{8,0},{12,4},{9,1},{13,5},{10,2},{14,6},{11,3},{15,7},{24,16},{28,... | collective-permute-start | bytes 331784 | tf_op jit(solution)/shard_map/ppermute | solution.py:1015
  102.8 11.0 %collective-permute-start.22 = (bf16[144,384]{1,0:T(8,128)(2,1)S(1)}, bf16[144,384]{1,0:T(8,128)(2,1)S(1)}, u32[]{:S(2)}, u32[]{:S(2)}) collective-permute-start(bf16[144,384]{1,0:T(8,128)(2,1)S(1)} %copy-done.49), channel_id=1, source_target_pairs={{4,0},{8,4},{12,8},{5,1},{9,5},{13,9},{6,2},{10,6},{14,10},{7,3},{... | collective-permute-start | bytes 331784 | tf_op jit(solution)/shard_map/ppermute | solution.py:1015
  127.5 28.0 %collective-permute-start.32 = (bf16[256,768]{1,0:T(8,128)(2,1)}, bf16[256,768]{1,0:T(8,128)(2,1)S(1)}, u32[]{:S(2)}, u32[]{:S(2)}) collective-permute-start(bf16[256,768]{1,0:T(8,128)(2,1)} %get-tuple-element.138.refs_36_), channel_id=1, source_target_pairs={{0,2},{1,3},{2,0},{3,1},{4,6},{5,7},{6,4},{7,5},{8,10},{9,11},{10,... | collective-permute-start | bytes 1179656 | tf_op jit(solution)/shard_map/ppermute | solution.py:1037
  129.0 26.5 %collective-permute-start.26 = (bf16[256,128]{1,0:T(8,128)(2,1)}, bf16[256,128]{1,0:T(8,128)(2,1)S(1)}, u32[]{:S(2)}, u32[]{:S(2)}) collective-permute-start(bf16[256,128]{1,0:T(8,128)(2,1)} %get-tuple-element.132), channel_id=1, source_target_pairs={{0,1},{1,0},{2,3},{3,2},{4,5},{5,4},{6,7},{7,6},{8,9},{9,8},{10,11... | collective-permute-start | bytes 196616 | tf_op jit(solution)/shard_map/ppermute | solution.py:1031
  129.0 26.5 %collective-permute-start.27 = (bf16[256,128]{1,0:T(8,128)(2,1)}, bf16[256,128]{1,0:T(8,128)(2,1)S(1)}, u32[]{:S(2)}, u32[]{:S(2)}) collective-permute-start(bf16[256,128]{1,0:T(8,128)(2,1)} %get-tuple-element.133), channel_id=1, source_target_pairs={{0,2},{1,3},{2,0},{3,1},{4,6},{5,7},{6,4},{7,5},{8,10},{9,11},{10,... | collective-permute-start | bytes 196616 | tf_op jit(solution)/shard_map/ppermute | solution.py:1031
  129.6 25.9 %collective-permute-start.28 = (bf16[256,128]{1,0:T(8,128)(2,1)}, bf16[256,128]{1,0:T(8,128)(2,1)S(1)}, u32[]{:S(2)}, u32[]{:S(2)}) collective-permute-start(bf16[256,128]{1,0:T(8,128)(2,1)} %get-tuple-element.134), channel_id=1, source_target_pairs={{0,3},{1,2},{2,1},{3,0},{4,7},{5,6},{6,5},{7,4},{8,11},{9,10},{10,... | collective-permute-start | bytes 196616 | tf_op jit(solution)/shard_map/ppermute | solution.py:1031
  166.4 11.9 %collective-permute-start.44 = (bf16[192,768]{1,0:T(8,128)(2,1)S(1)}, bf16[192,768]{1,0:T(8,128)(2,1)S(1)}, u32[]{:S(2)}, u32[]{:S(2)}) collective-permute-start(bf16[192,768]{1,0:T(8,128)(2,1)S(1)} %copy-done.48), channel_id=1, source_target_pairs={{0,4},{4,8},{8,12},{12,0},{1,5},{5,9},{9,13},{13,1},{2,6},{6,10},{... | collective-permute-start | bytes 884744 | tf_op jit(solution)/shard_map/ppermute | solution.py:1041
  168.3 22.1 %collective-permute-start.45 = (bf16[192,768]{1,0:T(8,128)(2,1)S(1)}, bf16[192,768]{1,0:T(8,128)(2,1)S(1)}, u32[]{:S(2)}, u32[]{:S(2)}) collective-permute-start(bf16[192,768]{1,0:T(8,128)(2,1)S(1)} %copy-done.47), channel_id=1, source_target_pairs={{0,8},{4,12},{8,0},{12,4},{1,9},{5,13},{9,1},{13,5},{2,10},{6,14},... | collective-permute-start | bytes 884744 | tf_op jit(solution)/shard_map/ppermute | solution.py:1041
  168.3 22.6 %collective-permute-start.46 = (bf16[192,768]{1,0:T(8,128)(2,1)S(1)}, bf16[192,768]{1,0:T(8,128)(2,1)S(1)}, u32[]{:S(2)}, u32[]{:S(2)}) collective-permute-start(bf16[192,768]{1,0:T(8,128)(2,1)S(1)} %copy-done.46), channel_id=1, source_target_pairs={{0,12},{4,0},{8,4},{12,8},{1,13},{5,1},{9,5},{13,9},{2,14},{6,2},{... | collective-permute-start | bytes 884744 | tf_op jit(solution)/shard_map/ppermute | solution.py:1041
  170.8 34.8 %collective-permute-start.37 = (bf16[112,512]{1,0:T(8,128)(2,1)}, bf16[112,512]{1,0:T(8,128)(2,1)}, u32[]{:S(2)}, u32[]{:S(2)}) collective-permute-start(bf16[112,512]{1,0:T(8,128)(2,1)} %get-tuple-element.144), channel_id=1, source_target_pairs={{0,16},{16,0},{1,17},{17,1},{2,18},{18,2},{3,19},{19,3},{4,20},{20... | collective-permute-start | bytes 344072 | tf_op jit(solution)/shard_map/ppermute | solution.py:1051
  171.4 20.2 %collective-permute-start.38 = (bf16[112,512]{1,0:T(8,128)(2,1)}, bf16[112,512]{1,0:T(8,128)(2,1)S(1)}, u32[]{:S(2)}, u32[]{:S(2)}) collective-permute-start(bf16[112,512]{1,0:T(8,128)(2,1)} %get-tuple-element.146), channel_id=1, source_target_pairs={{0,16},{16,0},{1,17},{17,1},{2,18},{18,2},{3,19},{19,3},{4,20},{20... | collective-permute-start | bytes 344072 | tf_op jit(solution)/shard_map/ppermute | solution.py:1051
  178.2 16.6 %collective-permute-start.40 = (bf16[112,512]{1,0:T(8,128)(2,1)}, bf16[112,512]{1,0:T(8,128)(2,1)S(1)}, u32[]{:S(2)}, u32[]{:S(2)}) collective-permute-start(bf16[112,512]{1,0:T(8,128)(2,1)} %get-tuple-element.148), channel_id=1, source_target_pairs={{0,16},{16,0},{1,17},{17,1},{2,18},{18,2},{3,19},{19,3},{4,20},{20... | collective-permute-start | bytes 344072 | tf_op jit(solution)/shard_map/ppermute | solution.py:1051
  190.3 11.6 %collective-permute-start.42 = (bf16[112,512]{1,0:T(8,128)(2,1)}, bf16[112,512]{1,0:T(8,128)(2,1)}, u32[]{:S(2)}, u32[]{:S(2)}) collective-permute-start(bf16[112,512]{1,0:T(8,128)(2,1)} %get-tuple-element.150), channel_id=1, source_target_pairs={{0,16},{16,0},{1,17},{17,1},{2,18},{18,2},{3,19},{19,3},{4,20},{20... | collective-permute-start | bytes 344072 | tf_op jit(solution)/shard_map/ppermute | solution.py:1051
  190.8 31.3 %collective-permute-start.35 = (bf16[256,768]{1,0:T(8,128)(2,1)}, bf16[256,768]{1,0:T(8,128)(2,1)S(1)}, u32[]{:S(2)}, u32[]{:S(2)}) collective-permute-start(bf16[256,768]{1,0:T(8,128)(2,1)} %shard_map.307), channel_id=1, source_target_pairs={{0,2},{1,3},{2,0},{3,1},{4,6},{5,7},{6,4},{7,5},{8,10},{9,11},{10,... | collective-permute-start | bytes 1179656 | tf_op jit(solution)/shard_map/ppermute | solution.py:1061
  191.6 17.4 %collective-permute-start.47 = (bf16[96,768]{1,0:T(8,128)(2,1)S(1)}, bf16[96,768]{1,0:T(8,128)(2,1)}, u32[]{:S(2)}, u32[]{:S(2)}) collective-permute-start(bf16[96,768]{1,0:T(8,128)(2,1)S(1)} %slice.25), channel_id=1, source_target_pairs={{0,16},{16,0},{1,17},{17,1},{2,18},{18,2},{3,19},{19,3},{4,20},{20... | collective-permute-start | bytes 442376 | tf_op jit(solution)/shard_map/ppermute | solution.py:1043
  194.8 14.1 %collective-permute-start.39 = (bf16[112,512]{1,0:T(8,128)(2,1)}, bf16[112,512]{1,0:T(8,128)(2,1)}, u32[]{:S(2)}, u32[]{:S(2)}) collective-permute-start(bf16[112,512]{1,0:T(8,128)(2,1)} %shard_map.309), channel_id=1, source_target_pairs={{0,4},{4,8},{8,12},{12,0},{1,5},{5,9},{9,13},{13,1},{2,6},{6,10},{... | collective-permute-start | bytes 344072 | tf_op jit(solution)/shard_map/ppermute | solution.py:1055
  (69 other events, 648.9 us)
where the time goes:
time: 229 us; the launch traced here: 228 us
  Pallas kernels  79.3 us (35%)
  starting transfers between devices  74 us (32%)
  waiting for transfers between devices  49.4 us (22%)
  local copies, waits for them, and re-layouts  18.3 us (8%)
  other arithmetic  5.72 us (2%)
    pallas_call x12, Pallas kernels, call(): pl.pallas_call(kernel, grid=(grid,), in_specs=[spec(i) for i in ins], out...  70.5 us
    ppermute x6, starting transfers between devices, gather(): here.append(lax.ppermute(part, 'ctx', ring(n_ctx, k)))  17.7 us
    ppermute x3, waiting for transfers between devices, block(): lax.ppermute(edges[k - 1], ('ctx', 'tp'), [((i + 1) * n_tp + j, i * n_tp...  14.9 us
    ppermute x3, waiting for transfers between devices, block(): got = lax.ppermute(groups[r], 'ctx', ring(n_ctx, r))  14.9 us
    ppermute x8, starting transfers between devices, gather(): there.append(lax.ppermute(p, 'shard', ring(n_sh, 1)))  10.1 us
    unnamed x103, local copies, waits for them, and re-layouts  9.25 us
    pallas_call x5, Pallas kernels, pair_sum(): pl.pallas_call(kernel, in_specs=[vmem, vmem], out_specs=vmem, out_shape=j...  8.74 us
    ppermute x3, starting transfers between devices, block(): blocks.append(lax.ppermute(moved[r - 1], 'ctx', ring(n_ctx, r)))  8.35 us
  transfers between devices with their start and end apart: 51, of which 17 were waited for; matrix products, arithmetic and copies ran while one was open for 6% of the time, Pallas kernels for 17%

commit v1 on v0

--- a/solution.py
+++ b/solution.py
@@ -115,16 +115,25 @@
 
 
 def unrolled(kernel, ins, outs, count):
-    axes, wide = [], []
+    axes, wide, falls = [], [], []
     for item in (*ins, *outs):
-        axis = None
+        axis, falling = None, False
         if item[0] != "smem":
             moved = [d for d, (a, b) in enumerate(zip(item[1](0), item[1](1))) if a != b]
             axis = moved[0] if moved else None
         if axis is not None:
             block = tuple(n * count if d == axis else n for d, n in enumerate(item[0]))
-            item = (block,) + tuple(item[1:])
+            index = item[1]
+            top = index(0)[axis]
+            falling = index(1)[axis] < top
+            if falling:
+                top = (top + 1) // count - 1
+                index = lambda i, axis=axis, top=top, n=len(block): tuple(
+                    top - i if d == axis else 0 for d in range(n)
+                )
+            item = (block, index) + tuple(item[2:])
         axes.append(axis)
+        falls.append(falling)
         wide.append(item)
 
     def body(*refs):
@@ -136,8 +145,9 @@
                     views.append(ref)
                     continue
                 size = wide[k][0][axis] // count
+                j = count - 1 - inner if falls[k] else inner
                 at = tuple(
-                    slice(inner * size, (inner + 1) * size) if d == axis else slice(None)
+                    slice(j * size, (j + 1) * size) if d == axis else slice(None)
                     for d in range(len(wide[k][0]))
                 )
                 views.append(ref.at[at])
@@ -209,7 +219,7 @@
 
 
 def tri_leq():
-    return jnp.where(iota((L, L), 0) <= iota((L, L), 1), 1.0, 0.0)
+    return jnp.where(iota((L, L), 0) <= iota((L, L), 1), 1.0, 0.0).astype(bf16)
 
 
 def pair_mask(hw, which):
@@ -339,8 +349,8 @@
         dt = softplus(dot(slab, expand_matrix().astype(bf16)) + hp[0:1, :]) * mask_c
         dtr = softplus(dot(slab_select().astype(bf16), slab, NT) + hc[:, 0:1]) * mask8[0:1, :]
         tri = tri_leq()
-        cum = dot(tri, dt * hp[1:2, :], TN, HI)
-        cumr = dot(dtr * hc[:, 1:2], tri, NN, HI)
+        cum = dot3(tri, dt * hp[1:2, :], TN)
+        cumr = dot3(dtr * hc[:, 1:2], tri)
         dt_ref[...], cum_ref[...], dtr_ref[...], cumr_ref[...] = dt, cum, dtr, cumr
         prev, last = chunk_edges(meta, c)
         xd = dt * act[:, :IN]
@@ -450,9 +460,9 @@
         out = y + hp_ref[2:3, :] * act_ref[:, :IN]
         z = z_ref[...].astype(f32)
         gated = out * (z * sigmoid(z))
-        ones = jnp.ones((8, IN), f32)
-        sq = dot(ones, gated * gated, NT, HI)
-        bd = dot(ones, dm_ref[...] * gg_ref[0:1, :] * gated, NT, HI)
+        ones = jnp.ones((8, IN), bf16)
+        sq = dot3(ones, gated * gated, NT)
+        bd = dot3(ones, dm_ref[...] * gg_ref[0:1, :] * gated, NT)
         stat_ref[...] = jnp.where(iota((8, L), 0) == 0, sq, bd)
 
     def output(meta, act, cum, y, z, dm, hpre, pp, hp, gg, packs):
@@ -468,9 +478,9 @@
         stats = refs[8 : 8 + n_tp]
         mix_ref, dz_ref, dy_ref, suf_ref, psuf_ref, pack_ref, sums_ref = refs[8 + n_tp : 15 + n_tp]
         st_ref, ps_ref = refs[15 + n_tp :]
-        c = nC - 1 - pl.program_id(0)
-
-        @pl.when(pl.program_id(0) == 0)
+        c = nC - 1 - Step.chunk
+
+        @when_first
         def _():
             st_ref[...] = jnp.zeros((N, IN), f32)
             ps_ref[...] = jnp.ones((8, IN), f32)
@@ -484,8 +494,8 @@
         beta_r = inv_r * inv_r * inv_r * stat[1:2, :] / inner
         row = iota((8, L), 0)
         both = jnp.where(row == 0, inv_r, jnp.where(row == 1, beta_r, 0.0))
-        inv = dot(both, jnp.where(iota((8, IN), 0) == 0, 1.0, 0.0), TN, HI)
-        beta = dot(both, jnp.where(iota((8, IN), 0) == 1, 1.0, 0.0), TN, HI)
+        inv = dot3(both, jnp.where(iota((8, IN), 0) == 0, 1.0, 0.0).astype(bf16), TN)
+        beta = dot3(both, jnp.where(iota((8, IN), 0) == 1, 1.0, 0.0).astype(bf16), TN)
         gg, skip = gg_ref[0:1, :], hp_ref[2:3, :]
         x = act_ref[:, :IN]
         out = y_ref[...] + skip * x
@@ -517,7 +527,7 @@
         ps = passing * ps
         st_ref[...], ps_ref[...] = st, ps
 
-        @pl.when(c == 0)
+        @when_last
         def _():
             pack_ref[:N, :] = st.astype(bf16)
             pack_ref[N:, :] = jnp.concatenate([ps, ps], axis=0).astype(bf16)
@@ -534,7 +544,7 @@
                 o_whole((N + SP, IN), bf16), o_whole((8, IN), f32)]
         scratch = [pltpu.VMEM((N, IN), f32), pltpu.VMEM((8, IN), f32)]
         return call(k_norm, nC, ins, outs, scratch, 2 * T * IN * N,
-                    [meta, act, cum, y, z, dm, hp, gg, *stats])
+                    [meta, act, cum, y, z, dm, hp, gg, *stats], unroll=2)
 
     def k_intra_back(mref, act_ref, dt_ref, cum_ref, cumr_ref, dy_ref, dxd_ref, dbc_ref):
         meta = Meta(mref, sizes)
@@ -605,20 +615,20 @@
         @pl.when(c == 0)
         def _():
             load_weights(meta, shards, w_ref)
-            total[...] = jnp.zeros((D, 2 * IN), f32)
-
-        total[:, :IN] += dot(nb_ref[...], dz_ref[...], TN)
-        total[:, IN:] += dot(do_ref[...].astype(bf16), mix_ref[...], TN)
-        split_rows(meta, c, dot(mix_ref[...], w_ref[:, IN:], NT), keep_ref, send_ref)
+
+        mix = mix_ref[pl.ds(pl.multiple_of(c * L, L), L), :]
+        split_rows(meta, c, dot(mix, w_ref[:, IN:], NT), keep_ref, send_ref)
 
         @pl.when(c == nC - 1)
         def _():
+            total[:, :IN] = dot(nb_ref[...], dz_ref[...], TN)
+            total[:, IN:] = dot(do_ref[...].astype(bf16), mix_ref[...], TN)
             write_blocks(meta, total, outs)
 
     def outer(meta, nb, d_out, mix, dz, shards):
         outs = [o_whole((group_rows, 2 * IN), bf16)] * n_groups
         outs += [o_whole((T // 2, D), f32), o_whole((T // 2, D), bf16)]
-        ins = [SMEM, rows(nb), rows(d_out), rows(mix), rows(dz)] + [whole(s) for s in shards]
+        ins = [SMEM] + [whole(a) for a in (nb, d_out, mix, dz, *shards)]
         scratch = [pltpu.VMEM((D, 2 * IN), bf16), pltpu.VMEM((D, 2 * IN), f32)]
         got = call(k_outer, nC, ins, outs, scratch, 6 * T * D * IN,
                    [meta, nb, d_out, mix, dz, *shards])
@@ -659,20 +669,20 @@
         dxd = dxd_in + ws * leaving
         db = dbc_ref[:, :N] + dot3(wx, dhb, NT)
         dc = dbc_ref[:, N:] + dot3(ent * dyf, hinb, NT)
-        hs = head_select()
-        dcum = dot(hs, dyf * y_ref[...] - xd * dxd_in - wx.astype(f32) * leaving, NT, HI)
-        final = dot(hs, jnp.zeros((8, IN), f32) + jnp.sum(dhb.astype(f32) * hout, axis=0, keepdims=True), NT, HI)
-        da = dot(dcum, tri_leq(), NT, HI) + final[:, 0:1]
+        hs = head_select().astype(bf16)
+        dcum = dot3(hs, dyf * y_ref[...] - xd * dxd_in - wx.astype(f32) * leaving, NT)
+        final = dot3(hs, jnp.zeros((8, IN), f32) + jnp.sum(dhb.astype(f32) * hout, axis=0, keepdims=True), NT)
+        da = dot3(dcum, tri_leq(), NT) + final[:, 0:1]
         hc = hc_ref[...]
         dtr, mask8 = dtr_ref[...], mask_ref[...]
-        ddt = da * hc[:, 1:2] + dot(hs, dxd * x, NT, HI)
+        ddt = da * hc[:, 1:2] + dot3(hs, dxd * x, NT)
         slab = pr_ref[:, IN : IN + 128]
         pre_r = dot(slab_select().astype(bf16), slab, NT) + hc[:, 0:1]
         dpre = ddt * mask8[0:1, :] * sigmoid(pre_r)
         ddt_ref[...] = dot(dpre.astype(bf16), slab_select().astype(bf16), TN).astype(bf16)
-        ones = jnp.ones((L, 128), f32)
-        sums_ref[0:8, :] += dot(dpre, ones, NN, HI)
-        sums_ref[8:16, :] += dot(da * dtr, ones, NN, HI)
+        ones = jnp.ones((L, 128), bf16)
+        sums_ref[0:8, :] += dot3(dpre, ones)
+        sums_ref[8:16, :] += dot3(da * dtr, ones)
         sm = sm_ref[...]
         sig = sigmoid(sm)
         dsilu = sig * (1.0 + sm * (1.0 - sig))
@@ -734,22 +744,16 @@
         edges, at = refs[at : at + n_tp - 1], at + n_tp - 1
         shards, at = refs[at : at + NSH], at + NSH
         zshards, at = refs[at : at + NSH], at + NSH
-        halves, at = refs[at : at + n_tp // 2], at + n_tp // 2
         gs, at = refs[at : at + NSH], at + NSH
-        keep_ref, send_ref, half_ref = refs[at : at + 3]
-        at += 3
-        w_ref, wz_ref, ex_ref, px_ref, sl_ref, total, tap_ref = refs[at:]
+        keep_ref, send_ref = refs[at : at + 2]
+        at += 2
+        w_ref, wz_ref, ex_ref, px_ref, sl_ref, total, tap_ref, dp_ref = refs[at:]
         c = pl.program_id(0)
-        half = halves[0][...].astype(f32)
-        for h in halves[1:]:
-            half = half + h[...].astype(f32)
-        half_ref[...] = half.astype(bf16)
 
         @pl.when(c == 0)
         def _():
             load_weights(meta, shards, w_ref)
             load_weights(meta, zshards, wz_ref)
-            total[...] = jnp.zeros((D, PW), f32)
             tap_ref[...] = jnp.zeros((8, PW), f32)
             sl = slices[0][...].astype(f32)
             for s in slices[1:]:
@@ -794,13 +798,13 @@
         dproj = dpre.astype(bf16)
         dslab = (dpre[:, IN:] + ddt_ref[...].astype(f32)).astype(bf16)
         dproj = jnp.concatenate([dproj[:, :IN], dslab], axis=1)
-        nb = nb_ref[...]
-        total[...] += dot(nb, dproj, TN)
+        dp_ref[pl.ds(here, L), :] = dproj
         q = dot(dproj, w_ref[:, :PW], NT) + dot(dz_ref[...], wz_ref[:, :IN], NT)
         split_rows(meta, c, q, keep_ref, send_ref)
 
         @pl.when(c == nC - 1)
         def _():
+            total[...] = dot(nb_ref[...], dp_ref[...], TN)
             low8 = iota((8, PW), 1) < IN + SL
             s = ssum_ref[...]
             zero = jnp.zeros((8, 128), f32)
@@ -823,23 +827,22 @@
                     gs[i][br9:, :] = small
 
     def conv_back(meta, nb, pr, prh, dz, ddt, dsx, cw9, sums, ssum, edge, slices, edges, shards,
-                  zshards, halves):
+                  zshards):
         step = L // 16
         prior = ((16, PK), lambda i: (jnp.maximum(i * step - 1, 0), 0))
         after = ((8, IN), lambda i: (jnp.minimum((i + 1) * (L // 8), T // 8 - 1), 0))
-        ins = [SMEM, rows(nb), rows(pr), prior, whole(prh), rows(dz), rows(ddt), rows(dsx), after,
+        ins = [SMEM, whole(nb), rows(pr), prior, whole(prh), rows(dz), rows(ddt), rows(dsx), after,
                whole(cw9), whole(sums), whole(ssum), whole(edge)]
         ins += [whole(a) for a in (*slices, *edges, *shards, *zshards)]
-        ins += [rows(h, HB) for h in halves]
         outs = [o_whole((br9 + 16, PW), bf16)] * NSH
-        outs += [o_whole((T // 2, D), f32), o_whole((T // 2, D), bf16), o_rows((T // 2, D), bf16, HB)]
+        outs += [o_whole((T // 2, D), f32), o_whole((T // 2, D), bf16)]
         scratch = [pltpu.VMEM((D, PK), bf16), pltpu.VMEM((D, 2 * IN), bf16),
                    pltpu.VMEM((L + 8, PW), f32), pltpu.VMEM((L + 8, PW), f32),
                    pltpu.VMEM((T + 8, 128), f32), pltpu.VMEM((D, PW), f32),
-                   pltpu.VMEM((8, PW), f32)]
+                   pltpu.VMEM((8, PW), f32), pltpu.VMEM((T, PW), bf16)]
         got = call(k_conv_back, nC, ins, outs, scratch, 4 * T * D * (PW + IN),
                     [meta, nb, pr, pr, prh, dz, ddt, dsx, dsx, cw9, sums, ssum, edge, *slices, *edges,
-                     *shards, *zshards, *halves])
+                     *shards, *zshards])
         return got[:NSH], got[NSH:]
 
     def k_tables(mref, wx, bx, wbc, bbc, bias, alog, skip, gain, mask, cw, cw9, hp, hc, gg, mask8):
@@ -1028,13 +1031,14 @@
         meta, act, sm, pr, dt, cum, dtr, y, dy, dxd, dbc, hpre, pp, entry, suf, psuf, hp, hc, mask8,
         b_keep, b_got, bpacks)
     got_edge = lax.ppermute(edge, "ctx", [(i + 1, i) for i in range(n_ctx - 1)])
-    got_slices = [slices[0]] + [lax.ppermute(slices[k], "tp", xor(n_tp, k)) for k in range(1, n_tp)]
-    got_edges = [
-        lax.ppermute(edges[k - 1], ("ctx", "tp"),
-                     [((i + 1) * n_tp + j, i * n_tp + (j ^ k)) for i in range(n_ctx - 1) for j in range(n_tp)])
-        for k in range(1, n_tp)
-    ]
-    halves = [b_pair] + [lax.ppermute(b_pair, "tp", xor(n_tp, k)) for k in range(2, n_tp, 2)]
+    got_slices, got_edges = [slices[0]], []
+    for k in range(1, n_tp):
+        got_slices.append(lax.ppermute(slices[k], "tp", xor(n_tp, k)))
+        across = [((i + 1) * n_tp + j, i * n_tp + (j ^ k)) for i in range(n_ctx - 1) for j in range(n_tp)]
+        got_edges.append(lax.ppermute(edges[k - 1], ("ctx", "tp"), across))
+    b_half = b_pair.astype(f32)
+    for k in range(2, n_tp, 2):
+        b_half = b_half + lax.ppermute(b_pair, "tp", xor(n_tp, k)).astype(f32)
     if direct:
         total = groups[0].astype(f32)
         for r in range(1, n_ctx):
@@ -1042,9 +1046,9 @@
             total = total + got.astype(f32)
         other = lax.ppermute(total[br:].astype(bf16), "shard", ring(n_sh, 1))
         parts = [total[:br], other]
-    grads, (q_keep, q_send, b_half) = ops["conv_back"](
+    grads, (q_keep, q_send) = ops["conv_back"](
         meta, nb, pr, prh, dz, ddt, dsx, cw9, sums, ssum, got_edge, got_slices, got_edges, shards,
-        shards2, halves)
+        shards2)
     if direct:
         moved = []
         for r in [*range(1, n_ctx), 0]:
@@ -1059,21 +1063,26 @@
     q_half = q_pair.astype(f32)
     for k in range(2, n_tp, 2):
         q_half = q_half + lax.ppermute(q_pair, "tp", xor(n_tp, k)).astype(f32)
-    block_out = x_in + both_halves(b_half)
+    block_whole = both_halves(b_half)
+    block_out = x_in + block_whole
 
     x_half = lax.dynamic_slice_in_dim(x_in, (me_t % 2) * (T // 2), T // 2, 0)
     inv = lax.rsqrt(jnp.mean(x_half * x_half, axis=1, keepdims=True) + norm_eps)
     q_half = q_half * gain_row[0:1, :]
     row_dot = jnp.sum(q_half * x_half, axis=1, keepdims=True)
-    d_input = d_out + both_halves(q_half * inv - x_half * (inv * inv * inv) * row_dot / D)
+    q_whole = both_halves(q_half * inv - x_half * (inv * inv * inv) * row_dot / D)
+    d_input = d_out + q_whole
 
     if direct:
         g_z, g_out, g_x, g_slab, d_cx, d_bx, d_gg, d_dt_bias, d_a_log, d_skips, last = ops["finish"](
             meta, first, second, blocks, parts, a_log[None, :])
-        lasts = [last] + [lax.ppermute(last, "tp", xor(n_tp, k)) for k in range(1, n_tp)]
+        lasts = [last]
+        for k in range(1, n_tp):
+            lasts.append(lax.ppermute(last, "tp", xor(n_tp, k)))
+        d_w_dt = g_slab[:, SL : SL + H]
         d_w_bc, d_norm_gain, d_cbc, d_bbc = ops["spread"](meta, lasts)
         return (
-            block_out, d_input, d_norm_gain, g_z, g_x, d_w_bc, g_slab[:, SL : SL + H], g_out,
+            block_out, d_input, d_norm_gain, g_z, g_x, d_w_bc, d_w_dt, g_out,
             d_cx, d_bx, d_cbc, d_bbc, d_dt_bias, d_a_log, d_skips, d_gg,
         )
 

time: 229 us -> 222 us (0.969)
  starting transfers between devices: 74 us -> 67.3 us
  Pallas kernels: 79.3 us -> 73.2 us
  waiting for transfers between devices: 49.4 us -> 55.1 us
    ppermute x3, waiting for transfers between devices: 14.9 us -> 0.01 us  [block(): got = lax.ppermute(groups[r], 'ctx', ring(n_ctx, r))]
    ppermute x4, waiting for transfers between devices: 0.01 us -> 8.98 us  [block(): got = lax.ppermute(grads[n_ctx + r], 'shard', ring(n_sh, 1))]
    ppermute x10, waiting for transfers between devices: 15.9 us -> 24.5 us  [the longest x3 20.4 us: block(): got_edges.append(lax.ppermute(edges[k - 1], ('ctx', 'tp'), across))]
    pallas_call x12, Pallas kernels: 70.5 us -> 64.4 us  [call(): pl.pallas_call(kernel, grid=(grid,), in_specs=[spec(i) for i in ins], out...]
    ppermute x3, waiting for transfers between devices: 2.99 us -> 7.44 us  [block(): lax.ppermute(bpack, 'ctx', [(i + k, i) for i in range(n_ctx - k)])]
    ppermute x3, starting transfers between devices: 8.35 us -> 4.66 us  [block(): blocks.append(lax.ppermute(moved[r - 1], 'ctx', ring(n_ctx, r)))]
    unnamed x103 -> x109, local copies, waits for them, and re-layouts: 9.25 us -> 9.67 us
  transfers between devices with their start and end apart: 51 -> 51, of which waited for: 17 -> 20; matrix products, arithmetic and copies ran while one was open for 6% -> 6% of each run, Pallas kernels for 17% -> 26%
where the time goes in v1:
time: 222 us; the launch traced here: 220 us
  Pallas kernels  73.2 us (33%)
  starting transfers between devices  67.3 us (30%)
  waiting for transfers between devices  55.1 us (25%)
  local copies, waits for them, and re-layouts  18.7 us (8%)
  other arithmetic  4.91 us (2%)
    pallas_call x12, Pallas kernels, call(): pl.pallas_call(kernel, grid=(grid,), in_specs=[spec(i) for i in ins], out...  64.4 us
    ppermute x3, waiting for transfers between devices, block(): got_edges.append(lax.ppermute(edges[k - 1], ('ctx', 'tp'), across))  20.4 us
    ppermute x6, starting transfers between devices, gather(): here.append(lax.ppermute(part, 'ctx', ring(n_ctx, k)))  17.7 us
    ppermute x8, starting transfers between devices, gather(): there.append(lax.ppermute(p, 'shard', ring(n_sh, 1)))  10.1 us
    unnamed x109, local copies, waits for them, and re-layouts  9.67 us
    ppermute x4, waiting for transfers between devices, block(): got = lax.ppermute(grads[n_ctx + r], 'shard', ring(n_sh, 1))  8.98 us
    pallas_call x5, Pallas kernels, pair_sum(): pl.pallas_call(kernel, in_specs=[vmem, vmem], out_specs=vmem, out_shape=j...  8.74 us
    ppermute x3, waiting for transfers between devices, block(): lax.ppermute(bpack, 'ctx', [(i + k, i) for i in range(n_ctx - k)])  7.44 us
  transfers between devices with their start and end apart: 51, of which 20 were waited for; matrix products, arithmetic and copies ran while one was open for 6% of the time, Pallas kernels for 26%

profile of v1, /device:TPU:0, one launch (start us, length us, event | category | flops | bytes accessed | tf_op | source)
XLA Modules:
  0.0 220.5 jit_solution(527428772525491709)
XLA Ops:
  2.4 5.1 %collective-permute-start.10 = (bf16[96,768]{1,0:T(8,128)(2,1)S(1)}, bf16[96,768]{1,0:T(8,128)(2,1)S(1)}, u32[]{:S(2)}, u32[]{:S(2)}) collective-permute-start(bf16[96,768]{1,0:T(8,128)(2,1)S(1)} %constant_dynamic-update-slice_fusion.refs_3_.refs_5_.refs_28_.refs_2_), channel_id=1, source_target_pairs={{0,12},{4,0},{8,4},{12,8},{1,13},{5,1},{9,5},{13,9},{2,14},{6,2},{... | collective-permute-start | bytes 442376 | tf_op jit(solution)/shard_map/ppermute | solution.py:987
  11.5 2.6 %collective-permute-start.2 = (bf16[96,768]{1,0:T(8,128)(2,1)S(1)}, bf16[96,768]{1,0:T(8,128)(2,1)S(1)}, u32[]{:S(2)}, u32[]{:S(2)}) collective-permute-start(bf16[96,768]{1,0:T(8,128)(2,1)S(1)} %concatenate.16.refs_7_.refs_20_.refs_1_), channel_id=1, source_target_pairs={{0,8},{4,12},{8,0},{12,4},{1,9},{5,13},{9,1},{13,5},{2,10},{6,14},... | collective-permute-start | bytes 442376 | tf_op jit(solution)/shard_map/ppermute | solution.py:987
  14.8 3.8 %collective-permute-start = (f32[8,768]{1,0:T(8,128)S(1)}, f32[8,768]{1,0:T(8,128)S(1)}, u32[]{:S(2)}, u32[]{:S(2)}) collective-permute-start(f32[8,768]{1,0:T(8,128)S(1)} %slice.16), channel_id=1, source_target_pairs={{0,4},{4,8},{8,12},{1,5},{5,9},{9,13},{2,6},{6,10},{10,14},{3,7},{... | collective-permute-start | bytes 73736 | tf_op jit(solution)/shard_map/ppermute | solution.py:999
  18.6 2.1 collective-permute-done.refs_2_
  20.7 7.0 %collective-permute-start.1 = (bf16[96,768]{1,0:T(8,128)(2,1)S(1)}, bf16[96,768]{1,0:T(8,128)(2,1)S(1)}, u32[]{:S(2)}, u32[]{:S(2)}) collective-permute-start(bf16[96,768]{1,0:T(8,128)(2,1)S(1)} %concatenate.16.refs_7_.refs_20_.refs_1_), channel_id=1, source_target_pairs={{0,4},{4,8},{8,12},{12,0},{1,5},{5,9},{9,13},{13,1},{2,6},{6,10},{... | collective-permute-start | bytes 442376 | tf_op jit(solution)/shard_map/ppermute | solution.py:987
  27.8 2.5 %collective-permute-start.8 = (bf16[96,768]{1,0:T(8,128)(2,1)S(1)}, bf16[96,768]{1,0:T(8,128)(2,1)S(1)}, u32[]{:S(2)}, u32[]{:S(2)}) collective-permute-start(bf16[96,768]{1,0:T(8,128)(2,1)S(1)} %constant_dynamic-update-slice_fusion.refs_3_.refs_5_.refs_28_.refs_2_), channel_id=1, source_target_pairs={{0,4},{4,8},{8,12},{12,0},{1,5},{5,9},{9,13},{13,1},{2,6},{6,10},{... | collective-permute-start | bytes 442376 | tf_op jit(solution)/shard_map/ppermute | solution.py:987
  48.6 1.8 shard_map.297
  51.1 8.9 %shard_map.298 = (bf16[512,768]{1,0:T(8,128)(2,1)}, bf16[512,768]{1,0:T(8,128)(2,1)}, f32[8,768]{1,0:T(8,128)}, f32[512,640]{1,0:T(8,128)}, f32[512,640]{1,0:T(8...) custom-call(s32[6]{0:T(128)} %pad_add_fusion.refs_0_, ...), custom_call_target="tpu_custom_call" | custom-call | flops 603979776 | bytes 9834520 | tf_op jit(solution)/shard_map/pallas_call | solution.py:182
  60.0 3.2 %collective-permute-start.17 = (bf16[144,384]{1,0:T(8,128)(2,1)}, bf16[144,384]{1,0:T(8,128)(2,1)S(1)}, u32[]{:S(2)}, u32[]{:S(2)}) collective-permute-start(bf16[144,384]{1,0:T(8,128)(2,1)} %get-tuple-element.109), channel_id=1, source_target_pairs={{0,12},{1,13},{2,14},{3,15},{16,28},{17,29},{18,30},{19,31}} | collective-permute-start | bytes 331784 | tf_op jit(solution)/shard_map/ppermute | solution.py:1010
  64.6 2.5 %collective-permute-start.15 = (bf16[144,384]{1,0:T(8,128)(2,1)}, bf16[144,384]{1,0:T(8,128)(2,1)S(1)}, u32[]{:S(2)}, u32[]{:S(2)}) collective-permute-start(bf16[144,384]{1,0:T(8,128)(2,1)} %get-tuple-element.109), channel_id=1, source_target_pairs={{0,4},{4,8},{8,12},{1,5},{5,9},{9,13},{2,6},{6,10},{10,14},{3,7},{... | collective-permute-start | bytes 331784 | tf_op jit(solution)/shard_map/ppermute | solution.py:1010
  67.1 4.0 %shard_map.299.refs_3_ = f32[512,384]{1,0:T(8,128)} custom-call(s32[6]{0:T(128)} %pad_add_fusion.refs_0_, f32[512,640]{1,0:T(8,128)} %get-tuple-element.96.refs_1_, f32[512,384]{1,0:T(8,128)} %get-tuple-element.99.refs_2_.refs_4_, f32[512,384]{1,0:T(8,128)} %get-tuple-element.100.refs_3_.refs_2_.refs_5_, f32[8,512]{1,0:T(8,128)} %get-tuple-element.102.refs_4_), custom_call_target="tpu_custom_call" | custom-call | flops 100663296 | bytes 3686424 | tf_op jit(solution)/shard_map/pallas_call | solution.py:182
  71.8 3.6 %shard_map.300 = (bf16[512,384]{1,0:T(8,128)(2,1)}, f32[512,384]{1,0:T(8,128)}) custom-call(s32[6]{0:T(128)} %pad_add_fusion.refs_0_, bf16[512,768]{1,0:T(8,128)(2,1)} %get-tuple-element.103.refs_1_, f32[512,768]{1,0:T(8,128)} %refs_2_.3, bf16[96,768]{1,0:T(8,128)(2,1)} %copy-done.3, bf16[96,768]{1,0:T(8,128)(2,1)} %copy-done.7, bf16[96,768]{1,0:T(8,128)(2,1)} %copy-done.6, ...), custom_call_target="tpu_custom_call" | custom-call | flops 603979776 | bytes 4718616 | tf_op jit(solution)/shard_map/pallas_call | solution.py:182
  76.2 4.4 %shard_map.301 = (f32[512,384]{1,0:T(8,128)}, f32[8,512]{1,0:T(8,128)}, f32[128,384]{1,0:T(8,128)}) custom-call(s32[6]{0:T(128)} %pad_add_fusion.refs_0_, f32[512,640]{1,0:T(8,128)} %get-tuple-element.96.refs_1_, f32[512,384]{1,0:T(8,128)} %get-tuple-element.100.refs_3_.refs_2_.refs_5_, f32[512,384]{1,0:T(8,128)} %shard_map.299.refs_3_, ...), custom_call_target="tpu_custom_call" | custom-call | flops 100663296 | bytes 6463512 | tf_op jit(solution)/shard_map/pallas_call | solution.py:182
  85.3 5.1 %shard_map.302 = (bf16[512,384]{1,0:T(8,128)(2,1)}, bf16[512,384]{1,0:T(8,128)(2,1)}, f32[512,384]{1,0:T(8,128)}, f32[512,384]{1,0:T(8,128)}, f32[32,384]{1,0:T(...) custom-call(s32[6]{0:T(128)} %pad_add_fusion.refs_0_, f32[512,640]{1,0:T(8,128)} %get-tuple-element.96.refs_1_, ...), custom_call_target="tpu_custom_call" | custom-call | flops 50331648 | bytes 6684696 | tf_op jit(solution)/shard_map/pallas_call | solution.py:182
  90.4 6.4 %shard_map.304 = (bf16[192,768]{1,0:T(8,128)(2,1)}, bf16[192,768]{1,0:T(8,128)(2,1)}, bf16[192,768]{1,0:T(8,128)(2,1)}, bf16[192,768]{1,0:T(8,128)(2,1)}, f32[256,768]{1,0:T(8,128)}, /*index=5*/bf16[256,768]{1,0:T(8,128)(2,1)}) custom-call(s32[6]{0:T(128)} %pad_add_fusion.refs_0_, bf16[512,768]{1,0:T(8,128)(2,1)} %get-tuple-element.103.refs_1_, ...), custom_call_target="tpu_custom_call" | custom-call | flops 905969664 | bytes 6684696 | tf_op jit(solution)/shard_map/pallas_call | solution.py:182
  101.1 2.7 %collective-permute-start.44 = (bf16[192,768]{1,0:T(8,128)(2,1)}, bf16[192,768]{1,0:T(8,128)(2,1)S(1)}, u32[]{:S(2)}, u32[]{:S(2)}) collective-permute-start(bf16[192,768]{1,0:T(8,128)(2,1)} %get-tuple-element.150), channel_id=1, source_target_pairs={{0,4},{4,8},{8,12},{12,0},{1,5},{5,9},{9,13},{13,1},{2,6},{6,10},{... | collective-permute-start | bytes 884744 | tf_op jit(solution)/shard_map/ppermute | solution.py:1045
  103.8 3.1 %collective-permute-done.24.refs_25_ = bf16[144,384]{1,0:T(8,128)(2,1)S(1)} collective-permute-done((bf16[144,384]{1,0:T(8,128)(2,1)S(1)}, bf16[144,384]{1,0:T(8,128)(2,1)S(1)}, u32[]{:S(2)}, u32[]{:S(2)}) %collective-permute-start.24) | collective-permute-done | bytes 110624 | tf_op jit(solution)/shard_map/ppermute | solution.py:1018
  107.4 4.3 %collective-permute-done.23.refs_24_ = bf16[144,384]{1,0:T(8,128)(2,1)S(1)} collective-permute-done((bf16[144,384]{1,0:T(8,128)(2,1)S(1)}, bf16[144,384]{1,0:T(8,128)(2,1)S(1)}, u32[]{:S(2)}, u32[]{:S(2)}) %collective-permute-start.23) | collective-permute-done | bytes 110624 | tf_op jit(solution)/shard_map/ppermute | solution.py:1018
  111.7 6.5 %shard_map.303 = (f32[512,384]{1,0:T(8,128)}, f32[512,256]{1,0:T(8,128)}) custom-call(s32[6]{0:T(128)} %pad_add_fusion.refs_0_, f32[512,640]{1,0:T(8,128)} %get-tuple-element.96.refs_1_, f32[512,384]{1,0:T(8,128)} %get-tuple-element.99.refs_2_.refs_4_, f32[512,384]{1,0:T(8,128)} %get-tuple-element.100.refs_3_.refs_2_.refs_5_, ...), custom_call_target="tpu_custom_call" | custom-call | flops 201326592 | bytes 4997144 | tf_op jit(solution)/shard_map/pallas_call | solution.py:182
  119.0 10.4 %shard_map.305 = (f32[512,384]{1,0:T(8,128)}, bf16[512,128]{1,0:T(8,128)(2,1)}, f32[16,128]{1,0:T(8,128)}, f32[8,512]{1,0:T(8,128)}, bf16[256,768]{1,0:T(8,128)(...) custom-call(s32[6]{0:T(128)} %pad_add_fusion.refs_0_, ...), custom_call_target="tpu_custom_call" | custom-call | flops 150994944 | bytes 14155800 | tf_op jit(solution)/shard_map/pallas_call | solution.py:182
  130.8 10.3 %collective-permute-done.31.refs_17_ = f32[8,128]{1,0:T(8,128)S(1)} collective-permute-done((f32[8,128]{1,0:T(8,128)}, f32[8,128]{1,0:T(8,128)S(1)}, u32[]{:S(2)}, u32[]{:S(2)}) %collective-permute-start.31) | collective-permute-done | bytes 4128 | tf_op jit(solution)/shard_map/ppermute | solution.py:1038
  142.4 5.3 %collective-permute-done.32.refs_18_ = f32[8,128]{1,0:T(8,128)S(1)} collective-permute-done((f32[8,128]{1,0:T(8,128)}, f32[8,128]{1,0:T(8,128)S(1)}, u32[]{:S(2)}, u32[]{:S(2)}) %collective-permute-start.32) | collective-permute-done | bytes 4128 | tf_op jit(solution)/shard_map/ppermute | solution.py:1038
  149.0 4.7 %collective-permute-done.33.refs_19_ = f32[8,128]{1,0:T(8,128)S(1)} collective-permute-done((f32[8,128]{1,0:T(8,128)}, f32[8,128]{1,0:T(8,128)S(1)}, u32[]{:S(2)}, u32[]{:S(2)}) %collective-permute-start.33) | collective-permute-done | bytes 4128 | tf_op jit(solution)/shard_map/ppermute | solution.py:1038
  155.1 4.5 %collective-permute-done.27.refs_12_ = f32[8,512]{1,0:T(8,128)S(1)} collective-permute-done((f32[8,512]{1,0:T(8,128)}, f32[8,512]{1,0:T(8,128)S(1)}, u32[]{:S(2)}, u32[]{:S(2)}) %collective-permute-start.27) | collective-permute-done | bytes 16416 | tf_op jit(solution)/shard_map/ppermute | solution.py:1033
  161.1 3.0 %collective-permute-done.29.refs_15_ = bf16[256,128]{1,0:T(8,128)(2,1)S(1)} collective-permute-done((bf16[256,128]{1,0:T(8,128)(2,1)}, bf16[256,128]{1,0:T(8,128)(2,1)S(1)}, u32[]{:S(2)}, u32[]{:S(2)}) %collective-permute-start.29) | collective-permute-done | bytes 65568 | tf_op jit(solution)/shard_map/ppermute | solution.py:1036
  164.1 2.2 collective-permute-start.25
  166.9 9.3 %shard_map.306 = (bf16[112,512]{1,0:T(8,128)(2,1)}, bf16[112,512]{1,0:T(8,128)(2,1)}, bf16[112,512]{1,0:T(8,128)(2,1)}, bf16[112,512]{1,0:T(8,128)(2,1)}, bf16[1...) custom-call(s32[6]{0:T(128)} %pad_add_fusion.refs_0_, ...), custom_call_target="tpu_custom_call" | custom-call | flops 1409286144 | bytes 9265176 | tf_op jit(solution)/shard_map/pallas_call | solution.py:182
  179.0 3.4 %collective-permute-done.38.b = bf16[112,512]{1,0:T(8,128)(2,1)S(1)} collective-permute-done((bf16[112,512]{1,0:T(8,128)(2,1)}, bf16[112,512]{1,0:T(8,128)(2,1)S(1)}, u32[]{:S(2)}, u32[]{:S(2)}) %collective-permute-start.38) | collective-permute-done | bytes 114720 | tf_op jit(solution)/shard_map/ppermute | solution.py:1055
  182.4 5.6 %collective-permute-done.40.b = bf16[112,512]{1,0:T(8,128)(2,1)S(1)} collective-permute-done((bf16[112,512]{1,0:T(8,128)(2,1)S(1)}, bf16[112,512]{1,0:T(8,128)(2,1)S(1)}, u32[]{:S(2)}, u32[]{:S(2)}) %collective-permute-start.40) | collective-permute-done | bytes 114720 | tf_op jit(solution)/shard_map/ppermute | solution.py:1055
  195.1 2.5 %collective-permute-start.43 = (bf16[112,512]{1,0:T(8,128)(2,1)}, bf16[112,512]{1,0:T(8,128)(2,1)}, u32[]{:S(2)}, u32[]{:S(2)}) collective-permute-start(bf16[112,512]{1,0:T(8,128)(2,1)} %shard_map.311), channel_id=1, source_target_pairs={{0,12},{4,0},{8,4},{12,8},{1,13},{5,1},{9,5},{13,9},{2,14},{6,2},{... | collective-permute-start | bytes 344072 | tf_op jit(solution)/shard_map/ppermute | solution.py:1059
  197.6 2.0 shard_map.307
  203.8 2.4 %shard_map.312 = (f32[96,384]{1,0:T(8,128)}, f32[96,384]{1,0:T(8,128)}, f32[96,384]{1,0:T(8,128)}, f32[96,128]{1,0:T(8,128)}, f32[4,384]{1,0:T(4,128)}, /*index=...) custom-call(s32[6]{0:T(128)} %pad_add_fusion.refs_0_, ...), custom_call_target="tpu_custom_call" | custom-call | bytes 1750136 | tf_op jit(solution)/shard_map/pallas_call | solution.py:182
  (218 shorter events, 73.8 us)
Async XLA Ops:
  2.4 25.3 %collective-permute-start.10 = (bf16[96,768]{1,0:T(8,128)(2,1)S(1)}, bf16[96,768]{1,0:T(8,128)(2,1)S(1)}, u32[]{:S(2)}, u32[]{:S(2)}) collective-permute-start(bf16[96,768]{1,0:T(8,128)(2,1)S(1)} %constant_dynamic-update-slice_fusion.refs_3_.refs_5_.refs_28_.refs_2_), channel_id=1, source_target_pairs={{0,12},{4,0},{8,4},{12,8},{1,13},{5,1},{9,5},{13,9},{2,14},{6,2},{... | collective-permute-start | bytes 442376 | tf_op jit(solution)/shard_map/ppermute | solution.py:987
  7.6 22.7 %collective-permute-start.9 = (bf16[96,768]{1,0:T(8,128)(2,1)S(1)}, bf16[96,768]{1,0:T(8,128)(2,1)S(1)}, u32[]{:S(2)}, u32[]{:S(2)}) collective-permute-start(bf16[96,768]{1,0:T(8,128)(2,1)S(1)} %constant_dynamic-update-slice_fusion.refs_3_.refs_5_.refs_28_.refs_2_), channel_id=1, source_target_pairs={{0,8},{4,12},{8,0},{12,4},{1,9},{5,13},{9,1},{13,5},{2,10},{6,14},... | collective-permute-start | bytes 442376 | tf_op jit(solution)/shard_map/ppermute | solution.py:987
  11.0 20.8 %collective-permute-start.3 = (bf16[96,768]{1,0:T(8,128)(2,1)S(1)}, bf16[96,768]{1,0:T(8,128)(2,1)S(1)}, u32[]{:S(2)}, u32[]{:S(2)}) collective-permute-start(bf16[96,768]{1,0:T(8,128)(2,1)S(1)} %concatenate.16.refs_7_.refs_20_.refs_1_), channel_id=1, source_target_pairs={{0,12},{4,0},{8,4},{12,8},{1,13},{5,1},{9,5},{13,9},{2,14},{6,2},{... | collective-permute-start | bytes 442376 | tf_op jit(solution)/shard_map/ppermute | solution.py:987
  11.5 20.8 %collective-permute-start.2 = (bf16[96,768]{1,0:T(8,128)(2,1)S(1)}, bf16[96,768]{1,0:T(8,128)(2,1)S(1)}, u32[]{:S(2)}, u32[]{:S(2)}) collective-permute-start(bf16[96,768]{1,0:T(8,128)(2,1)S(1)} %concatenate.16.refs_7_.refs_20_.refs_1_), channel_id=1, source_target_pairs={{0,8},{4,12},{8,0},{12,4},{1,9},{5,13},{9,1},{13,5},{2,10},{6,14},... | collective-permute-start | bytes 442376 | tf_op jit(solution)/shard_map/ppermute | solution.py:987
  20.7 13.1 %collective-permute-start.1 = (bf16[96,768]{1,0:T(8,128)(2,1)S(1)}, bf16[96,768]{1,0:T(8,128)(2,1)S(1)}, u32[]{:S(2)}, u32[]{:S(2)}) collective-permute-start(bf16[96,768]{1,0:T(8,128)(2,1)S(1)} %concatenate.16.refs_7_.refs_20_.refs_1_), channel_id=1, source_target_pairs={{0,4},{4,8},{8,12},{12,0},{1,5},{5,9},{9,13},{13,1},{2,6},{6,10},{... | collective-permute-start | bytes 442376 | tf_op jit(solution)/shard_map/ppermute | solution.py:987
  32.3 11.0 %collective-permute-start.6 = (bf16[96,768]{1,0:T(8,128)(2,1)S(1)}, bf16[96,768]{1,0:T(8,128)(2,1)S(1)}, u32[]{:S(2)}, u32[]{:S(2)}) collective-permute-start(bf16[96,768]{1,0:T(8,128)(2,1)S(1)} %collective-permute-done.2.refs_9_.refs_22_), channel_id=1, source_target_pairs={{0,16},{16,0},{1,17},{17,1},{2,18},{18,2},{3,19},{19,3},{4,20},{20... | collective-permute-start | bytes 442376 | tf_op jit(solution)/shard_map/ppermute | solution.py:990
  33.8 16.6 %collective-permute-start.5 = (bf16[96,768]{1,0:T(8,128)(2,1)S(1)}, bf16[96,768]{1,0:T(8,128)(2,1)S(1)}, u32[]{:S(2)}, u32[]{:S(2)}) collective-permute-start(bf16[96,768]{1,0:T(8,128)(2,1)S(1)} %collective-permute-done.1.refs_8_.refs_21_), channel_id=1, source_target_pairs={{0,16},{16,0},{1,17},{17,1},{2,18},{18,2},{3,19},{19,3},{4,20},{20... | collective-permute-start | bytes 442376 | tf_op jit(solution)/shard_map/ppermute | solution.py:990
  34.7 28.6 %collective-permute-start.11 = (bf16[96,768]{1,0:T(8,128)(2,1)S(1)}, bf16[96,768]{1,0:T(8,128)(2,1)S(1)}, u32[]{:S(2)}, u32[]{:S(2)}) collective-permute-start(bf16[96,768]{1,0:T(8,128)(2,1)S(1)} %constant_dynamic-update-slice_fusion.refs_3_.refs_5_.refs_28_.refs_2_), channel_id=1, source_target_pairs={{0,16},{16,0},{1,17},{17,1},{2,18},{18,2},{3,19},{19,3},{4,20},{20... | collective-permute-start | bytes 442376 | tf_op jit(solution)/shard_map/ppermute | solution.py:990
  37.0 27.6 %collective-permute-start.14 = (bf16[96,768]{1,0:T(8,128)(2,1)S(1)}, bf16[96,768]{1,0:T(8,128)(2,1)S(1)}, u32[]{:S(2)}, u32[]{:S(2)}) collective-permute-start(bf16[96,768]{1,0:T(8,128)(2,1)S(1)} %collective-permute-done.10.refs_6_.refs_8_.refs_31_), channel_id=1, source_target_pairs={{0,16},{16,0},{1,17},{17,1},{2,18},{18,2},{3,19},{19,3},{4,20},{20... | collective-permute-start | bytes 442376 | tf_op jit(solution)/shard_map/ppermute | solution.py:990
  40.1 31.0 %collective-permute-start.13 = (bf16[96,768]{1,0:T(8,128)(2,1)S(1)}, bf16[96,768]{1,0:T(8,128)(2,1)S(1)}, u32[]{:S(2)}, u32[]{:S(2)}) collective-permute-start(bf16[96,768]{1,0:T(8,128)(2,1)S(1)} %collective-permute-done.9.refs_5_.refs_7_.refs_30_), channel_id=1, source_target_pairs={{0,16},{16,0},{1,17},{17,1},{2,18},{18,2},{3,19},{19,3},{4,20},{20... | collective-permute-start | bytes 442376 | tf_op jit(solution)/shard_map/ppermute | solution.py:990
  43.3 27.8 %collective-permute-start.12 = (bf16[96,768]{1,0:T(8,128)(2,1)S(1)}, bf16[96,768]{1,0:T(8,128)(2,1)S(1)}, u32[]{:S(2)}, u32[]{:S(2)}) collective-permute-start(bf16[96,768]{1,0:T(8,128)(2,1)S(1)} %collective-permute-done.8.refs_4_.refs_6_.refs_29_), channel_id=1, source_target_pairs={{0,16},{16,0},{1,17},{17,1},{2,18},{18,2},{3,19},{19,3},{4,20},{20... | collective-permute-start | bytes 442376 | tf_op jit(solution)/shard_map/ppermute | solution.py:990
  60.0 15.5 %collective-permute-start.17 = (bf16[144,384]{1,0:T(8,128)(2,1)}, bf16[144,384]{1,0:T(8,128)(2,1)S(1)}, u32[]{:S(2)}, u32[]{:S(2)}) collective-permute-start(bf16[144,384]{1,0:T(8,128)(2,1)} %get-tuple-element.109), channel_id=1, source_target_pairs={{0,12},{1,13},{2,14},{3,15},{16,28},{17,29},{18,30},{19,31}} | collective-permute-start | bytes 331784 | tf_op jit(solution)/shard_map/ppermute | solution.py:1010
  63.3 12.2 %collective-permute-start.16 = (bf16[144,384]{1,0:T(8,128)(2,1)}, bf16[144,384]{1,0:T(8,128)(2,1)S(1)}, u32[]{:S(2)}, u32[]{:S(2)}) collective-permute-start(bf16[144,384]{1,0:T(8,128)(2,1)} %get-tuple-element.109), channel_id=1, source_target_pairs={{0,8},{4,12},{1,9},{5,13},{2,10},{6,14},{3,11},{7,15},{16,24},{20,... | collective-permute-start | bytes 331784 | tf_op jit(solution)/shard_map/ppermute | solution.py:1010
  64.6 10.9 %collective-permute-start.15 = (bf16[144,384]{1,0:T(8,128)(2,1)}, bf16[144,384]{1,0:T(8,128)(2,1)S(1)}, u32[]{:S(2)}, u32[]{:S(2)}) collective-permute-start(bf16[144,384]{1,0:T(8,128)(2,1)} %get-tuple-element.109), channel_id=1, source_target_pairs={{0,4},{4,8},{8,12},{1,5},{5,9},{9,13},{2,6},{6,10},{10,14},{3,7},{... | collective-permute-start | bytes 331784 | tf_op jit(solution)/shard_map/ppermute | solution.py:1010
  96.8 21.4 %collective-permute-start.21 = (bf16[256,768]{1,0:T(8,128)(2,1)}, bf16[256,768]{1,0:T(8,128)(2,1)S(1)}, u32[]{:S(2)}, u32[]{:S(2)}) collective-permute-start(bf16[256,768]{1,0:T(8,128)(2,1)} %get-tuple-element.121), channel_id=1, source_target_pairs={{0,1},{1,0},{2,3},{3,2},{4,5},{5,4},{6,7},{7,6},{8,9},{9,8},{10,11... | collective-permute-start | bytes 1179656 | tf_op jit(solution)/shard_map/ppermute | solution.py:1029
  97.2 9.7 %collective-permute-start.24 = (bf16[144,384]{1,0:T(8,128)(2,1)S(1)}, bf16[144,384]{1,0:T(8,128)(2,1)S(1)}, u32[]{:S(2)}, u32[]{:S(2)}) collective-permute-start(bf16[144,384]{1,0:T(8,128)(2,1)S(1)} %copy-done.52), channel_id=1, source_target_pairs={{12,0},{13,1},{14,2},{15,3},{28,16},{29,17},{30,18},{31,19}} | collective-permute-start | bytes 331784 | tf_op jit(solution)/shard_map/ppermute | solution.py:1018
  98.5 13.2 %collective-permute-start.23 = (bf16[144,384]{1,0:T(8,128)(2,1)S(1)}, bf16[144,384]{1,0:T(8,128)(2,1)S(1)}, u32[]{:S(2)}, u32[]{:S(2)}) collective-permute-start(bf16[144,384]{1,0:T(8,128)(2,1)S(1)} %copy-done.52), channel_id=1, source_target_pairs={{8,0},{12,4},{9,1},{13,5},{10,2},{14,6},{11,3},{15,7},{24,16},{28,... | collective-permute-start | bytes 331784 | tf_op jit(solution)/shard_map/ppermute | solution.py:1018
  99.8 18.4 %collective-permute-start.22 = (bf16[144,384]{1,0:T(8,128)(2,1)S(1)}, bf16[144,384]{1,0:T(8,128)(2,1)S(1)}, u32[]{:S(2)}, u32[]{:S(2)}) collective-permute-start(bf16[144,384]{1,0:T(8,128)(2,1)S(1)} %copy-done.52), channel_id=1, source_target_pairs={{4,0},{8,4},{12,8},{5,1},{9,5},{13,9},{6,2},{10,6},{14,10},{7,3},{... | collective-permute-start | bytes 331784 | tf_op jit(solution)/shard_map/ppermute | solution.py:1018
  101.1 75.6 %collective-permute-start.44 = (bf16[192,768]{1,0:T(8,128)(2,1)}, bf16[192,768]{1,0:T(8,128)(2,1)S(1)}, u32[]{:S(2)}, u32[]{:S(2)}) collective-permute-start(bf16[192,768]{1,0:T(8,128)(2,1)} %get-tuple-element.150), channel_id=1, source_target_pairs={{0,4},{4,8},{8,12},{12,0},{1,5},{5,9},{9,13},{13,1},{2,6},{6,10},{... | collective-permute-start | bytes 884744 | tf_op jit(solution)/shard_map/ppermute | solution.py:1045
  106.9 69.8 %collective-permute-start.45 = (bf16[192,768]{1,0:T(8,128)(2,1)}, bf16[192,768]{1,0:T(8,128)(2,1)S(1)}, u32[]{:S(2)}, u32[]{:S(2)}) collective-permute-start(bf16[192,768]{1,0:T(8,128)(2,1)} %get-tuple-element.151), channel_id=1, source_target_pairs={{0,8},{4,12},{8,0},{12,4},{1,9},{5,13},{9,1},{13,5},{2,10},{6,14},... | collective-permute-start | bytes 884744 | tf_op jit(solution)/shard_map/ppermute | solution.py:1045
  111.7 65.1 %collective-permute-start.46 = (bf16[192,768]{1,0:T(8,128)(2,1)}, bf16[192,768]{1,0:T(8,128)(2,1)S(1)}, u32[]{:S(2)}, u32[]{:S(2)}) collective-permute-start(bf16[192,768]{1,0:T(8,128)(2,1)} %get-tuple-element.152), channel_id=1, source_target_pairs={{0,12},{4,0},{8,4},{12,8},{1,13},{5,1},{9,5},{13,9},{2,14},{6,2},{... | collective-permute-start | bytes 884744 | tf_op jit(solution)/shard_map/ppermute | solution.py:1045
  129.4 31.7 %collective-permute-start.28 = (bf16[256,128]{1,0:T(8,128)(2,1)}, bf16[256,128]{1,0:T(8,128)(2,1)S(1)}, u32[]{:S(2)}, u32[]{:S(2)}) collective-permute-start(bf16[256,128]{1,0:T(8,128)(2,1)} %get-tuple-element.132), channel_id=1, source_target_pairs={{0,1},{1,0},{2,3},{3,2},{4,5},{5,4},{6,7},{7,6},{8,9},{9,8},{10,11... | collective-permute-start | bytes 196616 | tf_op jit(solution)/shard_map/ppermute | solution.py:1036
  129.5 11.6 %collective-permute-start.31 = (f32[8,128]{1,0:T(8,128)}, f32[8,128]{1,0:T(8,128)S(1)}, u32[]{:S(2)}, u32[]{:S(2)}) collective-permute-start(f32[8,128]{1,0:T(8,128)} %get-tuple-element.135), channel_id=1, source_target_pairs={{4,1},{5,0},{6,3},{7,2},{8,5},{9,4},{10,7},{11,6},{12,9},{13,8},{1... | collective-permute-start | bytes 12296 | tf_op jit(solution)/shard_map/ppermute | solution.py:1038
  164.1 50.3 %collective-permute-start.25 = (bf16[256,768]{1,0:T(8,128)(2,1)}, bf16[256,768]{1,0:T(8,128)(2,1)S(1)}, u32[]{:S(2)}, u32[]{:S(2)}) collective-permute-start(bf16[256,768]{1,0:T(8,128)(2,1)} %get-tuple-element.123), channel_id=1, source_target_pairs={{0,2},{1,3},{2,0},{3,1},{4,6},{5,7},{6,4},{7,5},{8,10},{9,11},{10,... | collective-permute-start | bytes 1179656 | tf_op jit(solution)/shard_map/ppermute | solution.py:1041
  176.7 18.4 %collective-permute-start.34 = (bf16[256,768]{1,0:T(8,128)(2,1)}, bf16[256,768]{1,0:T(8,128)(2,1)S(1)}, u32[]{:S(2)}, u32[]{:S(2)}) collective-permute-start(bf16[256,768]{1,0:T(8,128)(2,1)} %get-tuple-element.139), channel_id=1, source_target_pairs={{0,1},{1,0},{2,3},{3,2},{4,5},{5,4},{6,7},{7,6},{8,9},{9,8},{10,11... | collective-permute-start | bytes 1179656 | tf_op jit(solution)/shard_map/ppermute | solution.py:1061
  176.9 17.7 %collective-permute-start.47 = (bf16[96,768]{1,0:T(8,128)(2,1)S(1)}, bf16[96,768]{1,0:T(8,128)(2,1)S(1)}, u32[]{:S(2)}, u32[]{:S(2)}) collective-permute-start(bf16[96,768]{1,0:T(8,128)(2,1)S(1)} %slice.25), channel_id=1, source_target_pairs={{0,16},{16,0},{1,17},{17,1},{2,18},{18,2},{3,19},{19,3},{4,20},{20... | collective-permute-start | bytes 442376 | tf_op jit(solution)/shard_map/ppermute | solution.py:1047
  178.6 9.5 %collective-permute-start.40 = (bf16[112,512]{1,0:T(8,128)(2,1)S(1)}, bf16[112,512]{1,0:T(8,128)(2,1)S(1)}, u32[]{:S(2)}, u32[]{:S(2)}) collective-permute-start(bf16[112,512]{1,0:T(8,128)(2,1)S(1)} %copy-done.51), channel_id=1, source_target_pairs={{0,16},{16,0},{1,17},{17,1},{2,18},{18,2},{3,19},{19,3},{4,20},{20... | collective-permute-start | bytes 344072 | tf_op jit(solution)/shard_map/ppermute | solution.py:1055
  182.4 8.9 %collective-permute-start.42 = (bf16[112,512]{1,0:T(8,128)(2,1)S(1)}, bf16[112,512]{1,0:T(8,128)(2,1)S(1)}, u32[]{:S(2)}, u32[]{:S(2)}) collective-permute-start(bf16[112,512]{1,0:T(8,128)(2,1)S(1)} %copy-done.50), channel_id=1, source_target_pairs={{0,16},{16,0},{1,17},{17,1},{2,18},{18,2},{3,19},{19,3},{4,20},{20... | collective-permute-start | bytes 344072 | tf_op jit(solution)/shard_map/ppermute | solution.py:1055
  188.0 11.7 %collective-permute-start.37 = (bf16[112,512]{1,0:T(8,128)(2,1)}, bf16[112,512]{1,0:T(8,128)(2,1)S(1)}, u32[]{:S(2)}, u32[]{:S(2)}) collective-permute-start(bf16[112,512]{1,0:T(8,128)(2,1)} %get-tuple-element.142), channel_id=1, source_target_pairs={{0,16},{16,0},{1,17},{17,1},{2,18},{18,2},{3,19},{19,3},{4,20},{20... | collective-permute-start | bytes 344072 | tf_op jit(solution)/shard_map/ppermute | solution.py:1055
  191.3 11.5 %collective-permute-start.39 = (bf16[112,512]{1,0:T(8,128)(2,1)}, bf16[112,512]{1,0:T(8,128)(2,1)S(1)}, u32[]{:S(2)}, u32[]{:S(2)}) collective-permute-start(bf16[112,512]{1,0:T(8,128)(2,1)} %shard_map.309), channel_id=1, source_target_pairs={{0,4},{4,8},{8,12},{12,0},{1,5},{5,9},{9,13},{13,1},{2,6},{6,10},{... | collective-permute-start | bytes 344072 | tf_op jit(solution)/shard_map/ppermute | solution.py:1059
  194.6 8.5 %collective-permute-start.41 = (bf16[112,512]{1,0:T(8,128)(2,1)}, bf16[112,512]{1,0:T(8,128)(2,1)S(1)}, u32[]{:S(2)}, u32[]{:S(2)}) collective-permute-start(bf16[112,512]{1,0:T(8,128)(2,1)} %shard_map.310), channel_id=1, source_target_pairs={{0,8},{4,12},{8,0},{12,4},{1,9},{5,13},{9,1},{13,5},{2,10},{6,14},... | collective-permute-start | bytes 344072 | tf_op jit(solution)/shard_map/ppermute | solution.py:1059
  199.7 15.0 %collective-permute-start.35 = (bf16[256,768]{1,0:T(8,128)(2,1)}, bf16[256,768]{1,0:T(8,128)(2,1)S(1)}, u32[]{:S(2)}, u32[]{:S(2)}) collective-permute-start(bf16[256,768]{1,0:T(8,128)(2,1)} %shard_map.307), channel_id=1, source_target_pairs={{0,2},{1,3},{2,0},{3,1},{4,6},{5,7},{6,4},{7,5},{8,10},{9,11},{10,... | collective-permute-start | bytes 1179656 | tf_op jit(solution)/shard_map/ppermute | solution.py:1065
  (72 other events, 633.0 us)

commit v2 on v1

--- a/solution.py
+++ b/solution.py
@@ -13,6 +13,7 @@
 NN = ((1,), (0,))
 NT = ((1,), (1,))
 TN = ((0,), (0,))
+AS, AC, AT = "shard", "ctx", "tp"
 HI = lax.Precision.HIGHEST
 
 
@@ -63,7 +64,7 @@
         self.bounds = bounds
 
     def place(self, i, sign):
-        n_ctx, n_sh = self.sizes["ctx"], self.sizes["shards"] // self.sizes["ctx"]
+        n_ctx, n_sh = self.sizes[AC], self.sizes["shards"] // self.sizes[AC]
         shard = lax.rem(self.me_s + i // n_ctx, n_sh)
         ctx = lax.rem(self.me_c + sign * (i % n_ctx) + n_ctx, n_ctx)
         return (shard * n_ctx + ctx) * (self.sizes["D"] // self.sizes["shards"])
@@ -266,7 +267,7 @@
 
 def build(sizes):
     T, D, IN, N, H, TAPS = (sizes[k] for k in ("T", "D", "IN", "N", "H", "TAPS"))
-    n_tp, n_ctx, nC = sizes["tp"], sizes["ctx"], sizes["T"] // L
+    n_tp, n_ctx, nC = sizes[AT], sizes[AC], sizes["T"] // L
     HW = IN // H
     HPT = 128 // HW
     SL = 2 * N // n_tp
@@ -962,8 +963,8 @@
           a_log, d_skip, gate_gain, seq_lens, token_mask, d_out):
     T, D = x_in.shape
     H, IN, N, TAPS = dt_bias.shape[0], w_z.shape[1], w_bc.shape[1] // 2, conv_wx.shape[0]
-    n_sh, n_ctx, n_tp = (lax.axis_size(a) for a in ("shard", "ctx", "tp"))
-    me_s, me_c, me_t = (lax.axis_index(a) for a in ("shard", "ctx", "tp"))
+    n_sh, n_ctx, n_tp = (lax.axis_size(a) for a in (AS, AC, AT))
+    me_s, me_c, me_t = (lax.axis_index(a) for a in (AS, AC, AT))
     direct = n_sh == 2 and n_ctx == 4
     NSH = n_sh * n_ctx if direct else 1
     seqs = seq_lens.shape[1]
@@ -981,13 +982,13 @@
 
     def gather(part):
         if not direct:
-            return [lax.all_gather(part, ("shard", "ctx"), axis=0, tiled=True)]
+            return [lax.all_gather(part, (AS, AC), axis=0, tiled=True)]
         here = [part]
         for k in range(1, n_ctx):
-            here.append(lax.ppermute(part, "ctx", ring(n_ctx, k)))
+            here.append(lax.ppermute(part, AC, ring(n_ctx, k)))
         there = []
         for p in here:
-            there.append(lax.ppermute(p, "shard", ring(n_sh, 1)))
+            there.append(lax.ppermute(p, AS, ring(n_sh, 1)))
         return here + there
 
     meta = jnp.concatenate([jnp.stack([me_s, me_c, me_t]).astype(jnp.int32), seq_lens[0]])
@@ -996,7 +997,7 @@
     first = jnp.concatenate(
         [w_x, w_slice, w_dt, norm_gain[:, None], jnp.zeros((br, 127 - SL - H), bf16), w_bc], axis=1
     )
-    x_tail = lax.ppermute(x_in[T - 8 :], "ctx", [(i, i + 1) for i in range(n_ctx - 1)])
+    x_tail = lax.ppermute(x_in[T - 8 :], AC, [(i, i + 1) for i in range(n_ctx - 1)])
     shards = gather(first)
     second = jnp.concatenate([w_z, w_out], axis=1)
     shards2 = gather(second)
@@ -1007,44 +1008,44 @@
 
     (nb, pr, prh, sm, act, dt, cum, dtr, cumr, hpre, pp, pack, gain_row) = ops["project"](
         meta, x_in, x_tail, cw, hp, hc, mask8, shards)
-    packs = [lax.ppermute(pack, "ctx", [(i, i + k) for i in range(n_ctx - k)]) for k in range(1, n_ctx)]
+    packs = [lax.ppermute(pack, AC, [(i, i + k) for i in range(n_ctx - k)]) for k in range(1, n_ctx)]
     y_in = ops["intra"](meta, act, dt, cum, cumr)
     z, dm = ops["gate"](meta, nb, d_out, shards2)
     y, stat, entry = ops["output"](meta, act, cum, y_in, z, dm, hpre, pp, hp, gg, packs)
-    stats = [stat] + [lax.ppermute(stat, "tp", xor(n_tp, k)) for k in range(1, n_tp)]
+    stats = [stat] + [lax.ppermute(stat, AT, xor(n_tp, k)) for k in range(1, n_tp)]
     mix, dz, dy, suf, psuf, bpack, ssum = ops["norm"](meta, act, cum, y, z, dm, hp, gg, stats)
     bpacks = []
     for k in range(1, n_ctx):
-        bpacks.append(lax.ppermute(bpack, "ctx", [(i + k, i) for i in range(n_ctx - k)]))
+        bpacks.append(lax.ppermute(bpack, AC, [(i + k, i) for i in range(n_ctx - k)]))
     dxd, dbc = ops["intra_back"](meta, act, dt, cum, cumr, dy)
     groups, b_keep, b_send = ops["outer"](meta, nb, d_out, mix, dz, shards2)
 
     def both_halves(part):
         mine = part.astype(bf16)
-        other = lax.ppermute(mine, "tp", xor(n_tp, 1))
+        other = lax.ppermute(mine, AT, xor(n_tp, 1))
         flip = me_t % 2 == 1
         low, high = jnp.where(flip, other, mine), jnp.where(flip, mine, other)
         return jnp.concatenate([low, high], axis=0).astype(f32)
 
-    b_got = lax.ppermute(b_send, "tp", xor(n_tp, 1))
+    b_got = lax.ppermute(b_send, AT, xor(n_tp, 1))
     (dsx, ddt, sums, edge, b_pair), slices, edges = ops["scan_back"](
         meta, act, sm, pr, dt, cum, dtr, y, dy, dxd, dbc, hpre, pp, entry, suf, psuf, hp, hc, mask8,
         b_keep, b_got, bpacks)
-    got_edge = lax.ppermute(edge, "ctx", [(i + 1, i) for i in range(n_ctx - 1)])
+    got_edge = lax.ppermute(edge, AC, [(i + 1, i) for i in range(n_ctx - 1)])
     got_slices, got_edges = [slices[0]], []
     for k in range(1, n_tp):
-        got_slices.append(lax.ppermute(slices[k], "tp", xor(n_tp, k)))
+        got_slices.append(lax.ppermute(slices[k], AT, xor(n_tp, k)))
         across = [((i + 1) * n_tp + j, i * n_tp + (j ^ k)) for i in range(n_ctx - 1) for j in range(n_tp)]
-        got_edges.append(lax.ppermute(edges[k - 1], ("ctx", "tp"), across))
+        got_edges.append(lax.ppermute(edges[k - 1], (AC, AT), across))
     b_half = b_pair.astype(f32)
     for k in range(2, n_tp, 2):
-        b_half = b_half + lax.ppermute(b_pair, "tp", xor(n_tp, k)).astype(f32)
+        b_half = b_half + lax.ppermute(b_pair, AT, xor(n_tp, k)).astype(f32)
     if direct:
         total = groups[0].astype(f32)
         for r in range(1, n_ctx):
-            got = lax.ppermute(groups[r], "ctx", ring(n_ctx, r))
+            got = lax.ppermute(groups[r], AC, ring(n_ctx, r))
             total = total + got.astype(f32)
-        other = lax.ppermute(total[br:].astype(bf16), "shard", ring(n_sh, 1))
+        other = lax.ppermute(total[br:].astype(bf16), AS, ring(n_sh, 1))
         parts = [total[:br], other]
     grads, (q_keep, q_send) = ops["conv_back"](
         meta, nb, pr, prh, dz, ddt, dsx, cw9, sums, ssum, got_edge, got_slices, got_edges, shards,
@@ -1052,17 +1053,17 @@
     if direct:
         moved = []
         for r in [*range(1, n_ctx), 0]:
-            got = lax.ppermute(grads[n_ctx + r], "shard", ring(n_sh, 1))
+            got = lax.ppermute(grads[n_ctx + r], AS, ring(n_sh, 1))
             moved.append(pair_sum(grads[r], got))
         blocks = [moved[-1]]
         for r in range(1, n_ctx):
-            blocks.append(lax.ppermute(moved[r - 1], "ctx", ring(n_ctx, r)))
-
-    q_got = lax.ppermute(q_send, "tp", xor(n_tp, 1))
+            blocks.append(lax.ppermute(moved[r - 1], AC, ring(n_ctx, r)))
+
+    q_got = lax.ppermute(q_send, AT, xor(n_tp, 1))
     q_pair = pair_sum(q_keep, q_got)
     q_half = q_pair.astype(f32)
     for k in range(2, n_tp, 2):
-        q_half = q_half + lax.ppermute(q_pair, "tp", xor(n_tp, k)).astype(f32)
+        q_half = q_half + lax.ppermute(q_pair, AT, xor(n_tp, k)).astype(f32)
     block_whole = both_halves(b_half)
     block_out = x_in + block_whole
 
@@ -1078,7 +1079,7 @@
             meta, first, second, blocks, parts, a_log[None, :])
         lasts = [last]
         for k in range(1, n_tp):
-            lasts.append(lax.ppermute(last, "tp", xor(n_tp, k)))
+            lasts.append(lax.ppermute(last, AT, xor(n_tp, k)))
         d_w_dt = g_slab[:, SL : SL + H]
         d_w_bc, d_norm_gain, d_cbc, d_bbc = ops["spread"](meta, lasts)
         return (
@@ -1086,7 +1087,7 @@
             d_cx, d_bx, d_cbc, d_bbc, d_dt_bias, d_a_log, d_skips, d_gg,
         )
 
-    axes = ("shard", "ctx")
+    axes = (AS, AC)
     total = lax.psum_scatter(groups[0].astype(f32), axes, scatter_dimension=0, tiled=True)
     g_first = lax.psum_scatter(grads[0][:D].astype(f32), axes, scatter_dimension=0, tiled=True)
     small = lax.psum(grads[0][D:].astype(f32), axes)
@@ -1102,7 +1103,7 @@
         jnp.concatenate([g_slab[:, :SL], d_gain[:, None], jnp.zeros((br, 127 - SL), f32)], axis=1),
         jnp.pad(jnp.concatenate([small[:TAPS], bias_row[None, :]], axis=0)[:, IN : IN + SL],
                 ((0, 7 - TAPS), (0, 128 - SL)))], axis=0)
-    last = lax.all_gather(last, "tp")
+    last = lax.all_gather(last, AT)
     d_w_bc = jnp.concatenate([last[k, :br, :SL] for k in range(n_tp)], axis=1)
     d_norm_gain = jnp.sum(last[:, :br, SL], axis=0)
     d_cbc = jnp.concatenate([last[k, br : br + TAPS + 1, :SL] for k in range(n_tp)], axis=1)
@@ -1116,14 +1117,14 @@
 
 
 def solution(mesh):
-    row = ("shard", "ctx")
+    row = (AS, AC)
     in_specs = (
-        P(row, None), P(row), P(row, "tp"), P(row, "tp"), P(row, None), P(row, "tp"), P(row, "tp"),
-        P(None, "tp"), P("tp"), P(), P(), P("tp"), P("tp"), P("tp"), P("tp"), P("shard", None), P(row),
+        P(row, None), P(row), P(row, AT), P(row, AT), P(row, None), P(row, AT), P(row, AT),
+        P(None, AT), P(AT), P(), P(), P(AT), P(AT), P(AT), P(AT), P(AS, None), P(row),
         P(row, None),
     )
     out_specs = (
-        P(row, None), P(row, None), P(row), P(row, "tp"), P(row, "tp"), P(row, None), P(row, "tp"),
-        P(row, "tp"), P(None, "tp"), P("tp"), P(), P(), P("tp"), P("tp"), P("tp"), P("tp"),
+        P(row, None), P(row, None), P(row), P(row, AT), P(row, AT), P(row, None), P(row, AT),
+        P(row, AT), P(None, AT), P(AT), P(), P(), P(AT), P(AT), P(AT), P(AT),
     )
     return jax.shard_map(block, mesh=mesh, in_specs=in_specs, out_specs=out_specs, check_vma=False)

time: 222 us -> 222 us (level)
  no operation moved by 1% of the time
where the time goes in v2:
time: 222 us; the launch traced here: 220 us
  Pallas kernels  73.2 us (33%)
  starting transfers between devices  67.3 us (30%)
  waiting for transfers between devices  55.1 us (25%)
  local copies, waits for them, and re-layouts  18.7 us (8%)
  other arithmetic  4.91 us (2%)
    pallas_call x12, Pallas kernels, call(): pl.pallas_call(kernel, grid=(grid,), in_specs=[spec(i) for i in ins], out...  64.4 us
    ppermute x3, waiting for transfers between devices, block(): got_edges.append(lax.ppermute(edges[k - 1], (AC, AT), across))  20.4 us
    ppermute x6, starting transfers between devices, gather(): here.append(lax.ppermute(part, AC, ring(n_ctx, k)))  17.7 us
    ppermute x8, starting transfers between devices, gather(): there.append(lax.ppermute(p, AS, ring(n_sh, 1)))  10.1 us
    unnamed x109, local copies, waits for them, and re-layouts  9.67 us
    ppermute x4, waiting for transfers between devices, block(): got = lax.ppermute(grads[n_ctx + r], AS, ring(n_sh, 1))  8.98 us
    pallas_call x5, Pallas kernels, pair_sum(): pl.pallas_call(kernel, in_specs=[vmem, vmem], out_specs=vmem, out_shape=j...  8.74 us
    ppermute x3, waiting for transfers between devices, block(): lax.ppermute(bpack, AC, [(i + k, i) for i in range(n_ctx - k)])  7.44 us
  transfers between devices with their start and end apart: 51, of which 20 were waited for; matrix products, arithmetic and copies ran while one was open for 6% of the time, Pallas kernels for 26%

profile of v2, /device:TPU:0, one launch (start us, length us, event | category | flops | bytes accessed | tf_op | source)
XLA Modules:
  0.0 220.5 jit_solution(527428772525491709)
XLA Ops:
  2.4 5.1 %collective-permute-start.10 = (bf16[96,768]{1,0:T(8,128)(2,1)S(1)}, bf16[96,768]{1,0:T(8,128)(2,1)S(1)}, u32[]{:S(2)}, u32[]{:S(2)}) collective-permute-start(bf16[96,768]{1,0:T(8,128)(2,1)S(1)} %constant_dynamic-update-slice_fusion.refs_3_.refs_5_.refs_28_.refs_2_), channel_id=1, source_target_pairs={{0,12},{4,0},{8,4},{12,8},{1,13},{5,1},{9,5},{13,9},{2,14},{6,2},{... | collective-permute-start | bytes 442376 | tf_op jit(solution)/shard_map/ppermute | solution.py:988
  11.5 2.6 %collective-permute-start.2 = (bf16[96,768]{1,0:T(8,128)(2,1)S(1)}, bf16[96,768]{1,0:T(8,128)(2,1)S(1)}, u32[]{:S(2)}, u32[]{:S(2)}) collective-permute-start(bf16[96,768]{1,0:T(8,128)(2,1)S(1)} %concatenate.16.refs_7_.refs_20_.refs_1_), channel_id=1, source_target_pairs={{0,8},{4,12},{8,0},{12,4},{1,9},{5,13},{9,1},{13,5},{2,10},{6,14},... | collective-permute-start | bytes 442376 | tf_op jit(solution)/shard_map/ppermute | solution.py:988
  14.8 3.8 %collective-permute-start = (f32[8,768]{1,0:T(8,128)S(1)}, f32[8,768]{1,0:T(8,128)S(1)}, u32[]{:S(2)}, u32[]{:S(2)}) collective-permute-start(f32[8,768]{1,0:T(8,128)S(1)} %slice.16), channel_id=1, source_target_pairs={{0,4},{4,8},{8,12},{1,5},{5,9},{9,13},{2,6},{6,10},{10,14},{3,7},{... | collective-permute-start | bytes 73736 | tf_op jit(solution)/shard_map/ppermute | solution.py:1000
  18.6 2.1 collective-permute-done.refs_2_
  20.7 7.0 %collective-permute-start.1 = (bf16[96,768]{1,0:T(8,128)(2,1)S(1)}, bf16[96,768]{1,0:T(8,128)(2,1)S(1)}, u32[]{:S(2)}, u32[]{:S(2)}) collective-permute-start(bf16[96,768]{1,0:T(8,128)(2,1)S(1)} %concatenate.16.refs_7_.refs_20_.refs_1_), channel_id=1, source_target_pairs={{0,4},{4,8},{8,12},{12,0},{1,5},{5,9},{9,13},{13,1},{2,6},{6,10},{... | collective-permute-start | bytes 442376 | tf_op jit(solution)/shard_map/ppermute | solution.py:988
  27.8 2.5 %collective-permute-start.8 = (bf16[96,768]{1,0:T(8,128)(2,1)S(1)}, bf16[96,768]{1,0:T(8,128)(2,1)S(1)}, u32[]{:S(2)}, u32[]{:S(2)}) collective-permute-start(bf16[96,768]{1,0:T(8,128)(2,1)S(1)} %constant_dynamic-update-slice_fusion.refs_3_.refs_5_.refs_28_.refs_2_), channel_id=1, source_target_pairs={{0,4},{4,8},{8,12},{12,0},{1,5},{5,9},{9,13},{13,1},{2,6},{6,10},{... | collective-permute-start | bytes 442376 | tf_op jit(solution)/shard_map/ppermute | solution.py:988
  48.6 1.8 shard_map.297
  51.1 8.9 %shard_map.298 = (bf16[512,768]{1,0:T(8,128)(2,1)}, bf16[512,768]{1,0:T(8,128)(2,1)}, f32[8,768]{1,0:T(8,128)}, f32[512,640]{1,0:T(8,128)}, f32[512,640]{1,0:T(8...) custom-call(s32[6]{0:T(128)} %pad_add_fusion.refs_0_, ...), custom_call_target="tpu_custom_call" | custom-call | flops 603979776 | bytes 9834520 | tf_op jit(solution)/shard_map/pallas_call | solution.py:183
  60.0 3.2 %collective-permute-start.17 = (bf16[144,384]{1,0:T(8,128)(2,1)}, bf16[144,384]{1,0:T(8,128)(2,1)S(1)}, u32[]{:S(2)}, u32[]{:S(2)}) collective-permute-start(bf16[144,384]{1,0:T(8,128)(2,1)} %get-tuple-element.109), channel_id=1, source_target_pairs={{0,12},{1,13},{2,14},{3,15},{16,28},{17,29},{18,30},{19,31}} | collective-permute-start | bytes 331784 | tf_op jit(solution)/shard_map/ppermute | solution.py:1011
  64.6 2.5 %collective-permute-start.15 = (bf16[144,384]{1,0:T(8,128)(2,1)}, bf16[144,384]{1,0:T(8,128)(2,1)S(1)}, u32[]{:S(2)}, u32[]{:S(2)}) collective-permute-start(bf16[144,384]{1,0:T(8,128)(2,1)} %get-tuple-element.109), channel_id=1, source_target_pairs={{0,4},{4,8},{8,12},{1,5},{5,9},{9,13},{2,6},{6,10},{10,14},{3,7},{... | collective-permute-start | bytes 331784 | tf_op jit(solution)/shard_map/ppermute | solution.py:1011
  67.1 4.0 %shard_map.299.refs_3_ = f32[512,384]{1,0:T(8,128)} custom-call(s32[6]{0:T(128)} %pad_add_fusion.refs_0_, f32[512,640]{1,0:T(8,128)} %get-tuple-element.96.refs_1_, f32[512,384]{1,0:T(8,128)} %get-tuple-element.99.refs_2_.refs_4_, f32[512,384]{1,0:T(8,128)} %get-tuple-element.100.refs_3_.refs_2_.refs_5_, f32[8,512]{1,0:T(8,128)} %get-tuple-element.102.refs_4_), custom_call_target="tpu_custom_call" | custom-call | flops 100663296 | bytes 3686424 | tf_op jit(solution)/shard_map/pallas_call | solution.py:183
  71.8 3.6 %shard_map.300 = (bf16[512,384]{1,0:T(8,128)(2,1)}, f32[512,384]{1,0:T(8,128)}) custom-call(s32[6]{0:T(128)} %pad_add_fusion.refs_0_, bf16[512,768]{1,0:T(8,128)(2,1)} %get-tuple-element.103.refs_1_, f32[512,768]{1,0:T(8,128)} %refs_2_.3, bf16[96,768]{1,0:T(8,128)(2,1)} %copy-done.3, bf16[96,768]{1,0:T(8,128)(2,1)} %copy-done.7, bf16[96,768]{1,0:T(8,128)(2,1)} %copy-done.6, ...), custom_call_target="tpu_custom_call" | custom-call | flops 603979776 | bytes 4718616 | tf_op jit(solution)/shard_map/pallas_call | solution.py:183
  76.2 4.4 %shard_map.301 = (f32[512,384]{1,0:T(8,128)}, f32[8,512]{1,0:T(8,128)}, f32[128,384]{1,0:T(8,128)}) custom-call(s32[6]{0:T(128)} %pad_add_fusion.refs_0_, f32[512,640]{1,0:T(8,128)} %get-tuple-element.96.refs_1_, f32[512,384]{1,0:T(8,128)} %get-tuple-element.100.refs_3_.refs_2_.refs_5_, f32[512,384]{1,0:T(8,128)} %shard_map.299.refs_3_, ...), custom_call_target="tpu_custom_call" | custom-call | flops 100663296 | bytes 6463512 | tf_op jit(solution)/shard_map/pallas_call | solution.py:183
  85.3 5.1 %shard_map.302 = (bf16[512,384]{1,0:T(8,128)(2,1)}, bf16[512,384]{1,0:T(8,128)(2,1)}, f32[512,384]{1,0:T(8,128)}, f32[512,384]{1,0:T(8,128)}, f32[32,384]{1,0:T(...) custom-call(s32[6]{0:T(128)} %pad_add_fusion.refs_0_, f32[512,640]{1,0:T(8,128)} %get-tuple-element.96.refs_1_, ...), custom_call_target="tpu_custom_call" | custom-call | flops 50331648 | bytes 6684696 | tf_op jit(solution)/shard_map/pallas_call | solution.py:183
  90.4 6.4 %shard_map.304 = (bf16[192,768]{1,0:T(8,128)(2,1)}, bf16[192,768]{1,0:T(8,128)(2,1)}, bf16[192,768]{1,0:T(8,128)(2,1)}, bf16[192,768]{1,0:T(8,128)(2,1)}, f32[256,768]{1,0:T(8,128)}, /*index=5*/bf16[256,768]{1,0:T(8,128)(2,1)}) custom-call(s32[6]{0:T(128)} %pad_add_fusion.refs_0_, bf16[512,768]{1,0:T(8,128)(2,1)} %get-tuple-element.103.refs_1_, ...), custom_call_target="tpu_custom_call" | custom-call | flops 905969664 | bytes 6684696 | tf_op jit(solution)/shard_map/pallas_call | solution.py:183
  101.1 2.7 %collective-permute-start.44 = (bf16[192,768]{1,0:T(8,128)(2,1)}, bf16[192,768]{1,0:T(8,128)(2,1)S(1)}, u32[]{:S(2)}, u32[]{:S(2)}) collective-permute-start(bf16[192,768]{1,0:T(8,128)(2,1)} %get-tuple-element.150), channel_id=1, source_target_pairs={{0,4},{4,8},{8,12},{12,0},{1,5},{5,9},{9,13},{13,1},{2,6},{6,10},{... | collective-permute-start | bytes 884744 | tf_op jit(solution)/shard_map/ppermute | solution.py:1046
  103.8 3.1 %collective-permute-done.24.refs_25_ = bf16[144,384]{1,0:T(8,128)(2,1)S(1)} collective-permute-done((bf16[144,384]{1,0:T(8,128)(2,1)S(1)}, bf16[144,384]{1,0:T(8,128)(2,1)S(1)}, u32[]{:S(2)}, u32[]{:S(2)}) %collective-permute-start.24) | collective-permute-done | bytes 110624 | tf_op jit(solution)/shard_map/ppermute | solution.py:1019
  107.4 4.3 %collective-permute-done.23.refs_24_ = bf16[144,384]{1,0:T(8,128)(2,1)S(1)} collective-permute-done((bf16[144,384]{1,0:T(8,128)(2,1)S(1)}, bf16[144,384]{1,0:T(8,128)(2,1)S(1)}, u32[]{:S(2)}, u32[]{:S(2)}) %collective-permute-start.23) | collective-permute-done | bytes 110624 | tf_op jit(solution)/shard_map/ppermute | solution.py:1019
  111.7 6.5 %shard_map.303 = (f32[512,384]{1,0:T(8,128)}, f32[512,256]{1,0:T(8,128)}) custom-call(s32[6]{0:T(128)} %pad_add_fusion.refs_0_, f32[512,640]{1,0:T(8,128)} %get-tuple-element.96.refs_1_, f32[512,384]{1,0:T(8,128)} %get-tuple-element.99.refs_2_.refs_4_, f32[512,384]{1,0:T(8,128)} %get-tuple-element.100.refs_3_.refs_2_.refs_5_, ...), custom_call_target="tpu_custom_call" | custom-call | flops 201326592 | bytes 4997144 | tf_op jit(solution)/shard_map/pallas_call | solution.py:183
  119.0 10.4 %shard_map.305 = (f32[512,384]{1,0:T(8,128)}, bf16[512,128]{1,0:T(8,128)(2,1)}, f32[16,128]{1,0:T(8,128)}, f32[8,512]{1,0:T(8,128)}, bf16[256,768]{1,0:T(8,128)(...) custom-call(s32[6]{0:T(128)} %pad_add_fusion.refs_0_, ...), custom_call_target="tpu_custom_call" | custom-call | flops 150994944 | bytes 14155800 | tf_op jit(solution)/shard_map/pallas_call | solution.py:183
  130.8 10.3 %collective-permute-done.31.refs_17_ = f32[8,128]{1,0:T(8,128)S(1)} collective-permute-done((f32[8,128]{1,0:T(8,128)}, f32[8,128]{1,0:T(8,128)S(1)}, u32[]{:S(2)}, u32[]{:S(2)}) %collective-permute-start.31) | collective-permute-done | bytes 4128 | tf_op jit(solution)/shard_map/ppermute | solution.py:1039
  142.4 5.3 %collective-permute-done.32.refs_18_ = f32[8,128]{1,0:T(8,128)S(1)} collective-permute-done((f32[8,128]{1,0:T(8,128)}, f32[8,128]{1,0:T(8,128)S(1)}, u32[]{:S(2)}, u32[]{:S(2)}) %collective-permute-start.32) | collective-permute-done | bytes 4128 | tf_op jit(solution)/shard_map/ppermute | solution.py:1039
  149.0 4.7 %collective-permute-done.33.refs_19_ = f32[8,128]{1,0:T(8,128)S(1)} collective-permute-done((f32[8,128]{1,0:T(8,128)}, f32[8,128]{1,0:T(8,128)S(1)}, u32[]{:S(2)}, u32[]{:S(2)}) %collective-permute-start.33) | collective-permute-done | bytes 4128 | tf_op jit(solution)/shard_map/ppermute | solution.py:1039
  155.1 4.5 %collective-permute-done.27.refs_12_ = f32[8,512]{1,0:T(8,128)S(1)} collective-permute-done((f32[8,512]{1,0:T(8,128)}, f32[8,512]{1,0:T(8,128)S(1)}, u32[]{:S(2)}, u32[]{:S(2)}) %collective-permute-start.27) | collective-permute-done | bytes 16416 | tf_op jit(solution)/shard_map/ppermute | solution.py:1034
  161.1 3.0 %collective-permute-done.29.refs_15_ = bf16[256,128]{1,0:T(8,128)(2,1)S(1)} collective-permute-done((bf16[256,128]{1,0:T(8,128)(2,1)}, bf16[256,128]{1,0:T(8,128)(2,1)S(1)}, u32[]{:S(2)}, u32[]{:S(2)}) %collective-permute-start.29) | collective-permute-done | bytes 65568 | tf_op jit(solution)/shard_map/ppermute | solution.py:1037
  164.1 2.2 collective-permute-start.25
  166.9 9.3 %shard_map.306 = (bf16[112,512]{1,0:T(8,128)(2,1)}, bf16[112,512]{1,0:T(8,128)(2,1)}, bf16[112,512]{1,0:T(8,128)(2,1)}, bf16[112,512]{1,0:T(8,128)(2,1)}, bf16[1...) custom-call(s32[6]{0:T(128)} %pad_add_fusion.refs_0_, ...), custom_call_target="tpu_custom_call" | custom-call | flops 1409286144 | bytes 9265176 | tf_op jit(solution)/shard_map/pallas_call | solution.py:183
  179.0 3.4 %collective-permute-done.38.b = bf16[112,512]{1,0:T(8,128)(2,1)S(1)} collective-permute-done((bf16[112,512]{1,0:T(8,128)(2,1)}, bf16[112,512]{1,0:T(8,128)(2,1)S(1)}, u32[]{:S(2)}, u32[]{:S(2)}) %collective-permute-start.38) | collective-permute-done | bytes 114720 | tf_op jit(solution)/shard_map/ppermute | solution.py:1056
  182.4 5.6 %collective-permute-done.40.b = bf16[112,512]{1,0:T(8,128)(2,1)S(1)} collective-permute-done((bf16[112,512]{1,0:T(8,128)(2,1)S(1)}, bf16[112,512]{1,0:T(8,128)(2,1)S(1)}, u32[]{:S(2)}, u32[]{:S(2)}) %collective-permute-start.40) | collective-permute-done | bytes 114720 | tf_op jit(solution)/shard_map/ppermute | solution.py:1056
  195.1 2.5 %collective-permute-start.43 = (bf16[112,512]{1,0:T(8,128)(2,1)}, bf16[112,512]{1,0:T(8,128)(2,1)}, u32[]{:S(2)}, u32[]{:S(2)}) collective-permute-start(bf16[112,512]{1,0:T(8,128)(2,1)} %shard_map.311), channel_id=1, source_target_pairs={{0,12},{4,0},{8,4},{12,8},{1,13},{5,1},{9,5},{13,9},{2,14},{6,2},{... | collective-permute-start | bytes 344072 | tf_op jit(solution)/shard_map/ppermute | solution.py:1060
  197.6 2.0 shard_map.307
  203.8 2.4 %shard_map.312 = (f32[96,384]{1,0:T(8,128)}, f32[96,384]{1,0:T(8,128)}, f32[96,384]{1,0:T(8,128)}, f32[96,128]{1,0:T(8,128)}, f32[4,384]{1,0:T(4,128)}, /*index=...) custom-call(s32[6]{0:T(128)} %pad_add_fusion.refs_0_, ...), custom_call_target="tpu_custom_call" | custom-call | bytes 1750136 | tf_op jit(solution)/shard_map/pallas_call | solution.py:183
  (218 shorter events, 73.8 us)
Async XLA Ops:
  2.4 25.3 %collective-permute-start.10 = (bf16[96,768]{1,0:T(8,128)(2,1)S(1)}, bf16[96,768]{1,0:T(8,128)(2,1)S(1)}, u32[]{:S(2)}, u32[]{:S(2)}) collective-permute-start(bf16[96,768]{1,0:T(8,128)(2,1)S(1)} %constant_dynamic-update-slice_fusion.refs_3_.refs_5_.refs_28_.refs_2_), channel_id=1, source_target_pairs={{0,12},{4,0},{8,4},{12,8},{1,13},{5,1},{9,5},{13,9},{2,14},{6,2},{... | collective-permute-start | bytes 442376 | tf_op jit(solution)/shard_map/ppermute | solution.py:988
  7.6 22.7 %collective-permute-start.9 = (bf16[96,768]{1,0:T(8,128)(2,1)S(1)}, bf16[96,768]{1,0:T(8,128)(2,1)S(1)}, u32[]{:S(2)}, u32[]{:S(2)}) collective-permute-start(bf16[96,768]{1,0:T(8,128)(2,1)S(1)} %constant_dynamic-update-slice_fusion.refs_3_.refs_5_.refs_28_.refs_2_), channel_id=1, source_target_pairs={{0,8},{4,12},{8,0},{12,4},{1,9},{5,13},{9,1},{13,5},{2,10},{6,14},... | collective-permute-start | bytes 442376 | tf_op jit(solution)/shard_map/ppermute | solution.py:988
  11.0 20.8 %collective-permute-start.3 = (bf16[96,768]{1,0:T(8,128)(2,1)S(1)}, bf16[96,768]{1,0:T(8,128)(2,1)S(1)}, u32[]{:S(2)}, u32[]{:S(2)}) collective-permute-start(bf16[96,768]{1,0:T(8,128)(2,1)S(1)} %concatenate.16.refs_7_.refs_20_.refs_1_), channel_id=1, source_target_pairs={{0,12},{4,0},{8,4},{12,8},{1,13},{5,1},{9,5},{13,9},{2,14},{6,2},{... | collective-permute-start | bytes 442376 | tf_op jit(solution)/shard_map/ppermute | solution.py:988
  11.5 20.8 %collective-permute-start.2 = (bf16[96,768]{1,0:T(8,128)(2,1)S(1)}, bf16[96,768]{1,0:T(8,128)(2,1)S(1)}, u32[]{:S(2)}, u32[]{:S(2)}) collective-permute-start(bf16[96,768]{1,0:T(8,128)(2,1)S(1)} %concatenate.16.refs_7_.refs_20_.refs_1_), channel_id=1, source_target_pairs={{0,8},{4,12},{8,0},{12,4},{1,9},{5,13},{9,1},{13,5},{2,10},{6,14},... | collective-permute-start | bytes 442376 | tf_op jit(solution)/shard_map/ppermute | solution.py:988
  20.7 13.1 %collective-permute-start.1 = (bf16[96,768]{1,0:T(8,128)(2,1)S(1)}, bf16[96,768]{1,0:T(8,128)(2,1)S(1)}, u32[]{:S(2)}, u32[]{:S(2)}) collective-permute-start(bf16[96,768]{1,0:T(8,128)(2,1)S(1)} %concatenate.16.refs_7_.refs_20_.refs_1_), channel_id=1, source_target_pairs={{0,4},{4,8},{8,12},{12,0},{1,5},{5,9},{9,13},{13,1},{2,6},{6,10},{... | collective-permute-start | bytes 442376 | tf_op jit(solution)/shard_map/ppermute | solution.py:988
  32.3 11.0 %collective-permute-start.6 = (bf16[96,768]{1,0:T(8,128)(2,1)S(1)}, bf16[96,768]{1,0:T(8,128)(2,1)S(1)}, u32[]{:S(2)}, u32[]{:S(2)}) collective-permute-start(bf16[96,768]{1,0:T(8,128)(2,1)S(1)} %collective-permute-done.2.refs_9_.refs_22_), channel_id=1, source_target_pairs={{0,16},{16,0},{1,17},{17,1},{2,18},{18,2},{3,19},{19,3},{4,20},{20... | collective-permute-start | bytes 442376 | tf_op jit(solution)/shard_map/ppermute | solution.py:991
  33.8 16.6 %collective-permute-start.5 = (bf16[96,768]{1,0:T(8,128)(2,1)S(1)}, bf16[96,768]{1,0:T(8,128)(2,1)S(1)}, u32[]{:S(2)}, u32[]{:S(2)}) collective-permute-start(bf16[96,768]{1,0:T(8,128)(2,1)S(1)} %collective-permute-done.1.refs_8_.refs_21_), channel_id=1, source_target_pairs={{0,16},{16,0},{1,17},{17,1},{2,18},{18,2},{3,19},{19,3},{4,20},{20... | collective-permute-start | bytes 442376 | tf_op jit(solution)/shard_map/ppermute | solution.py:991
  34.7 28.6 %collective-permute-start.11 = (bf16[96,768]{1,0:T(8,128)(2,1)S(1)}, bf16[96,768]{1,0:T(8,128)(2,1)S(1)}, u32[]{:S(2)}, u32[]{:S(2)}) collective-permute-start(bf16[96,768]{1,0:T(8,128)(2,1)S(1)} %constant_dynamic-update-slice_fusion.refs_3_.refs_5_.refs_28_.refs_2_), channel_id=1, source_target_pairs={{0,16},{16,0},{1,17},{17,1},{2,18},{18,2},{3,19},{19,3},{4,20},{20... | collective-permute-start | bytes 442376 | tf_op jit(solution)/shard_map/ppermute | solution.py:991
  37.0 27.6 %collective-permute-start.14 = (bf16[96,768]{1,0:T(8,128)(2,1)S(1)}, bf16[96,768]{1,0:T(8,128)(2,1)S(1)}, u32[]{:S(2)}, u32[]{:S(2)}) collective-permute-start(bf16[96,768]{1,0:T(8,128)(2,1)S(1)} %collective-permute-done.10.refs_6_.refs_8_.refs_31_), channel_id=1, source_target_pairs={{0,16},{16,0},{1,17},{17,1},{2,18},{18,2},{3,19},{19,3},{4,20},{20... | collective-permute-start | bytes 442376 | tf_op jit(solution)/shard_map/ppermute | solution.py:991
  40.1 31.0 %collective-permute-start.13 = (bf16[96,768]{1,0:T(8,128)(2,1)S(1)}, bf16[96,768]{1,0:T(8,128)(2,1)S(1)}, u32[]{:S(2)}, u32[]{:S(2)}) collective-permute-start(bf16[96,768]{1,0:T(8,128)(2,1)S(1)} %collective-permute-done.9.refs_5_.refs_7_.refs_30_), channel_id=1, source_target_pairs={{0,16},{16,0},{1,17},{17,1},{2,18},{18,2},{3,19},{19,3},{4,20},{20... | collective-permute-start | bytes 442376 | tf_op jit(solution)/shard_map/ppermute | solution.py:991
  43.3 27.8 %collective-permute-start.12 = (bf16[96,768]{1,0:T(8,128)(2,1)S(1)}, bf16[96,768]{1,0:T(8,128)(2,1)S(1)}, u32[]{:S(2)}, u32[]{:S(2)}) collective-permute-start(bf16[96,768]{1,0:T(8,128)(2,1)S(1)} %collective-permute-done.8.refs_4_.refs_6_.refs_29_), channel_id=1, source_target_pairs={{0,16},{16,0},{1,17},{17,1},{2,18},{18,2},{3,19},{19,3},{4,20},{20... | collective-permute-start | bytes 442376 | tf_op jit(solution)/shard_map/ppermute | solution.py:991
  60.0 15.5 %collective-permute-start.17 = (bf16[144,384]{1,0:T(8,128)(2,1)}, bf16[144,384]{1,0:T(8,128)(2,1)S(1)}, u32[]{:S(2)}, u32[]{:S(2)}) collective-permute-start(bf16[144,384]{1,0:T(8,128)(2,1)} %get-tuple-element.109), channel_id=1, source_target_pairs={{0,12},{1,13},{2,14},{3,15},{16,28},{17,29},{18,30},{19,31}} | collective-permute-start | bytes 331784 | tf_op jit(solution)/shard_map/ppermute | solution.py:1011
  63.3 12.2 %collective-permute-start.16 = (bf16[144,384]{1,0:T(8,128)(2,1)}, bf16[144,384]{1,0:T(8,128)(2,1)S(1)}, u32[]{:S(2)}, u32[]{:S(2)}) collective-permute-start(bf16[144,384]{1,0:T(8,128)(2,1)} %get-tuple-element.109), channel_id=1, source_target_pairs={{0,8},{4,12},{1,9},{5,13},{2,10},{6,14},{3,11},{7,15},{16,24},{20,... | collective-permute-start | bytes 331784 | tf_op jit(solution)/shard_map/ppermute | solution.py:1011
  64.6 10.9 %collective-permute-start.15 = (bf16[144,384]{1,0:T(8,128)(2,1)}, bf16[144,384]{1,0:T(8,128)(2,1)S(1)}, u32[]{:S(2)}, u32[]{:S(2)}) collective-permute-start(bf16[144,384]{1,0:T(8,128)(2,1)} %get-tuple-element.109), channel_id=1, source_target_pairs={{0,4},{4,8},{8,12},{1,5},{5,9},{9,13},{2,6},{6,10},{10,14},{3,7},{... | collective-permute-start | bytes 331784 | tf_op jit(solution)/shard_map/ppermute | solution.py:1011
  96.8 21.4 %collective-permute-start.21 = (bf16[256,768]{1,0:T(8,128)(2,1)}, bf16[256,768]{1,0:T(8,128)(2,1)S(1)}, u32[]{:S(2)}, u32[]{:S(2)}) collective-permute-start(bf16[256,768]{1,0:T(8,128)(2,1)} %get-tuple-element.121), channel_id=1, source_target_pairs={{0,1},{1,0},{2,3},{3,2},{4,5},{5,4},{6,7},{7,6},{8,9},{9,8},{10,11... | collective-permute-start | bytes 1179656 | tf_op jit(solution)/shard_map/ppermute | solution.py:1030
  97.2 9.7 %collective-permute-start.24 = (bf16[144,384]{1,0:T(8,128)(2,1)S(1)}, bf16[144,384]{1,0:T(8,128)(2,1)S(1)}, u32[]{:S(2)}, u32[]{:S(2)}) collective-permute-start(bf16[144,384]{1,0:T(8,128)(2,1)S(1)} %copy-done.52), channel_id=1, source_target_pairs={{12,0},{13,1},{14,2},{15,3},{28,16},{29,17},{30,18},{31,19}} | collective-permute-start | bytes 331784 | tf_op jit(solution)/shard_map/ppermute | solution.py:1019
  98.5 13.2 %collective-permute-start.23 = (bf16[144,384]{1,0:T(8,128)(2,1)S(1)}, bf16[144,384]{1,0:T(8,128)(2,1)S(1)}, u32[]{:S(2)}, u32[]{:S(2)}) collective-permute-start(bf16[144,384]{1,0:T(8,128)(2,1)S(1)} %copy-done.52), channel_id=1, source_target_pairs={{8,0},{12,4},{9,1},{13,5},{10,2},{14,6},{11,3},{15,7},{24,16},{28,... | collective-permute-start | bytes 331784 | tf_op jit(solution)/shard_map/ppermute | solution.py:1019
  99.8 18.4 %collective-permute-start.22 = (bf16[144,384]{1,0:T(8,128)(2,1)S(1)}, bf16[144,384]{1,0:T(8,128)(2,1)S(1)}, u32[]{:S(2)}, u32[]{:S(2)}) collective-permute-start(bf16[144,384]{1,0:T(8,128)(2,1)S(1)} %copy-done.52), channel_id=1, source_target_pairs={{4,0},{8,4},{12,8},{5,1},{9,5},{13,9},{6,2},{10,6},{14,10},{7,3},{... | collective-permute-start | bytes 331784 | tf_op jit(solution)/shard_map/ppermute | solution.py:1019
  101.1 75.6 %collective-permute-start.44 = (bf16[192,768]{1,0:T(8,128)(2,1)}, bf16[192,768]{1,0:T(8,128)(2,1)S(1)}, u32[]{:S(2)}, u32[]{:S(2)}) collective-permute-start(bf16[192,768]{1,0:T(8,128)(2,1)} %get-tuple-element.150), channel_id=1, source_target_pairs={{0,4},{4,8},{8,12},{12,0},{1,5},{5,9},{9,13},{13,1},{2,6},{6,10},{... | collective-permute-start | bytes 884744 | tf_op jit(solution)/shard_map/ppermute | solution.py:1046
  106.9 69.8 %collective-permute-start.45 = (bf16[192,768]{1,0:T(8,128)(2,1)}, bf16[192,768]{1,0:T(8,128)(2,1)S(1)}, u32[]{:S(2)}, u32[]{:S(2)}) collective-permute-start(bf16[192,768]{1,0:T(8,128)(2,1)} %get-tuple-element.151), channel_id=1, source_target_pairs={{0,8},{4,12},{8,0},{12,4},{1,9},{5,13},{9,1},{13,5},{2,10},{6,14},... | collective-permute-start | bytes 884744 | tf_op jit(solution)/shard_map/ppermute | solution.py:1046
  111.7 65.1 %collective-permute-start.46 = (bf16[192,768]{1,0:T(8,128)(2,1)}, bf16[192,768]{1,0:T(8,128)(2,1)S(1)}, u32[]{:S(2)}, u32[]{:S(2)}) collective-permute-start(bf16[192,768]{1,0:T(8,128)(2,1)} %get-tuple-element.152), channel_id=1, source_target_pairs={{0,12},{4,0},{8,4},{12,8},{1,13},{5,1},{9,5},{13,9},{2,14},{6,2},{... | collective-permute-start | bytes 884744 | tf_op jit(solution)/shard_map/ppermute | solution.py:1046
  129.4 31.7 %collective-permute-start.28 = (bf16[256,128]{1,0:T(8,128)(2,1)}, bf16[256,128]{1,0:T(8,128)(2,1)S(1)}, u32[]{:S(2)}, u32[]{:S(2)}) collective-permute-start(bf16[256,128]{1,0:T(8,128)(2,1)} %get-tuple-element.132), channel_id=1, source_target_pairs={{0,1},{1,0},{2,3},{3,2},{4,5},{5,4},{6,7},{7,6},{8,9},{9,8},{10,11... | collective-permute-start | bytes 196616 | tf_op jit(solution)/shard_map/ppermute | solution.py:1037
  129.5 11.6 %collective-permute-start.31 = (f32[8,128]{1,0:T(8,128)}, f32[8,128]{1,0:T(8,128)S(1)}, u32[]{:S(2)}, u32[]{:S(2)}) collective-permute-start(f32[8,128]{1,0:T(8,128)} %get-tuple-element.135), channel_id=1, source_target_pairs={{4,1},{5,0},{6,3},{7,2},{8,5},{9,4},{10,7},{11,6},{12,9},{13,8},{1... | collective-permute-start | bytes 12296 | tf_op jit(solution)/shard_map/ppermute | solution.py:1039
  164.1 50.3 %collective-permute-start.25 = (bf16[256,768]{1,0:T(8,128)(2,1)}, bf16[256,768]{1,0:T(8,128)(2,1)S(1)}, u32[]{:S(2)}, u32[]{:S(2)}) collective-permute-start(bf16[256,768]{1,0:T(8,128)(2,1)} %get-tuple-element.123), channel_id=1, source_target_pairs={{0,2},{1,3},{2,0},{3,1},{4,6},{5,7},{6,4},{7,5},{8,10},{9,11},{10,... | collective-permute-start | bytes 1179656 | tf_op jit(solution)/shard_map/ppermute | solution.py:1042
  176.7 18.4 %collective-permute-start.34 = (bf16[256,768]{1,0:T(8,128)(2,1)}, bf16[256,768]{1,0:T(8,128)(2,1)S(1)}, u32[]{:S(2)}, u32[]{:S(2)}) collective-permute-start(bf16[256,768]{1,0:T(8,128)(2,1)} %get-tuple-element.139), channel_id=1, source_target_pairs={{0,1},{1,0},{2,3},{3,2},{4,5},{5,4},{6,7},{7,6},{8,9},{9,8},{10,11... | collective-permute-start | bytes 1179656 | tf_op jit(solution)/shard_map/ppermute | solution.py:1062
  176.9 17.7 %collective-permute-start.47 = (bf16[96,768]{1,0:T(8,128)(2,1)S(1)}, bf16[96,768]{1,0:T(8,128)(2,1)S(1)}, u32[]{:S(2)}, u32[]{:S(2)}) collective-permute-start(bf16[96,768]{1,0:T(8,128)(2,1)S(1)} %slice.25), channel_id=1, source_target_pairs={{0,16},{16,0},{1,17},{17,1},{2,18},{18,2},{3,19},{19,3},{4,20},{20... | collective-permute-start | bytes 442376 | tf_op jit(solution)/shard_map/ppermute | solution.py:1048
  178.6 9.5 %collective-permute-start.40 = (bf16[112,512]{1,0:T(8,128)(2,1)S(1)}, bf16[112,512]{1,0:T(8,128)(2,1)S(1)}, u32[]{:S(2)}, u32[]{:S(2)}) collective-permute-start(bf16[112,512]{1,0:T(8,128)(2,1)S(1)} %copy-done.51), channel_id=1, source_target_pairs={{0,16},{16,0},{1,17},{17,1},{2,18},{18,2},{3,19},{19,3},{4,20},{20... | collective-permute-start | bytes 344072 | tf_op jit(solution)/shard_map/ppermute | solution.py:1056
  182.4 8.9 %collective-permute-start.42 = (bf16[112,512]{1,0:T(8,128)(2,1)S(1)}, bf16[112,512]{1,0:T(8,128)(2,1)S(1)}, u32[]{:S(2)}, u32[]{:S(2)}) collective-permute-start(bf16[112,512]{1,0:T(8,128)(2,1)S(1)} %copy-done.50), channel_id=1, source_target_pairs={{0,16},{16,0},{1,17},{17,1},{2,18},{18,2},{3,19},{19,3},{4,20},{20... | collective-permute-start | bytes 344072 | tf_op jit(solution)/shard_map/ppermute | solution.py:1056
  188.0 11.7 %collective-permute-start.37 = (bf16[112,512]{1,0:T(8,128)(2,1)}, bf16[112,512]{1,0:T(8,128)(2,1)S(1)}, u32[]{:S(2)}, u32[]{:S(2)}) collective-permute-start(bf16[112,512]{1,0:T(8,128)(2,1)} %get-tuple-element.142), channel_id=1, source_target_pairs={{0,16},{16,0},{1,17},{17,1},{2,18},{18,2},{3,19},{19,3},{4,20},{20... | collective-permute-start | bytes 344072 | tf_op jit(solution)/shard_map/ppermute | solution.py:1056
  191.3 11.5 %collective-permute-start.39 = (bf16[112,512]{1,0:T(8,128)(2,1)}, bf16[112,512]{1,0:T(8,128)(2,1)S(1)}, u32[]{:S(2)}, u32[]{:S(2)}) collective-permute-start(bf16[112,512]{1,0:T(8,128)(2,1)} %shard_map.309), channel_id=1, source_target_pairs={{0,4},{4,8},{8,12},{12,0},{1,5},{5,9},{9,13},{13,1},{2,6},{6,10},{... | collective-permute-start | bytes 344072 | tf_op jit(solution)/shard_map/ppermute | solution.py:1060
  194.6 8.5 %collective-permute-start.41 = (bf16[112,512]{1,0:T(8,128)(2,1)}, bf16[112,512]{1,0:T(8,128)(2,1)S(1)}, u32[]{:S(2)}, u32[]{:S(2)}) collective-permute-start(bf16[112,512]{1,0:T(8,128)(2,1)} %shard_map.310), channel_id=1, source_target_pairs={{0,8},{4,12},{8,0},{12,4},{1,9},{5,13},{9,1},{13,5},{2,10},{6,14},... | collective-permute-start | bytes 344072 | tf_op jit(solution)/shard_map/ppermute | solution.py:1060
  199.7 15.0 %collective-permute-start.35 = (bf16[256,768]{1,0:T(8,128)(2,1)}, bf16[256,768]{1,0:T(8,128)(2,1)S(1)}, u32[]{:S(2)}, u32[]{:S(2)}) collective-permute-start(bf16[256,768]{1,0:T(8,128)(2,1)} %shard_map.307), channel_id=1, source_target_pairs={{0,2},{1,3},{2,0},{3,1},{4,6},{5,7},{6,4},{7,5},{8,10},{9,11},{10,... | collective-permute-start | bytes 1179656 | tf_op jit(solution)/shard_map/ppermute | solution.py:1066
  (72 other events, 633.0 us)
